TPU v7x, 128 devices: a whole 4x4x4 slice. The times are simulated.
128 devices in a mesh: narrow: 4 (over y_lo, core), wide: 32 (over y_hi, z, x).
Axes of the slice: x: 4, y: 4 (y_hi: 2, y_lo: 2; y = y_hi * 2 + y_lo), z: 4, core: 2. Of those that a mesh axis runs over, the one named last changes fastest.
Arguments:
- adjoint_hat: float32 [3, 2, 256, 256, 256], P(None, None, 'wide', 'narrow'), may hold values from -3 to 3
- velocity_hat: float32 [3, 2, 256, 256, 256], P(None, None, 'wide', 'narrow'), may hold values from -3 to 3
Outputs:
- adjoint_next: float32 [3, 2, 256, 256, 256], P(None, None, 'wide', 'narrow')
All inputs are finite; a program needn't handle non-finite values.
Results may differ from a plain program's by a relative error of at most 0.00005.
Values sent between devices are 32-bit elements; how exact they have to be, the bound alone decides.
No kernel may reach another device: no remote copies, remote signals or barrier semaphores. Data moves between devices by JAX's collectives and lax.ppermute only.
A program may use at most 128 MiB of HBM per device.

v0:
```python
import math

import jax
import jax.numpy as jnp
from jax import lax
from jax.sharding import PartitionSpec as P

NX = 512
NY = 256
NZ = 256
KX = 256


section_step = 0.25
viscous_rate = 0.05
highest = lax.Precision.HIGHEST


def phase_tables(modes, places, length):
    mode_index = jnp.arange(modes, dtype=jnp.int32)[:, None]
    place_index = jnp.arange(places, dtype=jnp.int32)[None, :]
    angle = 2.0 * math.pi / length * (mode_index * place_index % length).astype(jnp.float32)
    return (jnp.cos(angle), jnp.sin(angle))


def rotation_merged(cosine, sine_part):
    table = jnp.stack([jnp.stack([cosine, sine_part], 0), jnp.stack([-sine_part, cosine], 0)], 0)
    length = cosine.shape[0]
    return table.transpose(0, 2, 1, 3)


def signed_wave(count, start, length):
    number = jnp.arange(count, dtype=jnp.int32) + start
    return jnp.where(number < length // 2, number, number - length)


def contract(pattern, values, table):
    return jnp.einsum(pattern, values, table, precision=highest)


def cross_wave(waves, field):
    return jnp.stack(
        [
            waves[1] * field[2] - waves[2] * field[1],
            waves[2] * field[0] - waves[0] * field[2],
            waves[0] * field[1] - waves[1] * field[0],
        ],
        0,
    )


def to_physical(leading, tables):
    inverse_z, inverse_y, synth_x = (tables[0], tables[1], tables[2])
    fields, rows_k, rows_b, merged_z = leading.shape
    depth = contract("fkbq,qdm->mfkdb", leading, inverse_z.reshape(2 * NZ, 2, NZ))
    moved = lax.all_to_all(depth, "narrow", split_axis=0, concat_axis=4, tiled=True)
    planes = moved.shape[0]
    moved = moved.reshape(planes, fields, rows_k, 2 * NY)
    span = contract("mfkq,qej->mfjek", moved, inverse_y.reshape(2 * NY, 2, NY))
    moved = lax.all_to_all(span, "wide", split_axis=0, concat_axis=4, tiled=True)
    moved = moved.reshape(moved.shape[0], fields, NY, 2 * KX)
    return contract("mfjq,qx->mfjx", moved, synth_x)


def to_spectral(physical, tables):
    forward_y, forward_z, anal_x = (tables[3], tables[4], tables[5])
    planes, fields = (physical.shape[0], physical.shape[1])
    stacked = contract("zfyx,xck->kzfcy", physical, anal_x)
    moved = lax.all_to_all(stacked, "wide", split_axis=0, concat_axis=1, tiled=True)
    rows_k = moved.shape[0]
    moved = moved.reshape(rows_k, moved.shape[1], fields, 2 * NY)
    span = contract("kzfq,qdj->jkfdz", moved, forward_y.reshape(2 * NY, 2, NY))
    moved = lax.all_to_all(span, "narrow", split_axis=0, concat_axis=4, tiled=True)
    rows_j = moved.shape[0]
    moved = moved.reshape(rows_j, rows_k, fields, 2 * NZ)
    return contract("jkfq,qen->fekjn", moved, forward_z.reshape(2 * NZ, 2, NZ))


def cross_cells(first, second):
    return jnp.stack(
        [
            first[1] * second[2] - first[2] * second[1],
            first[2] * second[0] - first[0] * second[2],
            first[0] * second[1] - first[1] * second[0],
        ],
        1,
    )


def local(adjoint_hat, velocity_hat):
    rows_x = adjoint_hat.shape[2]
    rows_y = adjoint_hat.shape[3]
    number_x = (lax.axis_index("wide") * rows_x + jnp.arange(rows_x, dtype=jnp.int32))[
        :, None, None
    ]
    number_y = signed_wave(rows_y, lax.axis_index("narrow") * rows_y, NY)[None, :, None]
    number_z = signed_wave(NZ, 0, NZ)[None, None, :]
    waves = [
        2.0 * math.pi / NX * number_x.astype(jnp.float32),
        2.0 * math.pi / NY * number_y.astype(jnp.float32),
        2.0 * math.pi / NZ * number_z.astype(jnp.float32),
    ]
    norm_scale = 1.0 / math.sqrt(NX * NY * NZ)
    cosine_z, sine_z = phase_tables(NZ, NZ, NZ)
    cosine_y, sine_y = phase_tables(NY, NY, NY)
    cosine_x, sine_x = phase_tables(KX, NX, NX)
    weights = (
        jnp.where(jnp.arange(KX, dtype=jnp.int32) == 0, 1.0, 2.0).astype(jnp.float32)[:, None]
        * norm_scale
    )
    synth_x = jnp.stack([cosine_x * weights, -sine_x * weights], 0).reshape(2 * KX, NX)
    anal_x = jnp.stack([cosine_x * norm_scale, -sine_x * norm_scale], 0).transpose(2, 0, 1)
    tables = (
        rotation_merged(cosine_z, sine_z),
        rotation_merged(cosine_y, sine_y),
        synth_x,
        rotation_merged(cosine_y, -sine_y),
        rotation_merged(cosine_z, -sine_z),
        anal_x,
    )
    vorticity_hat = jnp.stack(
        [-cross_wave(waves, velocity_hat[:, 1]), cross_wave(waves, velocity_hat[:, 0])], 1
    )
    fields = jnp.concatenate([adjoint_hat, velocity_hat, vorticity_hat], 0)
    leading = fields.transpose(0, 2, 3, 1, 4).reshape(9, rows_x, rows_y, 2 * NZ)
    inverse_bounds = [(member, member + 1) for member in range(9)]
    forward_bounds = [(member, member + 1) for member in range(6)]
    physical = jnp.concatenate(
        [to_physical(leading[lower:upper], tables) for lower, upper in inverse_bounds], 1
    )
    adjoint_cells = [physical[:, 0], physical[:, 1], physical[:, 2]]
    velocity_cells = [physical[:, 3], physical[:, 4], physical[:, 5]]
    vorticity_cells = [physical[:, 6], physical[:, 7], physical[:, 8]]
    rotation = cross_cells(adjoint_cells, vorticity_cells)
    transport = cross_cells(velocity_cells, adjoint_cells)
    products = jnp.concatenate([rotation, transport], 1)
    spectra = jnp.concatenate(
        [to_spectral(products[:, lower:upper], tables) for lower, upper in forward_bounds], 0
    )
    first = spectra[0:3]
    second = spectra[3:6]
    conv_real = first[:, 0] - cross_wave(waves, second[:, 1])
    conv_imag = first[:, 1] + cross_wave(waves, second[:, 0])
    keep = (
        (3 * number_x < NX) & (3 * jnp.abs(number_y) < NY) & (3 * jnp.abs(number_z) < NZ)
    ).astype(jnp.float32)
    ksquare = waves[0] ** 2 + waves[1] ** 2 + waves[2] ** 2
    divisor = ksquare + (ksquare == 0).astype(jnp.float32)
    decay = jnp.exp(-viscous_rate * ksquare)
    projected = []
    for convect in (conv_real, conv_imag):
        along = (waves[0] * convect[0] + waves[1] * convect[1] + waves[2] * convect[2]) / divisor
        projected.append(
            keep * (convect - jnp.stack([waves[0] * along, waves[1] * along, waves[2] * along], 0))
        )
    projected = jnp.stack(projected, 1)
    return decay * (adjoint_hat + section_step * projected)


def solution(mesh):
    in_specs = (P(None, None, "wide", "narrow", None), P(None, None, "wide", "narrow", None))
    out_specs = P(None, None, "wide", "narrow", None)
    return jax.shard_map(local, mesh=mesh, in_specs=in_specs, out_specs=out_specs, check_vma=False)
```

profile of v0, /device:TPU:0, one launch (start us, length us, event | category | flops | bytes accessed | tf_op | source)
XLA Modules:
  0.0 777.7 jit_solution(18190431282732630563)
XLA Ops:
  24.0 4.9 all-to-all-start
  38.5 5.0 all-to-all-done
  57.2 5.0 all-to-all-done.4
  76.2 5.0 all-to-all-done.2
  95.0 5.1 all-to-all-done.6
  100.0 4.4 all-to-all-start.12
  114.1 4.9 all-to-all-done.12
  132.8 5.0 all-to-all-done.10
  137.8 4.7 all-to-all-start.20
  151.9 5.0 all-to-all-done.20
  170.7 5.0 all-to-all-done.24
  180.7 5.5 reduce.6
  197.3 11.2 %all-to-all-start.1 = ((f32[64,1,256,2,8]{2,4,3,1,0:T(8,128)}), f32[64,1,256,2,8]{2,4,3,1,0:T(8,128)}, u32[]{:S(2)}, u32[]{:S(2)}) async-start(f32[64,1,256,2,8]{2,4,3,1,0:T(8,128)} %copy.165), calls=%async_computation.1 | async-start | bytes 2097152 | tf_op jit(solution)/shard_map/all_to_all | solution.py:60
  208.5 5.5 reduce.1
  227.4 8.2 %all-to-all-start.5 = ((f32[64,1,256,2,8]{2,4,3,1,0:T(8,128)}), f32[64,1,256,2,8]{2,4,3,1,0:T(8,128)}, u32[]{:S(2)}, u32[]{:S(2)}) async-start(f32[64,1,256,2,8]{2,4,3,1,0:T(8,128)} %copy.177), calls=%async_computation.5 | async-start | bytes 2097152 | tf_op jit(solution)/shard_map/all_to_all | solution.py:60
  235.6 5.5 reduce.12
  253.9 8.6 %all-to-all-start.3 = ((f32[64,1,256,2,8]{2,4,3,1,0:T(8,128)}), f32[64,1,256,2,8]{2,4,3,1,0:T(8,128)}, u32[]{:S(2)}, u32[]{:S(2)}) async-start(f32[64,1,256,2,8]{2,4,3,1,0:T(8,128)} %copy.171), calls=%async_computation.3 | async-start | bytes 2097152 | tf_op jit(solution)/shard_map/all_to_all | solution.py:60
  262.5 5.5 reduce.10
  280.2 9.2 %all-to-all-start.7 = ((f32[64,1,256,2,8]{2,4,3,1,0:T(8,128)}), f32[64,1,256,2,8]{2,4,3,1,0:T(8,128)}, u32[]{:S(2)}, u32[]{:S(2)}) async-start(f32[64,1,256,2,8]{2,4,3,1,0:T(8,128)} %copy.183), calls=%async_computation.7 | async-start | bytes 2097152 | tf_op jit(solution)/shard_map/all_to_all | solution.py:60
  289.3 5.5 reduce.3
  306.5 10.0 %all-to-all-start.13 = ((f32[64,1,256,2,8]{2,4,3,1,0:T(8,128)}), f32[64,1,256,2,8]{2,4,3,1,0:T(8,128)}, u32[]{:S(2)}, u32[]{:S(2)}) async-start(f32[64,1,256,2,8]{2,4,3,1,0:T(8,128)} %copy.199), calls=%async_computation.13 | async-start | bytes 2097152 | tf_op jit(solution)/shard_map/all_to_all | solution.py:60
  316.4 5.5 reduce.9
  333.0 10.2 %all-to-all-start.11 = ((f32[64,1,256,2,8]{2,4,3,1,0:T(8,128)}), f32[64,1,256,2,8]{2,4,3,1,0:T(8,128)}, u32[]{:S(2)}, u32[]{:S(2)}) async-start(f32[64,1,256,2,8]{2,4,3,1,0:T(8,128)} %copy.193), calls=%async_computation.11 | async-start | bytes 2097152 | tf_op jit(solution)/shard_map/all_to_all | solution.py:60
  343.3 5.5 reduce.5
  359.9 10.3 %all-to-all-start.21 = ((f32[64,1,256,2,8]{2,4,3,1,0:T(8,128)}), f32[64,1,256,2,8]{2,4,3,1,0:T(8,128)}, u32[]{:S(2)}, u32[]{:S(2)}) async-start(f32[64,1,256,2,8]{2,4,3,1,0:T(8,128)} %copy.219), calls=%async_computation.21 | async-start | bytes 2097152 | tf_op jit(solution)/shard_map/all_to_all | solution.py:60
  370.1 5.5 reduce.2
  386.8 10.5 %all-to-all-start.25 = ((f32[64,1,256,2,8]{2,4,3,1,0:T(8,128)}), f32[64,1,256,2,8]{2,4,3,1,0:T(8,128)}, u32[]{:S(2)}, u32[]{:S(2)}) async-start(f32[64,1,256,2,8]{2,4,3,1,0:T(8,128)} %copy.229), calls=%async_computation.25 | async-start | bytes 2097152 | tf_op jit(solution)/shard_map/all_to_all | solution.py:60
  402.5 4.5 reduce
  425.5 10.1 %all-to-all-start.19 = ((f32[64,1,256,2,8]{2,4,3,1,0:T(8,128)}), f32[64,1,256,2,8]{2,4,3,1,0:T(8,128)}, u32[]{:S(2)}, u32[]{:S(2)}) async-start(f32[64,1,256,2,8]{2,4,3,1,0:T(8,128)} %copy.213), calls=%async_computation.19 | async-start | bytes 2097152 | tf_op jit(solution)/shard_map/all_to_all | solution.py:60
  449.9 9.2 %all-to-all-start.8 = ((f32[256,2,1,2,256]{4,1,3,2,0:T(2,128)}), f32[256,2,1,2,256]{4,1,3,2,0:T(2,128)}, u32[]{:S(2)}, u32[]{:S(2)}) async-start(f32[256,2,1,2,256]{4,1,3,2,0:T(2,128)} %copy.186), calls=%async_computation.8 | async-start | bytes 2097152 | tf_op jit(solution)/shard_map/all_to_all | solution.py:69
  473.1 6.4 all-to-all-start.14
  485.4 8.0 %all-to-all-done.14 = f32[256,2,1,2,256]{4,1,3,2,0:T(2,128)} async-done(((f32[256,2,1,2,256]{4,1,3,2,0:T(2,128)}), f32[256,2,1,2,256]{4,1,3,2,0:T(2,128)}, u32[]{:S(2)}, u32[]{:S(2)}) %all-to-all-start.14) | async-done | bytes 1048608 | tf_op jit(solution)/shard_map/all_to_all | solution.py:69
  493.4 5.1 all-to-all-start.16
  512.5 6.4 all-to-all-start.28
  526.1 6.8 all-to-all-done.28
  532.9 4.9 all-to-all-start.22
  543.1 8.7 %all-to-all-done.22 = f32[256,2,1,2,256]{4,1,3,2,0:T(2,128)} async-done(((f32[256,2,1,2,256]{4,1,3,2,0:T(2,128)}), f32[256,2,1,2,256]{4,1,3,2,0:T(2,128)}, u32[]{:S(2)}, u32[]{:S(2)}) %all-to-all-start.22) | async-done | bytes 1048608 | tf_op jit(solution)/shard_map/all_to_all | solution.py:69
  551.9 4.8 all-to-all-start.26
  589.4 4.5 all-to-all-start.15
  627.2 4.7 all-to-all-start.23
  653.9 5.5 reduce.14
  667.8 5.5 reduce.13
  681.8 5.5 reduce.8
  695.6 4.5 all-to-all-start.27
  700.2 5.5 reduce.7
  724.1 4.5 all-to-all-start.17
  728.6 5.5 reduce.4
  752.6 5.5 reduce.11
  (366 shorter events, 473.4 us)
Async XLA Ops:
  24.0 4.9 copy-start.35
  24.0 19.4 %all-to-all-start = ((f32[4,1,65536]{2,1,0:T(1,128)}), f32[4,1,65536]{2,1,0:T(1,128)}, u32[]{:S(2)}, u32[]{:S(2)}) async-start(f32[4,1,65536]{2,1,0:T(1,128)} %reshape.1119), calls=%async_computation | async-start | bytes 2097152 | tf_op jit(solution)/shard_map/all_to_all | solution.py:56
  38.5 9.3 %copy-start.34 = (f32[1,8,64,2,256]{4,2,1,3,0:T(8,128)S(1)}, f32[1,8,64,2,256]{4,2,1,3,0:T(8,128)}, u32[]{:S(2)}) copy-start(f32[1,8,64,2,256]{4,2,1,3,0:T(8,128)} %get-tuple-element.9) | copy-start | bytes 3145732
  43.5 18.8 %all-to-all-start.4 = ((f32[4,1,65536]{2,1,0:T(1,128)}), f32[4,1,65536]{2,1,0:T(1,128)}, u32[]{:S(2)}, u32[]{:S(2)}) async-start(f32[4,1,65536]{2,1,0:T(1,128)} %reshape.1123), calls=%async_computation.4 | async-start | bytes 2097152 | tf_op jit(solution)/shard_map/all_to_all | solution.py:56
  57.2 9.5 %copy-start.33 = (f32[1,8,64,2,256]{4,2,1,3,0:T(8,128)S(1)}, f32[1,8,64,2,256]{4,2,1,3,0:T(8,128)}, u32[]{:S(2)}) copy-start(f32[1,8,64,2,256]{4,2,1,3,0:T(8,128)} %get-tuple-element.15) | copy-start | bytes 3145732
  62.3 19.0 %all-to-all-start.2 = ((f32[4,1,65536]{2,1,0:T(1,128)}), f32[4,1,65536]{2,1,0:T(1,128)}, u32[]{:S(2)}, u32[]{:S(2)}) async-start(f32[4,1,65536]{2,1,0:T(1,128)} %reshape.1141), calls=%async_computation.2 | async-start | bytes 2097152 | tf_op jit(solution)/shard_map/all_to_all | solution.py:56
  76.2 9.3 %copy-start.32 = (f32[1,8,64,2,256]{4,2,1,3,0:T(8,128)S(1)}, f32[1,8,64,2,256]{4,2,1,3,0:T(8,128)}, u32[]{:S(2)}) copy-start(f32[1,8,64,2,256]{4,2,1,3,0:T(8,128)} %get-tuple-element.13) | copy-start | bytes 3145732
  81.2 18.8 %all-to-all-start.6 = ((f32[4,1,65536]{2,1,0:T(1,128)}), f32[4,1,65536]{2,1,0:T(1,128)}, u32[]{:S(2)}, u32[]{:S(2)}) async-start(f32[4,1,65536]{2,1,0:T(1,128)} %reshape.1137), calls=%async_computation.6 | async-start | bytes 2097152 | tf_op jit(solution)/shard_map/all_to_all | solution.py:56
  95.0 9.5 %copy-start.31 = (f32[1,8,64,2,256]{4,2,1,3,0:T(8,128)S(1)}, f32[1,8,64,2,256]{4,2,1,3,0:T(8,128)}, u32[]{:S(2)}) copy-start(f32[1,8,64,2,256]{4,2,1,3,0:T(8,128)} %get-tuple-element.14) | copy-start | bytes 3145732
  100.0 19.0 %all-to-all-start.12 = ((f32[4,1,65536]{2,1,0:T(1,128)}), f32[4,1,65536]{2,1,0:T(1,128)}, u32[]{:S(2)}, u32[]{:S(2)}) async-start(f32[4,1,65536]{2,1,0:T(1,128)} %reshape.1129), calls=%async_computation.12 | async-start | bytes 2097152 | tf_op jit(solution)/shard_map/all_to_all | solution.py:56
  114.1 9.2 %copy-start.30 = (f32[1,8,64,2,256]{4,2,1,3,0:T(8,128)S(1)}, f32[1,8,64,2,256]{4,2,1,3,0:T(8,128)}, u32[]{:S(2)}) copy-start(f32[1,8,64,2,256]{4,2,1,3,0:T(8,128)} %get-tuple-element.11) | copy-start | bytes 3145732
  119.0 18.8 %all-to-all-start.10 = ((f32[4,1,65536]{2,1,0:T(1,128)}), f32[4,1,65536]{2,1,0:T(1,128)}, u32[]{:S(2)}, u32[]{:S(2)}) async-start(f32[4,1,65536]{2,1,0:T(1,128)} %reshape.1135), calls=%async_computation.10 | async-start | bytes 2097152 | tf_op jit(solution)/shard_map/all_to_all | solution.py:56
  132.8 9.7 %copy-start.29 = (f32[1,8,64,2,256]{4,2,1,3,0:T(8,128)S(1)}, f32[1,8,64,2,256]{4,2,1,3,0:T(8,128)}, u32[]{:S(2)}) copy-start(f32[1,8,64,2,256]{4,2,1,3,0:T(8,128)} %get-tuple-element.10) | copy-start | bytes 3145732
  137.8 19.2 %all-to-all-start.20 = ((f32[4,1,65536]{2,1,0:T(1,128)}), f32[4,1,65536]{2,1,0:T(1,128)}, u32[]{:S(2)}, u32[]{:S(2)}) async-start(f32[4,1,65536]{2,1,0:T(1,128)} %reshape.1121), calls=%async_computation.20 | async-start | bytes 2097152 | tf_op jit(solution)/shard_map/all_to_all | solution.py:56
  151.9 9.3 %copy-start.28 = (f32[1,8,64,2,256]{4,2,1,3,0:T(8,128)S(1)}, f32[1,8,64,2,256]{4,2,1,3,0:T(8,128)}, u32[]{:S(2)}) copy-start(f32[1,8,64,2,256]{4,2,1,3,0:T(8,128)} %get-tuple-element.12) | copy-start | bytes 3145732
  157.0 18.8 %all-to-all-start.24 = ((f32[4,1,65536]{2,1,0:T(1,128)}), f32[4,1,65536]{2,1,0:T(1,128)}, u32[]{:S(2)}, u32[]{:S(2)}) async-start(f32[4,1,65536]{2,1,0:T(1,128)} %reshape.1117), calls=%async_computation.24 | async-start | bytes 2097152 | tf_op jit(solution)/shard_map/all_to_all | solution.py:56
  175.7 21.6 %all-to-all-start.18 = ((f32[4,1,65536]{2,1,0:T(1,128)}), f32[4,1,65536]{2,1,0:T(1,128)}, u32[]{:S(2)}, u32[]{:S(2)}) async-start(f32[4,1,65536]{2,1,0:T(1,128)} %reshape.1127), calls=%async_computation.18 | async-start | bytes 2097152 | tf_op jit(solution)/shard_map/all_to_all | solution.py:56
  197.3 30.1 %all-to-all-start.1 = ((f32[64,1,256,2,8]{2,4,3,1,0:T(8,128)}), f32[64,1,256,2,8]{2,4,3,1,0:T(8,128)}, u32[]{:S(2)}, u32[]{:S(2)}) async-start(f32[64,1,256,2,8]{2,4,3,1,0:T(8,128)} %copy.165), calls=%async_computation.1 | async-start | bytes 2097152 | tf_op jit(solution)/shard_map/all_to_all | solution.py:60
  227.4 26.5 %all-to-all-start.5 = ((f32[64,1,256,2,8]{2,4,3,1,0:T(8,128)}), f32[64,1,256,2,8]{2,4,3,1,0:T(8,128)}, u32[]{:S(2)}, u32[]{:S(2)}) async-start(f32[64,1,256,2,8]{2,4,3,1,0:T(8,128)} %copy.177), calls=%async_computation.5 | async-start | bytes 2097152 | tf_op jit(solution)/shard_map/all_to_all | solution.py:60
  253.9 26.3 %all-to-all-start.3 = ((f32[64,1,256,2,8]{2,4,3,1,0:T(8,128)}), f32[64,1,256,2,8]{2,4,3,1,0:T(8,128)}, u32[]{:S(2)}, u32[]{:S(2)}) async-start(f32[64,1,256,2,8]{2,4,3,1,0:T(8,128)} %copy.171), calls=%async_computation.3 | async-start | bytes 2097152 | tf_op jit(solution)/shard_map/all_to_all | solution.py:60
  280.2 26.3 %all-to-all-start.7 = ((f32[64,1,256,2,8]{2,4,3,1,0:T(8,128)}), f32[64,1,256,2,8]{2,4,3,1,0:T(8,128)}, u32[]{:S(2)}, u32[]{:S(2)}) async-start(f32[64,1,256,2,8]{2,4,3,1,0:T(8,128)} %copy.183), calls=%async_computation.7 | async-start | bytes 2097152 | tf_op jit(solution)/shard_map/all_to_all | solution.py:60
  306.5 26.5 %all-to-all-start.13 = ((f32[64,1,256,2,8]{2,4,3,1,0:T(8,128)}), f32[64,1,256,2,8]{2,4,3,1,0:T(8,128)}, u32[]{:S(2)}, u32[]{:S(2)}) async-start(f32[64,1,256,2,8]{2,4,3,1,0:T(8,128)} %copy.199), calls=%async_computation.13 | async-start | bytes 2097152 | tf_op jit(solution)/shard_map/all_to_all | solution.py:60
  333.0 26.8 %all-to-all-start.11 = ((f32[64,1,256,2,8]{2,4,3,1,0:T(8,128)}), f32[64,1,256,2,8]{2,4,3,1,0:T(8,128)}, u32[]{:S(2)}, u32[]{:S(2)}) async-start(f32[64,1,256,2,8]{2,4,3,1,0:T(8,128)} %copy.193), calls=%async_computation.11 | async-start | bytes 2097152 | tf_op jit(solution)/shard_map/all_to_all | solution.py:60
  359.9 26.9 %all-to-all-start.21 = ((f32[64,1,256,2,8]{2,4,3,1,0:T(8,128)}), f32[64,1,256,2,8]{2,4,3,1,0:T(8,128)}, u32[]{:S(2)}, u32[]{:S(2)}) async-start(f32[64,1,256,2,8]{2,4,3,1,0:T(8,128)} %copy.219), calls=%async_computation.21 | async-start | bytes 2097152 | tf_op jit(solution)/shard_map/all_to_all | solution.py:60
  386.8 38.7 %all-to-all-start.25 = ((f32[64,1,256,2,8]{2,4,3,1,0:T(8,128)}), f32[64,1,256,2,8]{2,4,3,1,0:T(8,128)}, u32[]{:S(2)}, u32[]{:S(2)}) async-start(f32[64,1,256,2,8]{2,4,3,1,0:T(8,128)} %copy.229), calls=%async_computation.25 | async-start | bytes 2097152 | tf_op jit(solution)/shard_map/all_to_all | solution.py:60
  425.5 24.4 %all-to-all-start.19 = ((f32[64,1,256,2,8]{2,4,3,1,0:T(8,128)}), f32[64,1,256,2,8]{2,4,3,1,0:T(8,128)}, u32[]{:S(2)}, u32[]{:S(2)}) async-start(f32[64,1,256,2,8]{2,4,3,1,0:T(8,128)} %copy.213), calls=%async_computation.19 | async-start | bytes 2097152 | tf_op jit(solution)/shard_map/all_to_all | solution.py:60
  449.9 23.1 %all-to-all-start.8 = ((f32[256,2,1,2,256]{4,1,3,2,0:T(2,128)}), f32[256,2,1,2,256]{4,1,3,2,0:T(2,128)}, u32[]{:S(2)}, u32[]{:S(2)}) async-start(f32[256,2,1,2,256]{4,1,3,2,0:T(2,128)} %copy.186), calls=%async_computation.8 | async-start | bytes 2097152 | tf_op jit(solution)/shard_map/all_to_all | solution.py:69
  473.1 20.4 %all-to-all-start.14 = ((f32[256,2,1,2,256]{4,1,3,2,0:T(2,128)}), f32[256,2,1,2,256]{4,1,3,2,0:T(2,128)}, u32[]{:S(2)}, u32[]{:S(2)}) async-start(f32[256,2,1,2,256]{4,1,3,2,0:T(2,128)} %copy.202), calls=%async_computation.14 | async-start | bytes 2097152 | tf_op jit(solution)/shard_map/all_to_all | solution.py:69
  493.4 19.1 %all-to-all-start.16 = ((f32[256,2,1,2,256]{4,1,3,2,0:T(2,128)}), f32[256,2,1,2,256]{4,1,3,2,0:T(2,128)}, u32[]{:S(2)}, u32[]{:S(2)}) async-start(f32[256,2,1,2,256]{4,1,3,2,0:T(2,128)} %copy.206), calls=%async_computation.16 | async-start | bytes 2097152 | tf_op jit(solution)/shard_map/all_to_all | solution.py:69
  503.1 4.0 copy-start.20
  512.5 20.4 %all-to-all-start.28 = ((f32[256,2,1,2,256]{4,1,3,2,0:T(2,128)}), f32[256,2,1,2,256]{4,1,3,2,0:T(2,128)}, u32[]{:S(2)}, u32[]{:S(2)}) async-start(f32[256,2,1,2,256]{4,1,3,2,0:T(2,128)} %copy.236), calls=%async_computation.28 | async-start | bytes 2097152 | tf_op jit(solution)/shard_map/all_to_all | solution.py:69
  524.3 13.5 %copy-start.2 = (f32[2,256,512]{2,1,0:T(8,128)S(1)}, f32[2,256,512]{2,1,0:T(8,128)}, u32[]{:S(2)}) copy-start(f32[2,256,512]{2,1,0:T(8,128)} %copy-done) | copy-start | bytes 3145732
  524.3 13.5 %copy-start.7 = (f32[1,256,512]{2,1,0:T(8,128)S(1)}, f32[1,256,512]{2,1,0:T(8,128)}, u32[]{:S(2)}) copy-start(f32[1,256,512]{2,1,0:T(8,128)} %get-tuple-element.70) | copy-start | bytes 1572868
  524.3 13.5 %copy-start.12 = (f32[1,256,512]{2,1,0:T(8,128)S(1)}, f32[1,256,512]{2,1,0:T(8,128)}, u32[]{:S(2)}) copy-start(f32[1,256,512]{2,1,0:T(8,128)} %get-tuple-element.71) | copy-start | bytes 1572868
  532.9 19.0 %all-to-all-start.22 = ((f32[256,2,1,2,256]{4,1,3,2,0:T(2,128)}), f32[256,2,1,2,256]{4,1,3,2,0:T(2,128)}, u32[]{:S(2)}, u32[]{:S(2)}) async-start(f32[256,2,1,2,256]{4,1,3,2,0:T(2,128)} %copy.222), calls=%async_computation.22 | async-start | bytes 2097152 | tf_op jit(solution)/shard_map/all_to_all | solution.py:69
  541.3 15.4 %copy-start.52 = (f32[1,2,256,256]{3,2,1,0:T(8,128)S(1)}, f32[1,2,256,256]{3,2,1,0:T(8,128)}, u32[]{:S(2)}) copy-start(f32[1,2,256,256]{3,2,1,0:T(8,128)} %get-tuple-element.53) | copy-start | bytes 1572868
  541.4 15.4 %copy-start.53 = (f32[1,2,256,256]{3,2,1,0:T(8,128)S(1)}, f32[1,2,256,256]{3,2,1,0:T(8,128)}, u32[]{:S(2)}) copy-start(f32[1,2,256,256]{3,2,1,0:T(8,128)} %get-tuple-element.56) | copy-start | bytes 1572868
  551.9 18.8 %all-to-all-start.26 = ((f32[256,2,1,2,256]{4,1,3,2,0:T(2,128)}), f32[256,2,1,2,256]{4,1,3,2,0:T(2,128)}, u32[]{:S(2)}, u32[]{:S(2)}) async-start(f32[256,2,1,2,256]{4,1,3,2,0:T(2,128)} %copy.232), calls=%async_computation.26 | async-start | bytes 2097152 | tf_op jit(solution)/shard_map/all_to_all | solution.py:69
  570.7 18.8 %all-to-all-start.9 = ((f32[4,1,65536]{2,1,0:T(1,128)}), f32[4,1,65536]{2,1,0:T(1,128)}, u32[]{:S(2)}, u32[]{:S(2)}) async-start(f32[4,1,65536]{2,1,0:T(1,128)} %reshape.1145), calls=%async_computation.9 | async-start | bytes 2097152 | tf_op jit(solution)/shard_map/all_to_all | solution.py:73
  589.4 19.0 %all-to-all-start.15 = ((f32[4,1,65536]{2,1,0:T(1,128)}), f32[4,1,65536]{2,1,0:T(1,128)}, u32[]{:S(2)}, u32[]{:S(2)}) async-start(f32[4,1,65536]{2,1,0:T(1,128)} %reshape.1143), calls=%async_computation.15 | async-start | bytes 2097152 | tf_op jit(solution)/shard_map/all_to_all | solution.py:73
  608.4 18.8 %all-to-all-start.29 = ((f32[4,1,65536]{2,1,0:T(1,128)}), f32[4,1,65536]{2,1,0:T(1,128)}, u32[]{:S(2)}, u32[]{:S(2)}) async-start(f32[4,1,65536]{2,1,0:T(1,128)} %reshape.1125), calls=%async_computation.29 | async-start | bytes 2097152 | tf_op jit(solution)/shard_map/all_to_all | solution.py:73
  621.8 10.1 %copy-start.63 = (f32[64]{0:T(128)S(1)}, f32[64]{0:T(128)}, u32[]{:S(2)}) copy-start(f32[64]{0:T(128)} %get-tuple-element.65) | copy-start | bytes 772
  621.8 10.1 %copy-start.64 = (f32[8]{0:T(128)S(1)}, f32[8]{0:T(128)}, u32[]{:S(2)}) copy-start(f32[8]{0:T(128)} %get-tuple-element.67) | copy-start | bytes 100
  621.8 10.2 %copy-start.62 = (f32[256]{0:T(256)S(1)}, f32[256]{0:T(256)}, u32[]{:S(2)}) copy-start(f32[256]{0:T(256)} %get-tuple-element.73) | copy-start | bytes 3076
  627.2 68.4 %all-to-all-start.23 = ((f32[4,1,65536]{2,1,0:T(1,128)}), f32[4,1,65536]{2,1,0:T(1,128)}, u32[]{:S(2)}, u32[]{:S(2)}) async-start(f32[4,1,65536]{2,1,0:T(1,128)} %reshape.1133), calls=%async_computation.23 | async-start | bytes 2097152 | tf_op jit(solution)/shard_map/all_to_all | solution.py:73
  695.6 28.5 %all-to-all-start.27 = ((f32[4,1,65536]{2,1,0:T(1,128)}), f32[4,1,65536]{2,1,0:T(1,128)}, u32[]{:S(2)}, u32[]{:S(2)}) async-start(f32[4,1,65536]{2,1,0:T(1,128)} %reshape.1131), calls=%async_computation.27 | async-start | bytes 2097152 | tf_op jit(solution)/shard_map/all_to_all | solution.py:73
  710.5 4.0 copy-start.24
  724.1 28.5 %all-to-all-start.17 = ((f32[4,1,65536]{2,1,0:T(1,128)}), f32[4,1,65536]{2,1,0:T(1,128)}, u32[]{:S(2)}, u32[]{:S(2)}) async-start(f32[4,1,65536]{2,1,0:T(1,128)} %reshape.1139), calls=%async_computation.17 | async-start | bytes 2097152 | tf_op jit(solution)/shard_map/all_to_all | solution.py:73
  (47 other events, 95.5 us)
where the time goes:
time: 791 us; the launch traced here: 778 us
  local copies, waits for them, and re-layouts  277 us (35%)
  starting transfers between devices  192 us (24%)
  matrix products  108 us (14%)
  other arithmetic  107 us (14%)
  waiting for transfers between devices  91.9 us (12%)
    dot_general x45, matrix products, contract(): return jnp.einsum(pattern, values, table, precision=highest)  108 us
    all_to_all x9, starting transfers between devices, to_physical(): lax.all_to_all(span, 'wide', split_axis=0, concat_axis=4, tiled=True)  88.2 us
    unnamed x160, local copies, waits for them, and re-layouts  77.5 us
    transpose x30, local copies, waits for them, and re-layouts, contract(): return jnp.einsum(pattern, values, table, precision=highest)  63.1 us
    another operation x30, local copies, waits for them, and re-layouts  58.4 us
    all_to_all x9, other arithmetic, to_physical(): lax.all_to_all(depth, 'narrow', split_axis=0, concat_axis=4, tiled=True)  48.5 us
    all_to_all x9, waiting for transfers between devices, to_physical(): lax.all_to_all(depth, 'narrow', split_axis=0, concat_axis=4, tiled=True)  40.1 us
    all_to_all x9, starting transfers between devices, to_physical(): lax.all_to_all(depth, 'narrow', split_axis=0, concat_axis=4, tiled=True)  39.9 us
  transfers between devices with their start and end apart: 30, of which 22 were waited for; matrix products, arithmetic and copies ran while one was open for 57% of the time, Pallas kernels for 0%

commit v1 on v0

v1 whole, which is shorter than its diff:
```python
import math

import jax
import jax.numpy as jnp
import ml_dtypes
import numpy as np
from jax import lax
from jax.experimental import pallas as pl
from jax.experimental.pallas import tpu as pltpu
from jax.sharding import PartitionSpec as P

NX = 512
NY = 256
NZ = 256
KX = 256
ROWS_X = 8
ROWS_Y = 64
WIDE = 32
NARROW = 4
DEVICES = WIDE * NARROW
SENT = 8
BACK = 5
KEPT_X = 176

section_step = 0.25
viscous_rate = 0.05
vmem_bytes = 60 * 1024 * 1024


def halves(table):
    upper = table.astype(ml_dtypes.bfloat16)
    lower = (table - upper.astype(np.float64)).astype(ml_dtypes.bfloat16)
    return np.stack([upper, lower])


def turn(modes, places, length):
    angle = 2.0 * np.pi / length * (np.outer(modes, places) % length)
    return np.cos(angle), np.sin(angle)


def tables_synth_z():
    quarter = np.arange(128)
    parts = []
    for plane in range(2):
        cosine, sine = turn(2 * np.arange(128) + plane, quarter, NZ)
        parts.append(halves(np.concatenate([cosine, sine], 1)))
    return np.stack(parts)


def tables_synth_y():
    mode = np.arange(128)
    parts = []
    for parity in range(2):
        cosine, sine = turn(mode, 2 * np.arange(128) + parity, NY)
        real_rows = np.concatenate([cosine, sine], 1)
        imag_rows = np.concatenate([-sine, cosine], 1)
        stacked = np.stack([real_rows.reshape(2, 64, 256), imag_rows.reshape(2, 64, 256)], 1)
        parts.append(halves(stacked.reshape(256, 256)))
    return np.stack(parts)


def norm_scale():
    return 1.0 / math.sqrt(NX * NY * NZ)


def tables_synth_x():
    weight = np.where(np.arange(KX) == 0, 1.0, 2.0) * norm_scale()
    cosine, sine = turn(np.arange(256), np.arange(KX), NX)
    return np.stack([halves(cosine * weight), halves(-sine * weight)])


def tables_anal_x():
    cosine, sine = turn(np.arange(KEPT_X), np.arange(256), NX)
    return np.stack([halves(cosine * norm_scale()), halves(-sine * norm_scale())])


def tables_anal_y():
    parts = []
    mode = np.arange(128)
    for parity in range(2):
        cosine, sine = turn(2 * np.arange(128) + parity, mode, NY)
        cosine = cosine.reshape(128, 2, 1, 64)
        sine = sine.reshape(128, 2, 1, 64)
        real_rows = np.concatenate([cosine, -sine], 2).reshape(128, 256)
        imag_rows = np.concatenate([sine, cosine], 2).reshape(128, 256)
        parts.append(halves(np.concatenate([real_rows, imag_rows], 0)))
    return np.stack(parts)


def tables_anal_z():
    place = np.concatenate([2 * np.arange(128), 2 * np.arange(128) + 1])
    cosine, sine = turn(place, np.arange(NZ), NZ)
    return halves(np.concatenate([cosine, sine], 1))


def split(value):
    upper = value.astype(jnp.bfloat16)
    lower = (value - upper.astype(jnp.float32)).astype(jnp.bfloat16)
    return upper, lower


def dot(left, right, dims):
    return lax.dot_general(left, right, (dims, ((), ())), preferred_element_type=jnp.float32)


def dot3(left, right, dims=((1,), (0,))):
    return (
        dot(left[0], right[0], dims)
        + dot(left[0], right[1], dims)
        + dot(left[1], right[0], dims)
    )


def signed(number, length):
    return jnp.where(number < length // 2, number, number - length)


def wave_y(start, shape, axis):
    number = lax.broadcasted_iota(jnp.int32, shape, axis) + start
    return 2.0 * math.pi / NY * signed(number, NY).astype(jnp.float32)


def wave_z(shape, axis):
    number = lax.broadcasted_iota(jnp.int32, shape, axis)
    return 2.0 * math.pi / NZ * signed(number, NZ).astype(jnp.float32)


def synth_z_kernel(place_ref, adjoint_ref, velocity_ref, table_ref, even_ref, odd_ref):
    outs = (even_ref, odd_ref)
    ky = wave_y(place_ref[1] * ROWS_Y, (ROWS_Y, 1), 0)
    kz = wave_z((1, NZ), 1)
    vel = [[velocity_ref[c, part, 0] for part in range(2)] for c in range(3)]
    fields = [(adjoint_ref[c, 0, 0], adjoint_ref[c, 1, 0]) for c in range(3)]
    fields += [(vel[c][0], vel[c][1]) for c in range(3)]
    fields.append((kz * vel[1][1] - ky * vel[2][1], ky * vel[2][0] - kz * vel[1][0]))
    fields.append((0.0, 0.0))
    number_x = place_ref[0] * ROWS_X + pl.program_id(0)
    kx = 2.0 * math.pi / NX * number_x.astype(jnp.float32)
    fields[7] = (kx * vel[2][1] - kz * vel[0][1], kz * vel[0][0] - kx * vel[2][0])
    for plane in range(2):
        table = (table_ref[plane, 0], table_ref[plane, 1])
        for pair in range(SENT // 2):
            blocks = []
            for real, imag in fields[2 * pair : 2 * pair + 2]:
                if plane == 0:
                    low_r = real[:, :128] + real[:, 128:]
                    low_i = imag[:, :128] + imag[:, 128:]
                else:
                    low_r = real[:, :128] - real[:, 128:]
                    low_i = imag[:, :128] - imag[:, 128:]
                blocks.append(jnp.concatenate([low_r, -low_i], 1))
                blocks.append(jnp.concatenate([low_i, low_r], 1))
            value = dot3(table, split(jnp.concatenate(blocks, 0)), ((1,), (1,)))
            outs[plane][:, 2 * pair, :] = value[:, :128]
            outs[plane][:, 2 * pair + 1, :] = value[:, 128:]


def synth_z(place, adjoint_hat, velocity_hat):
    whole = (3, 2, 1, ROWS_Y, NZ)
    table = tables_synth_z()
    shape = jax.ShapeDtypeStruct((DEVICES, ROWS_X * SENT, 128), jnp.float32)
    out_spec = pl.BlockSpec((DEVICES, SENT, 128), lambda k, s: (0, k, 0))
    return pl.pallas_call(
        synth_z_kernel,
        grid_spec=pltpu.PrefetchScalarGridSpec(
            num_scalar_prefetch=1,
            grid=(ROWS_X,),
            in_specs=[
                pl.BlockSpec(whole, lambda k, s: (0, 0, k, 0, 0)),
                pl.BlockSpec(whole, lambda k, s: (0, 0, k, 0, 0)),
                pl.BlockSpec(table.shape, lambda k, s: (0, 0, 0, 0)),
            ],
            out_specs=[out_spec, out_spec],
        ),
        out_shape=[shape, shape],
        compiler_params=pltpu.CompilerParams(vmem_limit_bytes=vmem_bytes),
        name="synth_z",
    )(place, adjoint_hat, velocity_hat, jnp.asarray(table))


def plane_kernel(got_ref, sy_ref, sx_ref, ax_ref, ay_ref, out_ref, spec_ref, cell_ref, anal_ref):
    chunk = ROWS_X * SENT
    half_sign = jnp.where(lax.broadcasted_iota(jnp.int32, (1, 128), 1) < 64, -1.0, 1.0)
    ky_lanes = []
    for n in range(NARROW):
        number = lax.broadcasted_iota(jnp.int32, (1, 128), 1) % 64 + n * ROWS_Y
        ky_lanes.append(2.0 * math.pi / NY * signed(number, NY).astype(jnp.float32))
    kx_rows = 2.0 * math.pi / NX * lax.broadcasted_iota(jnp.int32, (KX, 1), 0).astype(jnp.float32)
    alternate = jnp.where(lax.broadcasted_iota(jnp.int32, (KX, 1), 0) % 2 == 0, 1.0, -1.0)
    weight = (
        jnp.where(lax.broadcasted_iota(jnp.int32, (KX, 1), 0) == 0, 1.0, 2.0) * norm_scale()
    )
    first_row = lax.broadcasted_iota(jnp.int32, (256, 1), 0) == 0

    def rows_of(field, n):
        return jnp.concatenate(
            [
                got_ref[pl.ds((w * NARROW + n) * chunk + field, ROWS_X, stride=SENT), :]
                for w in range(WIDE)
            ],
            0,
        )

    def synth(parts, index):
        spans = []
        for parity in range(2):
            if parity == 0:
                merged = [parts[0] + parts[2], parts[1] + parts[3]]
            else:
                merged = [parts[0] - parts[2], parts[1] - parts[3]]
            spans.append(
                dot3(
                    split(jnp.concatenate(merged, 1)), (sy_ref[parity, 0], sy_ref[parity, 1])
                )
            )
        real = jnp.concatenate([spans[0][:, :128], spans[1][:, :128]], 1)
        imag = jnp.concatenate([spans[0][:, 128:], spans[1][:, 128:]], 1)
        cosine = dot3((sx_ref[0, 0], sx_ref[0, 1]), split(real))
        sine = dot3((sx_ref[1, 0], sx_ref[1, 1]), split(imag))
        middle = jnp.sum(real * (alternate * weight), 0, keepdims=True)
        cell_ref[index, 0] = cosine + sine
        cell_ref[index, 1] = jnp.where(first_row, middle, cosine - sine)

    def each_field(field, carry):
        synth([rows_of(field, n) for n in range(NARROW)], field)
        return carry

    lax.fori_loop(0, SENT, each_field, 0)
    swirl = []
    for n in range(NARROW):
        across = kx_rows * rows_of(4, n) - ky_lanes[n] * rows_of(3, n)
        swirl.append(pltpu.roll(across, 64, 1) * half_sign)
    synth(swirl, SENT)

    def product(kind, c, mirror):
        one, two = (c + 1) % 3, (c + 2) % 3
        if kind == 0:
            return (
                cell_ref[one, mirror] * cell_ref[6 + two, mirror]
                - cell_ref[two, mirror] * cell_ref[6 + one, mirror]
            )
        return (
            cell_ref[3 + one, mirror] * cell_ref[two, mirror]
            - cell_ref[3 + two, mirror] * cell_ref[one, mirror]
        )

    def analyse(index, kind, c):
        ahead = product(kind, c, 0)
        behind = product(kind, c, 1)
        middle = behind[0:1]
        both = ahead + jnp.where(first_row, 0.0, behind)
        apart = ahead - behind
        real = dot3((ax_ref[0, 0], ax_ref[0, 1]), split(both))
        real = real + alternate[:KEPT_X] * norm_scale() * middle
        imag = dot3((ax_ref[1, 0], ax_ref[1, 1]), split(apart))
        spans = []
        for parity in range(2):
            lanes = slice(128 * parity, 128 * parity + 128)
            spans.append(
                dot3(
                    split(jnp.concatenate([real[:, lanes], imag[:, lanes]], 1)),
                    (ay_ref[parity, 0], ay_ref[parity, 1]),
                )
            )
        spec_ref[index, 0] = spans[0] + spans[1]
        spec_ref[index, 1] = spans[0] - spans[1]

    for kind in range(2):
        for c in range(3):
            analyse(3 * kind + c, kind, c)

    kx_kept = kx_rows[:KEPT_X]

    def times_i(value):
        return pltpu.roll(value, 64, 1) * half_sign

    out_ref[KEPT_X // ROWS_X :] = jnp.zeros(
        (WIDE - KEPT_X // ROWS_X, NARROW, BACK * ROWS_X, 128), jnp.float32
    )
    for n in range(NARROW):
        at = (n // 2, slice(None), slice(128 * (n % 2), 128 * (n % 2) + 128))
        item = [spec_ref[(index,) + at] for index in range(6)]
        ky = ky_lanes[n]
        values = [
            item[0] + times_i(ky * item[5]),
            item[1] - times_i(kx_kept * item[5]),
            item[2] + times_i(kx_kept * item[4] - ky * item[3]),
            item[3],
            item[4],
        ]
        for f in range(BACK):
            out_ref[: KEPT_X // ROWS_X, n, f * ROWS_X : (f + 1) * ROWS_X, :] = values[f].reshape(
                KEPT_X // ROWS_X, ROWS_X, 128
            )


def plane(got):
    tables = [tables_synth_y(), tables_synth_x(), tables_anal_x(), tables_anal_y()]
    return pl.pallas_call(
        plane_kernel,
        out_shape=jax.ShapeDtypeStruct((WIDE, NARROW, BACK * ROWS_X, 128), jnp.float32),
        in_specs=[pl.BlockSpec(memory_space=pltpu.VMEM)] * 5,
        out_specs=pl.BlockSpec(memory_space=pltpu.VMEM),
        scratch_shapes=[
            pltpu.VMEM((6, 2, KEPT_X, 256), jnp.float32),
            pltpu.VMEM((9, 2, 256, 256), jnp.float32),
            pltpu.VMEM((8, 128), jnp.float32),
        ],
        compiler_params=pltpu.CompilerParams(vmem_limit_bytes=vmem_bytes),
        name="plane",
    )(got.reshape(DEVICES * ROWS_X * SENT, 128), *[jnp.asarray(t) for t in tables])


def finish_kernel(place_ref, even_ref, odd_ref, adjoint_ref, table_ref, out_ref):
    k = pl.program_id(0)
    number_x = place_ref[0] * ROWS_X + k
    kx = 2.0 * math.pi / NX * number_x.astype(jnp.float32)
    number_y = signed(
        lax.broadcasted_iota(jnp.int32, (ROWS_Y, 1), 0) + place_ref[1] * ROWS_Y, NY
    )
    number_z = signed(lax.broadcasted_iota(jnp.int32, (1, NZ), 1), NZ)
    ky = 2.0 * math.pi / NY * number_y.astype(jnp.float32)
    kz = 2.0 * math.pi / NZ * number_z.astype(jnp.float32)
    table = (table_ref[0], table_ref[1])
    got = []
    for f in range(BACK):
        stacked = jnp.concatenate(
            [
                ref[pl.ds(f * ROWS_X + k, DEVICES, stride=BACK * ROWS_X), :]
                for ref in (even_ref, odd_ref)
            ],
            0,
        )
        span = dot3(split(stacked.T), table)
        real = span[:64, :256] + span[64:, 256:]
        imag = span[64:, :256] - span[:64, 256:]
        got.append((real, imag))
    conv = [
        (got[0][0] + kz * got[4][1], got[0][1] - kz * got[4][0]),
        (got[1][0] - kz * got[3][1], got[1][1] + kz * got[3][0]),
        got[2],
    ]
    keep = (
        (3 * number_x < NX) & (3 * jnp.abs(number_y) < NY) & (3 * jnp.abs(number_z) < NZ)
    ).astype(jnp.float32)
    ksquare = kx * kx + ky * ky + kz * kz
    inverse = 1.0 / (ksquare + (ksquare == 0).astype(jnp.float32))
    decay = jnp.exp(-viscous_rate * ksquare)
    waves = (kx, ky, kz)
    for part in range(2):
        along = (kx * conv[0][part] + ky * conv[1][part] + kz * conv[2][part]) * inverse
        for c in range(3):
            projected = keep * (conv[c][part] - waves[c] * along)
            out_ref[c, part, 0] = decay * (adjoint_ref[c, part, 0] + section_step * projected)


def finish(place, even, odd, adjoint_hat):
    whole = (3, 2, 1, ROWS_Y, NZ)
    table = tables_anal_z()
    flat = (DEVICES * BACK * ROWS_X, 128)
    return pl.pallas_call(
        finish_kernel,
        grid_spec=pltpu.PrefetchScalarGridSpec(
            num_scalar_prefetch=1,
            grid=(ROWS_X,),
            in_specs=[
                pl.BlockSpec(flat, lambda k, s: (0, 0)),
                pl.BlockSpec(flat, lambda k, s: (0, 0)),
                pl.BlockSpec(whole, lambda k, s: (0, 0, k, 0, 0)),
                pl.BlockSpec(table.shape, lambda k, s: (0, 0, 0)),
            ],
            out_specs=pl.BlockSpec(whole, lambda k, s: (0, 0, k, 0, 0)),
        ),
        out_shape=jax.ShapeDtypeStruct((3, 2, ROWS_X, ROWS_Y, NZ), jnp.float32),
        compiler_params=pltpu.CompilerParams(vmem_limit_bytes=vmem_bytes),
        name="finish",
    )(place, even.reshape(flat), odd.reshape(flat), adjoint_hat, jnp.asarray(table))


def swap(chunks):
    return lax.all_to_all(chunks, ("wide", "narrow"), 0, 0, tiled=True)


def local(adjoint_hat, velocity_hat):
    place = jnp.stack([lax.axis_index("wide"), lax.axis_index("narrow")]).astype(jnp.int32)
    sent = synth_z(place, adjoint_hat, velocity_hat)
    got = [swap(part) for part in sent]
    back = [
        swap(plane(part).reshape(DEVICES, BACK * ROWS_X, 128)) for part in got
    ]
    return finish(place, back[0], back[1], adjoint_hat)


def solution(mesh):
    in_specs = (P(None, None, "wide", "narrow", None), P(None, None, "wide", "narrow", None))
    out_specs = P(None, None, "wide", "narrow", None)
    return jax.shard_map(local, mesh=mesh, in_specs=in_specs, out_specs=out_specs, check_vma=False)
```

time: 791 us -> 236 us (0.30); the launches traced: 778 us -> 235 us
  local copies, waits for them, and re-layouts: 277 us -> 0.01 us
  starting transfers between devices: 192 us -> 15 us
  matrix products: 108 us -> 0 us
  other arithmetic: 107 us -> 0.55 us
  blocking collectives: 0 us -> 105 us
  Pallas kernels: 0 us -> 55.5 us
  waiting for transfers between devices: 91.9 us -> 58.6 us
    all_to_all x30 -> x2, starting transfers between devices: 192 us -> 15 us  [swap(): return lax.all_to_all(chunks, ('wide', 'narrow'), 0, 0, tiled=True)]
    dot_general x45 -> x0, matrix products: 108 us -> none  [contract(): return jnp.einsum(pattern, values, table, precision=highest)]
    all_to_all x0 -> x2, blocking collectives: none -> 105 us  [swap(): return lax.all_to_all(chunks, ('wide', 'narrow'), 0, 0, tiled=True)]
    all_to_all x15 -> x0, other arithmetic: 81.4 us -> none  [the longest x9 48.5 us: to_physical(): lax.all_to_all(depth, 'narrow', split_axis=0, concat_axis=4, tiled=True)]
    unnamed x160 -> x2, local copies, waits for them, and re-layouts: 77.5 us -> 0.01 us
    all_to_all x31 -> x0, local copies, waits for them, and re-layouts: 67.3 us -> none  [the longest x10 26.2 us: to_physical(): lax.all_to_all(depth, 'narrow', split_axis=0, concat_axis=4, tiled=True)]
    transpose x31 -> x0, local copies, waits for them, and re-layouts: 63.2 us -> none  [the longest x30 63.1 us: contract(): return jnp.einsum(pattern, values, table, precision=highest)]
    another operation x30 -> x0, local copies, waits for them, and re-layouts: 58.4 us -> none
  transfers between devices with their start and end apart: 30 -> 2, of which waited for: 22 -> 2; matrix products, arithmetic and copies ran while one was open for 57% -> 0% of each run, Pallas kernels for 0% -> 12%
where the time goes in v1:
time: 236 us; the launch traced here: 235 us
  blocking collectives  105 us (44%)
  waiting for transfers between devices  58.6 us (25%)
  Pallas kernels  55.5 us (24%)
  starting transfers between devices  15 us (6%)
    all_to_all x2, blocking collectives, swap(): return lax.all_to_all(chunks, ('wide', 'narrow'), 0, 0, tiled=True)  105 us
    all_to_all x2, waiting for transfers between devices, swap(): return lax.all_to_all(chunks, ('wide', 'narrow'), 0, 0, tiled=True)  58.6 us
    pallas_call x2, Pallas kernels, plane(): pl.pallas_call(plane_kernel, out_shape=jax.ShapeDtypeStruct((WIDE, NARROW...  29.2 us
    all_to_all x2, starting transfers between devices, swap(): return lax.all_to_all(chunks, ('wide', 'narrow'), 0, 0, tiled=True)  15 us
    pallas_call x1, Pallas kernels, synth_z(): pl.pallas_call(synth_z_kernel, grid_spec=pltpu.PrefetchScalarGridSpec(num...  14.3 us
    pallas_call x1, Pallas kernels, finish(): pl.pallas_call(finish_kernel, grid_spec=pltpu.PrefetchScalarGridSpec(num_...  12 us
  transfers between devices with their start and end apart: 2, of which 2 were waited for; matrix products, arithmetic and copies ran while one was open for 0% of the time, Pallas kernels for 12%

profile of v1, /device:TPU:0, one launch (start us, length us, event | category | flops | bytes accessed | tf_op | source)
XLA Modules:
  0.0 235.2 jit_solution(9586479153229143416)
XLA Ops:
  0.0 0.6 pad_add_fusion.place_ref
  0.6 14.3 %synth_z.1 = (f32[128,64,128]{2,1,0:T(8,128)}, f32[128,64,128]{2,1,0:T(8,128)}) custom-call(s32[2]{0:T(128)} %pad_add_fusion.place_ref, f32[3,2,8,64,256]{4,3,2,1,0:T(8,128)} %adjoint_ref.3, f32[3,2,8,64,256]{4,3,2,1,0:T(8,128)} %velocity_ref.1, bf16[2,2,128,256]{3,2,1,0:T(8,128)(2,1)} %constant.21.clone.table_ref), custom_call_target="tpu_custom_call" | custom-call | tf_op jit(solution)/shard_map/synth_z/pallas_call | solution.py:163
  14.9 63.8 %all_to_all.20 = f32[128,64,128]{2,1,0:T(8,128)} all-to-all(f32[128,64,128]{2,1,0:T(8,128)} %get-tuple-element.7), channel_id=1, replica_groups=mesh['narrow'=4,'wide'=32] {'wide','narrow'}, dimensions={0} | all-to-all | bytes 8388608 | tf_op jit(solution)/shard_map/all_to_all | solution.py:381
  78.7 7.8 %all-to-all-start.2 = ((f32[128,64,128]{2,1,0:T(8,128)}), f32[128,64,128]{2,1,0:T(8,128)}, u32[]{:S(2)}, u32[]{:S(2)}) async-start(f32[128,64,128]{2,1,0:T(8,128)} %get-tuple-element.8), calls=%async_computation.2 | async-start | bytes 8388608 | tf_op jit(solution)/shard_map/all_to_all | solution.py:381
  86.4 14.6 %plane.2 = f32[32,4,40,128]{3,2,1,0:T(8,128)} custom-call(f32[8192,128]{1,0:T(8,128)} %bitcast.8, bf16[2,2,256,256]{3,2,1,0:T(8,128)(2,1)} %constant.22.clone.sy_ref, bf16[2,2,256,256]{3,2,1,0:T(8,128)(2,1)} %constant.23.clone.sx_ref, bf16[2,2,176,256]{3,2,1,0:T(8,128)(2,1)} %constant.24.clone.ax_ref, bf16[2,2,256,256]{3,2,1,0:T(8,128)(2,1)} %constant.25.clone.ay_ref), custom_call_target="tpu_custom_call" | custom-call | tf_op jit(solution)/shard_map/plane/pallas_call | solution.py:299
  101.0 37.5 %all-to-all-done.2 = f32[128,64,128]{2,1,0:T(8,128)} async-done(((f32[128,64,128]{2,1,0:T(8,128)}), f32[128,64,128]{2,1,0:T(8,128)}, u32[]{:S(2)}, u32[]{:S(2)}) %all-to-all-start.2) | async-done | bytes 4194336 | tf_op jit(solution)/shard_map/all_to_all | solution.py:381
  138.6 7.2 %all-to-all-start.1 = ((f32[128,40,128]{2,1,0:T(8,128)}), f32[128,40,128]{2,1,0:T(8,128)S(1)}, u32[]{:S(2)}, u32[]{:S(2)}) async-start(f32[128,40,128]{2,1,0:T(8,128)} %bitcast.9), calls=%async_computation.1 | async-start | bytes 5242880 | tf_op jit(solution)/shard_map/all_to_all | solution.py:381
  145.8 14.6 %plane.3 = f32[32,4,40,128]{3,2,1,0:T(8,128)} custom-call(f32[8192,128]{1,0:T(8,128)} %bitcast.5.got_ref, bf16[2,2,256,256]{3,2,1,0:T(8,128)(2,1)} %constant.22.clone.sy_ref, bf16[2,2,256,256]{3,2,1,0:T(8,128)(2,1)} %constant.23.clone.sx_ref, bf16[2,2,176,256]{3,2,1,0:T(8,128)(2,1)} %constant.24.clone.ax_ref, bf16[2,2,256,256]{3,2,1,0:T(8,128)(2,1)} %constant.25.clone.ay_ref), custom_call_target="tpu_custom_call" | custom-call | tf_op jit(solution)/shard_map/plane/pallas_call | solution.py:299
  160.4 21.1 %all-to-all-done.1 = f32[128,40,128]{2,1,0:T(8,128)S(1)} async-done(((f32[128,40,128]{2,1,0:T(8,128)}), f32[128,40,128]{2,1,0:T(8,128)S(1)}, u32[]{:S(2)}, u32[]{:S(2)}) %all-to-all-start.1) | async-done | bytes 2621472 | tf_op jit(solution)/shard_map/all_to_all | solution.py:381
  181.5 0.0 copy-start
  181.5 41.7 %all_to_all.21 = f32[128,40,128]{2,1,0:T(8,128)} all-to-all(f32[128,40,128]{2,1,0:T(8,128)} %bitcast.10), channel_id=1, replica_groups=mesh['narrow'=4,'wide'=32] {'wide','narrow'}, dimensions={0} | all-to-all | bytes 5242880 | tf_op jit(solution)/shard_map/all_to_all | solution.py:381
  223.2 0.0 copy-done
  223.2 12.0 %finish.1 = f32[3,2,8,64,256]{4,3,2,1,0:T(8,128)} custom-call(s32[2]{0:T(128)} %pad_add_fusion.place_ref, f32[5120,128]{1,0:T(8,128)} %bitcast.11, f32[5120,128]{1,0:T(8,128)} %bitcast.12, f32[3,2,8,64,256]{4,3,2,1,0:T(8,128)} %adjoint_ref.3, bf16[2,256,512]{2,1,0:T(8,128)(2,1)} %constant.26.clone.table_ref), custom_call_target="tpu_custom_call" | custom-call | tf_op jit(solution)/shard_map/finish/pallas_call | solution.py:361
Async XLA Ops:
  78.7 59.9 %all-to-all-start.2 = ((f32[128,64,128]{2,1,0:T(8,128)}), f32[128,64,128]{2,1,0:T(8,128)}, u32[]{:S(2)}, u32[]{:S(2)}) async-start(f32[128,64,128]{2,1,0:T(8,128)} %get-tuple-element.8), calls=%async_computation.2 | async-start | bytes 8388608 | tf_op jit(solution)/shard_map/all_to_all | solution.py:381
  138.6 43.0 %all-to-all-start.1 = ((f32[128,40,128]{2,1,0:T(8,128)}), f32[128,40,128]{2,1,0:T(8,128)S(1)}, u32[]{:S(2)}, u32[]{:S(2)}) async-start(f32[128,40,128]{2,1,0:T(8,128)} %bitcast.9), calls=%async_computation.1 | async-start | bytes 5242880 | tf_op jit(solution)/shard_map/all_to_all | solution.py:381
  181.5 41.7 %copy-start = (f32[128,40,128]{2,1,0:T(8,128)}, f32[128,40,128]{2,1,0:T(8,128)S(1)}, u32[]{:S(2)}) copy-start(f32[128,40,128]{2,1,0:T(8,128)S(1)} %all-to-all-done.1) | copy-start | bytes 7864324

commit v2 on v1

--- a/solution.py
+++ b/solution.py
@@ -1,3 +1,4 @@
+import functools
 import math
 
 import jax
@@ -21,6 +22,11 @@
 SENT = 8
 BACK = 5
 KEPT_X = 176
+KEPT_W = KEPT_X // ROWS_X
+HEAVY = (0, 3)
+LIGHT = (1, 2)
+LIGHT_ROW = (0, 40)
+SLOT = 24
 
 section_step = 0.25
 viscous_rate = 0.05
@@ -125,8 +131,7 @@
     return 2.0 * math.pi / NZ * signed(number, NZ).astype(jnp.float32)
 
 
-def synth_z_kernel(place_ref, adjoint_ref, velocity_ref, table_ref, even_ref, odd_ref):
-    outs = (even_ref, odd_ref)
+def synth_z_kernel(plane, place_ref, adjoint_ref, velocity_ref, table_ref, out_ref):
     ky = wave_y(place_ref[1] * ROWS_Y, (ROWS_Y, 1), 0)
     kz = wave_z((1, NZ), 1)
     vel = [[velocity_ref[c, part, 0] for part in range(2)] for c in range(3)]
@@ -137,48 +142,49 @@
     number_x = place_ref[0] * ROWS_X + pl.program_id(0)
     kx = 2.0 * math.pi / NX * number_x.astype(jnp.float32)
     fields[7] = (kx * vel[2][1] - kz * vel[0][1], kz * vel[0][0] - kx * vel[2][0])
-    for plane in range(2):
-        table = (table_ref[plane, 0], table_ref[plane, 1])
-        for pair in range(SENT // 2):
-            blocks = []
-            for real, imag in fields[2 * pair : 2 * pair + 2]:
-                if plane == 0:
-                    low_r = real[:, :128] + real[:, 128:]
-                    low_i = imag[:, :128] + imag[:, 128:]
-                else:
-                    low_r = real[:, :128] - real[:, 128:]
-                    low_i = imag[:, :128] - imag[:, 128:]
-                blocks.append(jnp.concatenate([low_r, -low_i], 1))
-                blocks.append(jnp.concatenate([low_i, low_r], 1))
-            value = dot3(table, split(jnp.concatenate(blocks, 0)), ((1,), (1,)))
-            outs[plane][:, 2 * pair, :] = value[:, :128]
-            outs[plane][:, 2 * pair + 1, :] = value[:, 128:]
-
-
-def synth_z(place, adjoint_hat, velocity_hat):
+    table = (table_ref[0], table_ref[1])
+    for pair in range(SENT // 2):
+        blocks = []
+        for real, imag in fields[2 * pair : 2 * pair + 2]:
+            if plane == 0:
+                low_r = real[:, :128] + real[:, 128:]
+                low_i = imag[:, :128] + imag[:, 128:]
+            else:
+                low_r = real[:, :128] - real[:, 128:]
+                low_i = imag[:, :128] - imag[:, 128:]
+            blocks.append(jnp.concatenate([low_r, -low_i], 1))
+            blocks.append(jnp.concatenate([low_i, low_r], 1))
+        value = dot3(table, split(jnp.concatenate(blocks, 0)), ((1,), (1,)))
+        out_ref[:, 2 * pair, :] = value[:, :128]
+        out_ref[:, 2 * pair + 1, :] = value[:, 128:]
+
+
+def synth_z(place, adjoint_hat, velocity_hat, plane):
     whole = (3, 2, 1, ROWS_Y, NZ)
-    table = tables_synth_z()
-    shape = jax.ShapeDtypeStruct((DEVICES, ROWS_X * SENT, 128), jnp.float32)
-    out_spec = pl.BlockSpec((DEVICES, SENT, 128), lambda k, s: (0, k, 0))
+    table = tables_synth_z()[plane]
     return pl.pallas_call(
-        synth_z_kernel,
+        functools.partial(synth_z_kernel, plane),
         grid_spec=pltpu.PrefetchScalarGridSpec(
             num_scalar_prefetch=1,
             grid=(ROWS_X,),
             in_specs=[
                 pl.BlockSpec(whole, lambda k, s: (0, 0, k, 0, 0)),
                 pl.BlockSpec(whole, lambda k, s: (0, 0, k, 0, 0)),
-                pl.BlockSpec(table.shape, lambda k, s: (0, 0, 0, 0)),
+                pl.BlockSpec(table.shape, lambda k, s: (0, 0, 0)),
             ],
-            out_specs=[out_spec, out_spec],
+            out_specs=pl.BlockSpec((DEVICES, SENT, 128), lambda k, s: (0, k, 0)),
         ),
-        out_shape=[shape, shape],
+        out_shape=jax.ShapeDtypeStruct((DEVICES, ROWS_X * SENT, 128), jnp.float32),
         compiler_params=pltpu.CompilerParams(vmem_limit_bytes=vmem_bytes),
         name="synth_z",
     )(place, adjoint_hat, velocity_hat, jnp.asarray(table))
 
 
-def plane_kernel(got_ref, sy_ref, sx_ref, ax_ref, ay_ref, out_ref, spec_ref, cell_ref, anal_ref):
+def plane_kernel(plane, got_ref, sy_ref, sx_ref, ax_ref, ay_ref, *refs):
+    if plane == 0:
+        out_ref, rest_ref, spec_ref, cell_ref = refs
+    else:
+        rest_ref, out_ref, spec_ref, cell_ref = refs
     chunk = ROWS_X * SENT
     half_sign = jnp.where(lax.broadcasted_iota(jnp.int32, (1, 128), 1) < 64, -1.0, 1.0)
     ky_lanes = []
@@ -274,98 +280,174 @@
     def times_i(value):
         return pltpu.roll(value, 64, 1) * half_sign
 
-    out_ref[KEPT_X // ROWS_X :] = jnp.zeros(
-        (WIDE - KEPT_X // ROWS_X, NARROW, BACK * ROWS_X, 128), jnp.float32
-    )
-    for n in range(NARROW):
+    out_ref[KEPT_W:] = jnp.zeros((WIDE - KEPT_W,) + out_ref.shape[1:], jnp.float32)
+    if plane == 0:
+        rest_ref[KEPT_W:] = jnp.zeros((WIDE - KEPT_W,) + rest_ref.shape[1:], jnp.float32)
+
+    def put(n, tile, value):
+        rows = slice(tile * ROWS_X, tile * ROWS_X + ROWS_X)
+        out_ref[:KEPT_W, n, rows, :] = value.reshape(KEPT_W, ROWS_X, 128)
+
+    def values_of(n):
         at = (n // 2, slice(None), slice(128 * (n % 2), 128 * (n % 2) + 128))
         item = [spec_ref[(index,) + at] for index in range(6)]
         ky = ky_lanes[n]
-        values = [
+        return [
             item[0] + times_i(ky * item[5]),
             item[1] - times_i(kx_kept * item[5]),
             item[2] + times_i(kx_kept * item[4] - ky * item[3]),
             item[3],
             item[4],
         ]
+
+    lane = lax.broadcasted_iota(jnp.int32, (1, 128), 1)
+    for half in range(2):
+        heavy, light = HEAVY[half], LIGHT[half]
+        values = values_of(heavy)
+        direct = 3 if plane == 0 else 4
         for f in range(BACK):
-            out_ref[: KEPT_X // ROWS_X, n, f * ROWS_X : (f + 1) * ROWS_X, :] = values[f].reshape(
-                KEPT_X // ROWS_X, ROWS_X, 128
-            )
-
-
-def plane(got):
+            if f < direct:
+                put(heavy, f, values[f])
+            else:
+                put(light, f - direct if plane == 0 else 3, values[f])
+        values = values_of(light)
+        packed = []
+        for tile in range(2):
+            value = jnp.zeros((KEPT_X, 128), jnp.float32)
+            for slot in range(5):
+                f, part = divmod(5 * tile + slot, 2)
+                moved = pltpu.roll(
+                    values[f], (SLOT * slot - 64 * part - LIGHT_ROW[half]) % 128, 1
+                )
+                value = jnp.where((lane >= SLOT * slot) & (lane < SLOT * slot + SLOT), moved, value)
+            packed.append(value)
+        if plane == 0:
+            put(light, 2, packed[0])
+            rest_ref[:KEPT_W, half] = packed[1].reshape(KEPT_W, ROWS_X, 128)
+        else:
+            out_ref[:, light, 0:ROWS_X, :] = rest_ref[:, half]
+            put(light, 1, packed[0])
+            put(light, 2, packed[1])
+
+
+def run_plane(plane, got, rest=None):
     tables = [tables_synth_y(), tables_synth_x(), tables_anal_x(), tables_anal_y()]
-    return pl.pallas_call(
-        plane_kernel,
-        out_shape=jax.ShapeDtypeStruct((WIDE, NARROW, BACK * ROWS_X, 128), jnp.float32),
-        in_specs=[pl.BlockSpec(memory_space=pltpu.VMEM)] * 5,
-        out_specs=pl.BlockSpec(memory_space=pltpu.VMEM),
+    tiles = 3 + plane
+    out_shape = [jax.ShapeDtypeStruct((WIDE, NARROW, tiles * ROWS_X, 128), jnp.float32)]
+    operands = [got.reshape(DEVICES * ROWS_X * SENT, 128)] + [jnp.asarray(t) for t in tables]
+    if plane == 0:
+        out_shape.append(jax.ShapeDtypeStruct((WIDE, 2, ROWS_X, 128), jnp.float32))
+    else:
+        operands.append(rest)
+    outs = pl.pallas_call(
+        functools.partial(plane_kernel, plane),
+        out_shape=out_shape,
+        in_specs=[pl.BlockSpec(memory_space=pltpu.VMEM)] * len(operands),
+        out_specs=[pl.BlockSpec(memory_space=pltpu.VMEM)] * len(out_shape),
         scratch_shapes=[
             pltpu.VMEM((6, 2, KEPT_X, 256), jnp.float32),
             pltpu.VMEM((9, 2, 256, 256), jnp.float32),
-            pltpu.VMEM((8, 128), jnp.float32),
         ],
         compiler_params=pltpu.CompilerParams(vmem_limit_bytes=vmem_bytes),
         name="plane",
-    )(got.reshape(DEVICES * ROWS_X * SENT, 128), *[jnp.asarray(t) for t in tables])
-
-
-def finish_kernel(place_ref, even_ref, odd_ref, adjoint_ref, table_ref, out_ref):
+    )(*operands)
+    return [outs[0].reshape(DEVICES, tiles * ROWS_X, 128)] + list(outs[1:])
+
+
+def finish_kernel(
+    place_ref, got0_ref, got1_ref, more0_ref, more1_ref, adjoint_ref, table_ref, out_ref
+):
     k = pl.program_id(0)
+    narrow = place_ref[1]
     number_x = place_ref[0] * ROWS_X + k
     kx = 2.0 * math.pi / NX * number_x.astype(jnp.float32)
-    number_y = signed(
-        lax.broadcasted_iota(jnp.int32, (ROWS_Y, 1), 0) + place_ref[1] * ROWS_Y, NY
-    )
     number_z = signed(lax.broadcasted_iota(jnp.int32, (1, NZ), 1), NZ)
-    ky = 2.0 * math.pi / NY * number_y.astype(jnp.float32)
     kz = 2.0 * math.pi / NZ * number_z.astype(jnp.float32)
     table = (table_ref[0], table_ref[1])
-    got = []
-    for f in range(BACK):
-        stacked = jnp.concatenate(
-            [
-                ref[pl.ds(f * ROWS_X + k, DEVICES, stride=BACK * ROWS_X), :]
-                for ref in (even_ref, odd_ref)
-            ],
-            0,
+
+    def span_of(first, second):
+        rows = [
+            ref[pl.ds(tile * ROWS_X + k, DEVICES, stride=tiles * ROWS_X), :]
+            for ref, tile, tiles in (first, second)
+        ]
+        return dot3(split(jnp.concatenate(rows, 0).T), table)
+
+    def unite(real_rows, imag_rows):
+        return (
+            real_rows[:, :NZ] + imag_rows[:, NZ:],
+            imag_rows[:, :NZ] - real_rows[:, NZ:],
         )
-        span = dot3(split(stacked.T), table)
-        real = span[:64, :256] + span[64:, 256:]
-        imag = span[64:, :256] - span[:64, 256:]
-        got.append((real, imag))
-    conv = [
-        (got[0][0] + kz * got[4][1], got[0][1] - kz * got[4][0]),
-        (got[1][0] - kz * got[3][1], got[1][1] + kz * got[3][0]),
-        got[2],
-    ]
-    keep = (
-        (3 * number_x < NX) & (3 * jnp.abs(number_y) < NY) & (3 * jnp.abs(number_z) < NZ)
-    ).astype(jnp.float32)
-    ksquare = kx * kx + ky * ky + kz * kz
-    inverse = 1.0 / (ksquare + (ksquare == 0).astype(jnp.float32))
-    decay = jnp.exp(-viscous_rate * ksquare)
-    waves = (kx, ky, kz)
-    for part in range(2):
-        along = (kx * conv[0][part] + ky * conv[1][part] + kz * conv[2][part]) * inverse
+
+    def emit(got, start, rows):
+        number_y = lax.broadcasted_iota(jnp.int32, (rows, 1), 0) + start + narrow * ROWS_Y
+        number_y = signed(number_y, NY)
+        ky = 2.0 * math.pi / NY * number_y.astype(jnp.float32)
+        conv = [
+            (got[0][0] + kz * got[4][1], got[0][1] - kz * got[4][0]),
+            (got[1][0] - kz * got[3][1], got[1][1] + kz * got[3][0]),
+            got[2],
+        ]
+        keep = (
+            (3 * number_x < NX) & (3 * jnp.abs(number_y) < NY) & (3 * jnp.abs(number_z) < NZ)
+        ).astype(jnp.float32)
+        ksquare = kx * kx + ky * ky + kz * kz
+        inverse = 1.0 / (ksquare + (ksquare == 0).astype(jnp.float32))
+        decay = jnp.exp(-viscous_rate * ksquare)
+        waves = (kx, ky, kz)
+        for part in range(2):
+            along = (kx * conv[0][part] + ky * conv[1][part] + kz * conv[2][part]) * inverse
+            for c in range(3):
+                projected = keep * (conv[c][part] - waves[c] * along)
+                old = adjoint_ref[c, part, 0, pl.ds(start, rows), :]
+                out_ref[c, part, 0, pl.ds(start, rows), :] = decay * (
+                    old + section_step * projected
+                )
+
+    is_light = (narrow == LIGHT[0]) | (narrow == LIGHT[1])
+
+    @pl.when(jnp.logical_not(is_light))
+    def _():
+        got = []
+        for f in range(BACK):
+            first = (got0_ref, f, 3) if f < 3 else (more0_ref, f - 3, 2)
+            second = (got1_ref, f, 4) if f < 4 else (more1_ref, 0, 1)
+            span = span_of(first, second)
+            got.append(unite(span[:64], span[64:]))
+        emit(got, 0, ROWS_Y)
+
+    @pl.when(is_light)
+    def _():
+        spans = [
+            span_of((got0_ref, 2, 3), (got1_ref, 1, 4)),
+            span_of((got1_ref, 0, 4), (got1_ref, 2, 4)),
+        ]
+
+        def item(index):
+            tile, slot = divmod(index, 5)
+            return spans[tile][SLOT * slot : SLOT * slot + SLOT]
+
+        number_y = lax.broadcasted_iota(jnp.int32, (ROWS_Y, 1), 0) + narrow * ROWS_Y
+        ky = 2.0 * math.pi / NY * signed(number_y, NY).astype(jnp.float32)
+        decay = jnp.exp(-viscous_rate * (kx * kx + ky * ky + kz * kz))
         for c in range(3):
-            projected = keep * (conv[c][part] - waves[c] * along)
-            out_ref[c, part, 0] = decay * (adjoint_ref[c, part, 0] + section_step * projected)
-
-
-def finish(place, even, odd, adjoint_hat):
+            for part in range(2):
+                out_ref[c, part, 0] = decay * adjoint_ref[c, part, 0]
+        got = [unite(item(2 * f), item(2 * f + 1)) for f in range(BACK)]
+        start = jnp.where(narrow == LIGHT[0], 0, LIGHT_ROW[1])
+        emit(got, pl.multiple_of(start, 8), SLOT)
+
+
+def finish(place, arrays, adjoint_hat):
     whole = (3, 2, 1, ROWS_Y, NZ)
     table = tables_anal_z()
-    flat = (DEVICES * BACK * ROWS_X, 128)
+    flats = [array.reshape(-1, 128) for array in arrays]
     return pl.pallas_call(
         finish_kernel,
         grid_spec=pltpu.PrefetchScalarGridSpec(
             num_scalar_prefetch=1,
             grid=(ROWS_X,),
-            in_specs=[
-                pl.BlockSpec(flat, lambda k, s: (0, 0)),
-                pl.BlockSpec(flat, lambda k, s: (0, 0)),
+            in_specs=[pl.BlockSpec(flat.shape, lambda k, s: (0, 0)) for flat in flats]
+            + [
                 pl.BlockSpec(whole, lambda k, s: (0, 0, k, 0, 0)),
                 pl.BlockSpec(table.shape, lambda k, s: (0, 0, 0)),
             ],
@@ -374,21 +456,27 @@
         out_shape=jax.ShapeDtypeStruct((3, 2, ROWS_X, ROWS_Y, NZ), jnp.float32),
         compiler_params=pltpu.CompilerParams(vmem_limit_bytes=vmem_bytes),
         name="finish",
-    )(place, even.reshape(flat), odd.reshape(flat), adjoint_hat, jnp.asarray(table))
+    )(place, *flats, adjoint_hat, jnp.asarray(table))
 
 
 def swap(chunks):
     return lax.all_to_all(chunks, ("wide", "narrow"), 0, 0, tiled=True)
 
 
+def forward(tiles):
+    return lax.ppermute(tiles, "narrow", [(LIGHT[0], HEAVY[0]), (LIGHT[1], HEAVY[1])])
+
+
 def local(adjoint_hat, velocity_hat):
     place = jnp.stack([lax.axis_index("wide"), lax.axis_index("narrow")]).astype(jnp.int32)
-    sent = synth_z(place, adjoint_hat, velocity_hat)
-    got = [swap(part) for part in sent]
-    back = [
-        swap(plane(part).reshape(DEVICES, BACK * ROWS_X, 128)) for part in got
-    ]
-    return finish(place, back[0], back[1], adjoint_hat)
+    got = [swap(synth_z(place, adjoint_hat, velocity_hat, plane)) for plane in range(2)]
+    out0, rest = run_plane(0, got[0])
+    back0 = swap(out0)
+    (out1,) = run_plane(1, got[1], rest)
+    back1 = swap(out1)
+    more0 = forward(back0[:, : 2 * ROWS_X])
+    more1 = forward(back1[:, 3 * ROWS_X :])
+    return finish(place, [back0, back1, more0, more1], adjoint_hat)
 
 
 def solution(mesh):

time: 236 us -> 222 us (0.941)
  blocking collectives: 105 us -> 0 us
  waiting for transfers between devices: 58.6 us -> 119 us
  starting transfers between devices: 15 us -> 35 us
  Pallas kernels: 55.5 us -> 63.7 us
  local copies, waits for them, and re-layouts: 0.01 us -> 3.3 us
    all_to_all x2 -> x0, blocking collectives: 105 us -> none  [swap(): return lax.all_to_all(chunks, ('wide', 'narrow'), 0, 0, tiled=True)]
    all_to_all x2 -> x4, waiting for transfers between devices: 58.6 us -> 116 us  [swap(): return lax.all_to_all(chunks, ('wide', 'narrow'), 0, 0, tiled=True)]
    all_to_all x2 -> x4, starting transfers between devices: 15 us -> 32.5 us  [swap(): return lax.all_to_all(chunks, ('wide', 'narrow'), 0, 0, tiled=True)]
    pallas_call x3 -> x4, Pallas kernels: 43.5 us -> 50.8 us  [the longest x2 29.1 us: run_plane(): pl.pallas_call(functools.partial(plane_kernel, plane), out_shape=out_shap...]
    ppermute x0 -> x2, starting transfers between devices: none -> 2.57 us  [forward(): lax.ppermute(tiles, 'narrow', [(LIGHT[0], HEAVY[0]), (LIGHT[1], HEAVY[1])])]
    ppermute x0 -> x2, waiting for transfers between devices: none -> 2.51 us  [forward(): lax.ppermute(tiles, 'narrow', [(LIGHT[0], HEAVY[0]), (LIGHT[1], HEAVY[1])])]
  transfers between devices with their start and end apart: 2 -> 6, of which waited for: 2 -> 5; matrix products, arithmetic and copies ran while one was open for 0% -> 1% of each run, Pallas kernels for 12% -> 18%
where the time goes in v2:
time: 222 us; the launch traced here: 221 us
  waiting for transfers between devices  119 us (54%)
  Pallas kernels  63.7 us (29%)
  starting transfers between devices  35 us (16%)
  local copies, waits for them, and re-layouts  3.3 us (1%)
    all_to_all x4, waiting for transfers between devices, swap(): return lax.all_to_all(chunks, ('wide', 'narrow'), 0, 0, tiled=True)  116 us
    all_to_all x4, starting transfers between devices, swap(): return lax.all_to_all(chunks, ('wide', 'narrow'), 0, 0, tiled=True)  32.5 us
    pallas_call x2, Pallas kernels, run_plane(): pl.pallas_call(functools.partial(plane_kernel, plane), out_shape=out_shap...  29.1 us
    pallas_call x2, Pallas kernels, synth_z(): pl.pallas_call(functools.partial(synth_z_kernel, plane), grid_spec=pltpu....  21.7 us
    pallas_call x1, Pallas kernels, finish(): pl.pallas_call(finish_kernel, grid_spec=pltpu.PrefetchScalarGridSpec(num_...  12.9 us
  transfers between devices with their start and end apart: 6, of which 5 were waited for; matrix products, arithmetic and copies ran while one was open for 1% of the time, Pallas kernels for 18%

profile of v2, /device:TPU:0, one launch (start us, length us, event | category | flops | bytes accessed | tf_op | source)
XLA Modules:
  0.0 221.3 jit_solution(7485891558810429197)
XLA Ops:
  0.0 0.6 pad_add_fusion.place_ref
  0.6 10.8 %synth_z.2 = f32[128,64,128]{2,1,0:T(8,128)} custom-call(s32[2]{0:T(128)} %pad_add_fusion.place_ref, f32[3,2,8,64,256]{4,3,2,1,0:T(8,128)} %adjoint_ref.5, f32[3,2,8,64,256]{4,3,2,1,0:T(8,128)} %velocity_ref.3, bf16[2,128,256]{2,1,0:T(8,128)(2,1)} %constant.23.clone.table_ref), custom_call_target="tpu_custom_call" | custom-call | tf_op jit(solution)/shard_map/synth_z/pallas_call | solution.py:165
  11.4 11.7 %all-to-all-start = ((f32[128,64,128]{2,1,0:T(8,128)}), f32[128,64,128]{2,1,0:T(8,128)}, u32[]{:S(2)}, u32[]{:S(2)}) async-start(f32[128,64,128]{2,1,0:T(8,128)} %synth_z.2), calls=%async_computation | async-start | bytes 8388608 | tf_op jit(solution)/shard_map/all_to_all | solution.py:463
  23.1 10.9 %synth_z.3 = f32[128,64,128]{2,1,0:T(8,128)} custom-call(s32[2]{0:T(128)} %pad_add_fusion.place_ref, f32[3,2,8,64,256]{4,3,2,1,0:T(8,128)} %adjoint_ref.5, f32[3,2,8,64,256]{4,3,2,1,0:T(8,128)} %velocity_ref.3, bf16[2,128,256]{2,1,0:T(8,128)(2,1)} %constant.24.clone.table_ref), custom_call_target="tpu_custom_call" | custom-call | tf_op jit(solution)/shard_map/synth_z/pallas_call | solution.py:165
  33.9 41.3 %all-to-all-done = f32[128,64,128]{2,1,0:T(8,128)} async-done(((f32[128,64,128]{2,1,0:T(8,128)}), f32[128,64,128]{2,1,0:T(8,128)}, u32[]{:S(2)}, u32[]{:S(2)}) %all-to-all-start) | async-done | bytes 4194336 | tf_op jit(solution)/shard_map/all_to_all | solution.py:463
  75.2 7.8 %all-to-all-start.2 = ((f32[128,64,128]{2,1,0:T(8,128)}), f32[128,64,128]{2,1,0:T(8,128)}, u32[]{:S(2)}, u32[]{:S(2)}) async-start(f32[128,64,128]{2,1,0:T(8,128)} %synth_z.3), calls=%async_computation.2 | async-start | bytes 8388608 | tf_op jit(solution)/shard_map/all_to_all | solution.py:463
  83.0 14.5 %plane.2 = (f32[32,4,24,128]{3,2,1,0:T(8,128)}, f32[32,2,8,128]{3,2,1,0:T(8,128)}) custom-call(f32[8192,128]{1,0:T(8,128)} %bitcast.2.got_ref, bf16[2,2,256,256]{3,2,1,0:T(8,128)(2,1)} %constant.25.clone.sy_ref, bf16[2,2,256,256]{3,2,1,0:T(8,128)(2,1)} %constant.26.clone.sx_ref, bf16[2,2,176,256]{3,2,1,0:T(8,128)(2,1)} %constant.27.clone.ax_ref, ...), custom_call_target="tpu_custom_call" | custom-call | tf_op jit(solution)/shard_map/plane/pallas_call | solution.py:342
  97.4 37.6 %all-to-all-done.2 = f32[128,64,128]{2,1,0:T(8,128)} async-done(((f32[128,64,128]{2,1,0:T(8,128)}), f32[128,64,128]{2,1,0:T(8,128)}, u32[]{:S(2)}, u32[]{:S(2)}) %all-to-all-start.2) | async-done | bytes 4194336 | tf_op jit(solution)/shard_map/all_to_all | solution.py:463
  135.1 7.2 %all-to-all-start.1 = ((f32[128,24,128]{2,1,0:T(8,128)}), f32[128,24,128]{2,1,0:T(8,128)S(1)}, u32[]{:S(2)}, u32[]{:S(2)}) async-start(f32[128,24,128]{2,1,0:T(8,128)} %bitcast.12), calls=%async_computation.1 | async-start | bytes 3145728 | tf_op jit(solution)/shard_map/all_to_all | solution.py:463
  142.3 14.6 %plane.3 = f32[32,4,32,128]{3,2,1,0:T(8,128)} custom-call(f32[8192,128]{1,0:T(8,128)} %bitcast.5.got_ref, bf16[2,2,256,256]{3,2,1,0:T(8,128)(2,1)} %constant.25.clone.sy_ref, bf16[2,2,256,256]{3,2,1,0:T(8,128)(2,1)} %constant.26.clone.sx_ref, bf16[2,2,176,256]{3,2,1,0:T(8,128)(2,1)} %constant.27.clone.ax_ref, ...), custom_call_target="tpu_custom_call" | custom-call | tf_op jit(solution)/shard_map/plane/pallas_call | solution.py:342
  157.0 9.8 %all-to-all-done.1 = f32[128,24,128]{2,1,0:T(8,128)S(1)} async-done(((f32[128,24,128]{2,1,0:T(8,128)}), f32[128,24,128]{2,1,0:T(8,128)S(1)}, u32[]{:S(2)}, u32[]{:S(2)}) %all-to-all-start.1) | async-done | bytes 1572896 | tf_op jit(solution)/shard_map/all_to_all | solution.py:463
  166.8 0.0 copy-start
  166.8 5.8 %all-to-all-start.3 = ((f32[128,32,128]{2,1,0:T(8,128)}), f32[128,32,128]{2,1,0:T(8,128)}, u32[]{:S(2)}, u32[]{:S(2)}) async-start(f32[128,32,128]{2,1,0:T(8,128)} %bitcast.11), calls=%async_computation.3 | async-start | bytes 4194304 | tf_op jit(solution)/shard_map/all_to_all | solution.py:463
  172.6 1.1 slice.8
  173.7 0.0 copy-done
  173.7 1.3 collective-permute-start
  175.0 27.4 %all-to-all-done.3 = f32[128,32,128]{2,1,0:T(8,128)} async-done(((f32[128,32,128]{2,1,0:T(8,128)}), f32[128,32,128]{2,1,0:T(8,128)}, u32[]{:S(2)}, u32[]{:S(2)}) %all-to-all-start.3) | async-done | bytes 2097184 | tf_op jit(solution)/shard_map/all_to_all | solution.py:463
  202.3 1.1 slice.9
  203.4 1.3 collective-permute-start.1
  204.7 2.5 %collective-permute-done.1 = f32[128,8,128]{2,1,0:T(8,128)S(1)} collective-permute-done((f32[128,8,128]{2,1,0:T(8,128)S(1)}, f32[128,8,128]{2,1,0:T(8,128)S(1)}, u32[]{:S(2)}, u32[]{:S(2)}) %collective-permute-start.1) | collective-permute-done | bytes 524320 | tf_op jit(solution)/shard_map/ppermute | solution.py:467
  207.2 0.0 copy-start.2
  207.2 0.0 collective-permute-done
  207.2 0.0 copy-start.1
  207.2 0.8 copy-done.2
  208.0 0.4 copy-done.1
  208.4 12.9 %finish.1 = f32[3,2,8,64,256]{4,3,2,1,0:T(8,128)} custom-call(s32[2]{0:T(128)} %pad_add_fusion.place_ref, f32[3072,128]{1,0:T(8,128)} %bitcast.10, f32[4096,128]{1,0:T(8,128)} %bitcast.7.got1_ref, f32[2048,128]{1,0:T(8,128)} %bitcast.13, f32[1024,128]{1,0:T(8,128)} %bitcast.14, f32[3,2,8,64,256]{4,3,2,1,0:T(8,128)} %adjoint_ref.5, ...), custom_call_target="tpu_custom_call" | custom-call | tf_op jit(solution)/shard_map/finish/pallas_call | solution.py:444
Async XLA Ops:
  11.4 63.8 %all-to-all-start = ((f32[128,64,128]{2,1,0:T(8,128)}), f32[128,64,128]{2,1,0:T(8,128)}, u32[]{:S(2)}, u32[]{:S(2)}) async-start(f32[128,64,128]{2,1,0:T(8,128)} %synth_z.2), calls=%async_computation | async-start | bytes 8388608 | tf_op jit(solution)/shard_map/all_to_all | solution.py:463
  75.2 59.9 %all-to-all-start.2 = ((f32[128,64,128]{2,1,0:T(8,128)}), f32[128,64,128]{2,1,0:T(8,128)}, u32[]{:S(2)}, u32[]{:S(2)}) async-start(f32[128,64,128]{2,1,0:T(8,128)} %synth_z.3), calls=%async_computation.2 | async-start | bytes 8388608 | tf_op jit(solution)/shard_map/all_to_all | solution.py:463
  135.1 31.7 %all-to-all-start.1 = ((f32[128,24,128]{2,1,0:T(8,128)}), f32[128,24,128]{2,1,0:T(8,128)S(1)}, u32[]{:S(2)}, u32[]{:S(2)}) async-start(f32[128,24,128]{2,1,0:T(8,128)} %bitcast.12), calls=%async_computation.1 | async-start | bytes 3145728 | tf_op jit(solution)/shard_map/all_to_all | solution.py:463
  166.8 6.9 %copy-start = (f32[128,24,128]{2,1,0:T(8,128)}, f32[128,24,128]{2,1,0:T(8,128)S(1)}, u32[]{:S(2)}) copy-start(f32[128,24,128]{2,1,0:T(8,128)S(1)} %all-to-all-done.1) | copy-start | bytes 4718596
  166.8 35.5 %all-to-all-start.3 = ((f32[128,32,128]{2,1,0:T(8,128)}), f32[128,32,128]{2,1,0:T(8,128)}, u32[]{:S(2)}, u32[]{:S(2)}) async-start(f32[128,32,128]{2,1,0:T(8,128)} %bitcast.11), calls=%async_computation.3 | async-start | bytes 4194304 | tf_op jit(solution)/shard_map/all_to_all | solution.py:463
  173.7 33.6 %collective-permute-start = (f32[128,16,128]{2,1,0:T(8,128)}, f32[128,16,128]{2,1,0:T(8,128)S(1)}, u32[]{:S(2)}, u32[]{:S(2)}) collective-permute-start(f32[128,16,128]{2,1,0:T(8,128)} %slice.8), channel_id=1, source_target_pairs={{32,0},{64,96},{33,1},{65,97},{34,2},{66,98},{35,3},{67,99},{36,4}... | collective-permute-start | bytes 3145736 | tf_op jit(solution)/shard_map/ppermute | solution.py:467
  203.4 3.8 %collective-permute-start.1 = (f32[128,8,128]{2,1,0:T(8,128)S(1)}, f32[128,8,128]{2,1,0:T(8,128)S(1)}, u32[]{:S(2)}, u32[]{:S(2)}) collective-permute-start(f32[128,8,128]{2,1,0:T(8,128)S(1)} %slice.9), channel_id=1, source_target_pairs={{32,0},{64,96},{33,1},{65,97},{34,2},{66,98},{35,3},{67,99},{36,4}... | collective-permute-start | bytes 1572872 | tf_op jit(solution)/shard_map/ppermute | solution.py:467
  207.2 0.8 copy-start.2
  207.2 1.2 copy-start.1

commit v3 on v2

v3 whole, which is shorter than its diff:
```python
import functools
import math

import jax
import jax.numpy as jnp
import ml_dtypes
import numpy as np
from jax import lax
from jax.experimental import pallas as pl
from jax.experimental.pallas import tpu as pltpu
from jax.sharding import PartitionSpec as P

NX = 512
NY = 256
NZ = 256
KX = 256
ROWS_X = 8
ROWS_Y = 64
WIDE = 32
NARROW = 4
DEVICES = WIDE * NARROW
SENT = 8
BACK = 5
KEPT_X = 176
KEPT_W = KEPT_X // ROWS_X
HEAVY = (0, 3)
LIGHT = (1, 2)
LIGHT_ROW = (0, 40)
SLOT = 24
TILES = 7

section_step = 0.25
viscous_rate = 0.05
vmem_bytes = 60 * 1024 * 1024


def halves(table):
    upper = table.astype(ml_dtypes.bfloat16)
    lower = (table - upper.astype(np.float64)).astype(ml_dtypes.bfloat16)
    return np.stack([upper, lower])


def turn(modes, places, length):
    angle = 2.0 * np.pi / length * (np.outer(modes, places) % length)
    return np.cos(angle), np.sin(angle)


def tables_synth_z():
    quarter = np.arange(128)
    parts = []
    for plane in range(2):
        cosine, sine = turn(2 * np.arange(128) + plane, quarter, NZ)
        upper, lower = halves(np.concatenate([cosine, sine], 0))
        parts.append(np.concatenate([upper, upper, lower], 1))
    return np.stack(parts)


def tables_synth_y():
    mode = np.arange(128)
    parts = []
    for parity in range(2):
        cosine, sine = turn(mode, 2 * np.arange(128) + parity, NY)
        real_rows = np.concatenate([cosine, sine], 1)
        imag_rows = np.concatenate([-sine, cosine], 1)
        stacked = np.stack([real_rows.reshape(2, 64, 256), imag_rows.reshape(2, 64, 256)], 1)
        parts.append(halves(stacked.reshape(256, 256)))
    return np.stack(parts)


def norm_scale():
    return 1.0 / math.sqrt(NX * NY * NZ)


def tables_synth_x():
    weight = np.where(np.arange(KX) == 0, 1.0, 2.0) * norm_scale()
    cosine, sine = turn(np.arange(256), np.arange(KX), NX)
    return np.stack([halves(cosine * weight), halves(-sine * weight)])


def tables_anal_x():
    cosine, sine = turn(np.arange(KEPT_X), np.arange(256), NX)
    return np.stack([halves(cosine * norm_scale()), halves(-sine * norm_scale())])


def tables_anal_y():
    parts = []
    mode = np.arange(128)
    for parity in range(2):
        cosine, sine = turn(2 * np.arange(128) + parity, mode, NY)
        cosine = cosine.reshape(128, 2, 1, 64)
        sine = sine.reshape(128, 2, 1, 64)
        real_rows = np.concatenate([cosine, -sine], 2).reshape(128, 256)
        imag_rows = np.concatenate([sine, cosine], 2).reshape(128, 256)
        parts.append(halves(np.concatenate([real_rows, imag_rows], 0)))
    return np.stack(parts)


def tables_anal_z():
    parts = []
    for plane in range(2):
        cosine, sine = turn(2 * np.arange(128) + plane, np.arange(128), NZ)
        upper, lower = halves(np.concatenate([cosine, sine], 1))
        parts.append(np.concatenate([upper, upper, lower], 0))
    return np.stack(parts)


def split(value):
    upper = value.astype(jnp.bfloat16)
    lower = (value - upper.astype(jnp.float32)).astype(jnp.bfloat16)
    return upper, lower


def dot(left, right, dims):
    return lax.dot_general(left, right, (dims, ((), ())), preferred_element_type=jnp.float32)


def dot3(left, right, dims=((1,), (0,))):
    return (
        dot(left[0], right[0], dims)
        + dot(left[0], right[1], dims)
        + dot(left[1], right[0], dims)
    )


def signed(number, length):
    return jnp.where(number < length // 2, number, number - length)


def wave_y(start, shape, axis):
    number = lax.broadcasted_iota(jnp.int32, shape, axis) + start
    return 2.0 * math.pi / NY * signed(number, NY).astype(jnp.float32)


def wave_z(shape, axis):
    number = lax.broadcasted_iota(jnp.int32, shape, axis)
    return 2.0 * math.pi / NZ * signed(number, NZ).astype(jnp.float32)


def synth_z_kernel(
    place_ref, adjoint_ref, velocity_ref, table_ref, out_ref, adj_ref, vel_ref, sent_ref, sems
):
    def load(k, which):
        source, target = ((adjoint_ref, adj_ref), (velocity_ref, vel_ref))[which]
        return pltpu.make_async_copy(source.at[:, :, k], target.at[:, :, k], sems.at[which, k])

    def store(k):
        rows = pl.ds(k * SENT, SENT)
        return pltpu.make_async_copy(
            sent_ref.at[:, :, rows], out_ref.at[:, :, rows], sems.at[2, k]
        )

    for k in range(ROWS_X):
        for which in range(2):
            load(k, which).start()
    ky = wave_y(place_ref[1] * ROWS_Y, (ROWS_Y, 1), 0)
    kz = wave_z((1, NZ), 1)
    half_sign = jnp.where(lax.broadcasted_iota(jnp.int32, (1, 128), 1) < 64, -1.0, 1.0)

    for k in range(ROWS_X):
        number_x = place_ref[0] * ROWS_X + k
        kx = 2.0 * math.pi / NX * number_x.astype(jnp.float32)
        for which in range(2):
            load(k, which).wait()
        vel = [[vel_ref[c, part, k] for part in range(2)] for c in range(3)]
        fields = [(adj_ref[c, 0, k], adj_ref[c, 1, k]) for c in range(3)]
        fields += [(vel[c][0], vel[c][1]) for c in range(3)]
        fields.append((kz * vel[1][1] - ky * vel[2][1], ky * vel[2][0] - kz * vel[1][0]))
        fields.append((kx * vel[2][1] - kz * vel[0][1], kz * vel[0][0] - kx * vel[2][0]))
        for pair in range(SENT // 2):
            rows = [part for field in fields[2 * pair : 2 * pair + 2] for part in field]
            value = jnp.concatenate(rows, 0)
            for plane in range(2):
                if plane == 0:
                    merged = value[:, :128] + value[:, 128:]
                else:
                    merged = value[:, :128] - value[:, 128:]
                upper, lower = split(merged)
                both = dot(
                    table_ref[plane],
                    jnp.concatenate([upper, lower, upper], 1),
                    ((1,), (1,)),
                )
                for f in range(2):
                    lanes = slice(128 * f, 128 * f + 128)
                    sent_ref[:, plane, k * SENT + 2 * pair + f, :] = both[
                        :128, lanes
                    ] + half_sign * pltpu.roll(both[128:, lanes], 64, 1)
        store(k).start()
    for k in range(ROWS_X):
        store(k).wait()


def synth_z(place, adjoint_hat, velocity_hat):
    table = tables_synth_z()
    shape = (DEVICES, 2, ROWS_X * SENT, 128)
    block = (3, 2, ROWS_X, ROWS_Y, NZ)
    return pl.pallas_call(
        synth_z_kernel,
        in_specs=[
            pl.BlockSpec(memory_space=pltpu.SMEM),
            pl.BlockSpec(memory_space=pl.ANY),
            pl.BlockSpec(memory_space=pl.ANY),
            pl.BlockSpec(memory_space=pltpu.VMEM),
        ],
        out_specs=pl.BlockSpec(memory_space=pl.ANY),
        out_shape=jax.ShapeDtypeStruct(shape, jnp.float32),
        scratch_shapes=[
            pltpu.VMEM(block, jnp.float32),
            pltpu.VMEM(block, jnp.float32),
            pltpu.VMEM(shape, jnp.float32),
            pltpu.SemaphoreType.DMA((3, ROWS_X)),
        ],
        compiler_params=pltpu.CompilerParams(vmem_limit_bytes=vmem_bytes),
        name="synth_z",
    )(place, adjoint_hat, velocity_hat, jnp.asarray(table))


def plane_kernel(got_ref, sy_ref, sx_ref, ax_ref, ay_ref, out_ref, spec_ref, cell_ref):
    plane = pl.program_id(0)
    half_sign = jnp.where(lax.broadcasted_iota(jnp.int32, (1, 128), 1) < 64, -1.0, 1.0)
    ky_lanes = []
    for n in range(NARROW):
        number = lax.broadcasted_iota(jnp.int32, (1, 128), 1) % 64 + n * ROWS_Y
        ky_lanes.append(2.0 * math.pi / NY * signed(number, NY).astype(jnp.float32))
    kx_rows = 2.0 * math.pi / NX * lax.broadcasted_iota(jnp.int32, (KX, 1), 0).astype(jnp.float32)
    alternate = jnp.where(lax.broadcasted_iota(jnp.int32, (KX, 1), 0) % 2 == 0, 1.0, -1.0)
    weight = (
        jnp.where(lax.broadcasted_iota(jnp.int32, (KX, 1), 0) == 0, 1.0, 2.0) * norm_scale()
    )
    first_row = lax.broadcasted_iota(jnp.int32, (256, 1), 0) == 0

    def rows_of(field, n):
        return jnp.concatenate(
            [
                got_ref[w * NARROW + n, 0, pl.ds(field, ROWS_X, stride=SENT), :]
                for w in range(WIDE)
            ],
            0,
        )

    def synth(parts, index):
        spans = []
        for parity in range(2):
            if parity == 0:
                merged = [parts[0] + parts[2], parts[1] + parts[3]]
            else:
                merged = [parts[0] - parts[2], parts[1] - parts[3]]
            spans.append(
                dot3(
                    split(jnp.concatenate(merged, 1)), (sy_ref[parity, 0], sy_ref[parity, 1])
                )
            )
        real = jnp.concatenate([spans[0][:, :128], spans[1][:, :128]], 1)
        imag = jnp.concatenate([spans[0][:, 128:], spans[1][:, 128:]], 1)
        cosine = dot3((sx_ref[0, 0], sx_ref[0, 1]), split(real))
        sine = dot3((sx_ref[1, 0], sx_ref[1, 1]), split(imag))
        middle = jnp.sum(real * (alternate * weight), 0, keepdims=True)
        cell_ref[index, 0] = cosine + sine
        cell_ref[index, 1] = jnp.where(first_row, middle, cosine - sine)

    def each_field(field, carry):
        synth([rows_of(field, n) for n in range(NARROW)], field)
        return carry

    lax.fori_loop(0, SENT, each_field, 0, unroll=True)
    swirl = []
    for n in range(NARROW):
        across = kx_rows * rows_of(4, n) - ky_lanes[n] * rows_of(3, n)
        swirl.append(pltpu.roll(across, 64, 1) * half_sign)
    synth(swirl, SENT)

    def product(kind, c, mirror):
        one, two = (c + 1) % 3, (c + 2) % 3
        if kind == 0:
            return (
                cell_ref[one, mirror] * cell_ref[6 + two, mirror]
                - cell_ref[two, mirror] * cell_ref[6 + one, mirror]
            )
        return (
            cell_ref[3 + one, mirror] * cell_ref[two, mirror]
            - cell_ref[3 + two, mirror] * cell_ref[one, mirror]
        )

    def analyse(index, kind, c):
        ahead = product(kind, c, 0)
        behind = product(kind, c, 1)
        middle = behind[0:1]
        both = ahead + jnp.where(first_row, 0.0, behind)
        apart = ahead - behind
        real = dot3((ax_ref[0, 0], ax_ref[0, 1]), split(both))
        real = real + alternate[:KEPT_X] * norm_scale() * middle
        imag = dot3((ax_ref[1, 0], ax_ref[1, 1]), split(apart))
        spans = []
        for parity in range(2):
            lanes = slice(128 * parity, 128 * parity + 128)
            spans.append(
                dot3(
                    split(jnp.concatenate([real[:, lanes], imag[:, lanes]], 1)),
                    (ay_ref[parity, 0], ay_ref[parity, 1]),
                )
            )
        spec_ref[index, 0] = spans[0] + spans[1]
        spec_ref[index, 1] = spans[0] - spans[1]

    for kind in range(2):
        for c in range(3):
            analyse(3 * kind + c, kind, c)

    kx_kept = kx_rows[:KEPT_X]

    def times_i(value):
        return pltpu.roll(value, 64, 1) * half_sign

    @pl.when(plane == 0)
    def _():
        out_ref[KEPT_W:] = jnp.zeros((WIDE - KEPT_W,) + out_ref.shape[1:], jnp.float32)

    def put(n, tile, value):
        rows = pl.ds(pl.multiple_of(tile * ROWS_X, ROWS_X), ROWS_X)
        out_ref[:KEPT_W, n, rows, :] = value.reshape(KEPT_W, ROWS_X, 128)

    def values_of(n):
        at = (n // 2, slice(None), slice(128 * (n % 2), 128 * (n % 2) + 128))
        item = [spec_ref[(index,) + at] for index in range(6)]
        ky = ky_lanes[n]
        return [
            item[0] + times_i(ky * item[5]),
            item[1] - times_i(kx_kept * item[5]),
            item[2] + times_i(kx_kept * item[4] - ky * item[3]),
            item[3],
            item[4],
        ]

    lane = lax.broadcasted_iota(jnp.int32, (1, 128), 1)
    for half in range(2):
        heavy, light = HEAVY[half], LIGHT[half]
        values = values_of(heavy)
        for f in range(3):
            put(heavy, 3 * plane + f, values[f])

        @pl.when(plane == 0)
        def _(heavy=heavy, value=values[3]):
            put(heavy, 6, value)

        @pl.when(plane == 1)
        def _(light=light, value=values[3]):
            put(light, 1, value)

        put(light, 2 * plane, values[4])
        values = values_of(light)
        packed = []
        for tile in range(2):
            value = jnp.zeros((KEPT_X, 128), jnp.float32)
            for slot in range(5):
                f, part = divmod(5 * tile + slot, 2)
                moved = pltpu.roll(
                    values[f], (SLOT * slot - 64 * part - LIGHT_ROW[half]) % 128, 1
                )
                value = jnp.where((lane >= SLOT * slot) & (lane < SLOT * slot + SLOT), moved, value)
            packed.append(value)
        for tile in range(2):
            put(light, 3 + 2 * plane + tile, packed[tile])


def run_planes(got):
    tables = [tables_synth_y(), tables_synth_x(), tables_anal_x(), tables_anal_y()]
    shape = (WIDE, NARROW, TILES * ROWS_X, 128)
    return pl.pallas_call(
        plane_kernel,
        grid=(2,),
        out_shape=jax.ShapeDtypeStruct(shape, jnp.float32),
        in_specs=[pl.BlockSpec((DEVICES, 1, ROWS_X * SENT, 128), lambda i: (0, i, 0, 0))]
        + [pl.BlockSpec(table.shape, lambda i: (0, 0, 0, 0)) for table in tables],
        out_specs=pl.BlockSpec(shape, lambda i: (0, 0, 0, 0)),
        scratch_shapes=[
            pltpu.VMEM((6, 2, KEPT_X, 256), jnp.float32),
            pltpu.VMEM((9, 2, 256, 256), jnp.float32),
        ],
        compiler_params=pltpu.CompilerParams(vmem_limit_bytes=vmem_bytes),
        name="plane",
    )(got, *[jnp.asarray(table) for table in tables])


def finish_kernel(
    place_ref,
    back_ref,
    more_ref,
    adjoint_ref,
    table_ref,
    out_ref,
    got_ref,
    fwd_ref,
    old_ref,
    new_ref,
    sems,
    whole_sems,
):
    narrow = place_ref[1]
    is_light = (narrow == LIGHT[0]) | (narrow == LIGHT[1])

    def load(k):
        return pltpu.make_async_copy(
            adjoint_ref.at[:, :, k], old_ref.at[:, :, k], sems.at[0, k]
        )

    def store(k):
        return pltpu.make_async_copy(new_ref.at[:, :, k], out_ref.at[:, :, k], sems.at[1, k])

    wholes = [
        pltpu.make_async_copy(back_ref, got_ref, whole_sems.at[0]),
        pltpu.make_async_copy(more_ref, fwd_ref, whole_sems.at[1]),
    ]
    for copy in wholes:
        copy.start()
    for k in range(ROWS_X):
        load(k).start()
    for copy in wholes:
        copy.wait()
    number_z = signed(lax.broadcasted_iota(jnp.int32, (1, NZ), 1), NZ)
    kz = 2.0 * math.pi / NZ * number_z.astype(jnp.float32)

    def span_of(k, first, second):
        spans = []
        for plane, (ref, tile) in enumerate((first, second)):
            rows = ref[:, tile * ROWS_X + k, :]
            upper, lower = split(rows.T)
            spans.append(dot(jnp.concatenate([upper, lower, upper], 1), table_ref[plane], ((1,), (0,))))
        return spans

    def unite(spans, real_rows, imag_rows):
        parts = []
        for span in spans:
            real, imag = span[real_rows], span[imag_rows]
            parts.append((real[:, :128] + imag[:, 128:], imag[:, :128] - real[:, 128:]))
        (real_0, imag_0), (real_1, imag_1) = parts
        return (
            jnp.concatenate([real_0 + real_1, real_0 - real_1], 1),
            jnp.concatenate([imag_0 + imag_1, imag_0 - imag_1], 1),
        )

    def emit(k, got, start, rows):
        number_x = place_ref[0] * ROWS_X + k
        kx = 2.0 * math.pi / NX * number_x.astype(jnp.float32)
        number_y = lax.broadcasted_iota(jnp.int32, (rows, 1), 0) + start + narrow * ROWS_Y
        number_y = signed(number_y, NY)
        ky = 2.0 * math.pi / NY * number_y.astype(jnp.float32)
        conv = [
            (got[0][0] + kz * got[4][1], got[0][1] - kz * got[4][0]),
            (got[1][0] - kz * got[3][1], got[1][1] + kz * got[3][0]),
            got[2],
        ]
        keep = (
            (3 * number_x < NX) & (3 * jnp.abs(number_y) < NY) & (3 * jnp.abs(number_z) < NZ)
        ).astype(jnp.float32)
        ksquare = kx * kx + ky * ky + kz * kz
        inverse = 1.0 / (ksquare + (ksquare == 0).astype(jnp.float32))
        decay = jnp.exp(-viscous_rate * ksquare)
        waves = (kx, ky, kz)
        for part in range(2):
            along = (kx * conv[0][part] + ky * conv[1][part] + kz * conv[2][part]) * inverse
            for c in range(3):
                projected = keep * (conv[c][part] - waves[c] * along)
                old = old_ref[c, part, k, pl.ds(start, rows), :]
                new_ref[c, part, k, pl.ds(start, rows), :] = decay * (
                    old + section_step * projected
                )

    @pl.when(jnp.logical_not(is_light))
    def _():
        for k in range(ROWS_X):
            got = []
            for f in range(BACK):
                first = (got_ref, (0, 1, 2, 6)[f]) if f < 4 else (fwd_ref, 0)
                second = (got_ref, 3 + f) if f < 3 else (fwd_ref, f - 2)
                spans = span_of(k, first, second)
                got.append(unite(spans, slice(0, 64), slice(64, 128)))
            load(k).wait()
            emit(k, got, 0, ROWS_Y)
            store(k).start()

    @pl.when(is_light)
    def _():
        for k in range(ROWS_X):
            tiles = [
                span_of(k, (got_ref, 3), (got_ref, 5)),
                span_of(k, (got_ref, 4), (got_ref, 6)),
            ]
            number_x = place_ref[0] * ROWS_X + k
            kx = 2.0 * math.pi / NX * number_x.astype(jnp.float32)
            number_y = lax.broadcasted_iota(jnp.int32, (ROWS_Y, 1), 0) + narrow * ROWS_Y
            ky = 2.0 * math.pi / NY * signed(number_y, NY).astype(jnp.float32)
            decay = jnp.exp(-viscous_rate * (kx * kx + ky * ky + kz * kz))
            load(k).wait()
            for c in range(3):
                for part in range(2):
                    new_ref[c, part, k] = decay * old_ref[c, part, k]
            got = []
            for f in range(BACK):
                (tile, slot), (tile_i, slot_i) = divmod(2 * f, 5), divmod(2 * f + 1, 5)
                real = [span[SLOT * slot : SLOT * slot + SLOT] for span in tiles[tile]]
                imag = [span[SLOT * slot_i : SLOT * slot_i + SLOT] for span in tiles[tile_i]]
                pairs = [jnp.concatenate([r, i], 0) for r, i in zip(real, imag)]
                got.append(unite(pairs, slice(0, SLOT), slice(SLOT, 2 * SLOT)))
            start = pl.multiple_of(jnp.where(narrow == LIGHT[0], 0, LIGHT_ROW[1]), 8)
            emit(k, got, start, SLOT)
            store(k).start()

    for k in range(ROWS_X):
        store(k).wait()


def finish(place, back, more, adjoint_hat):
    table = tables_anal_z()
    block = (3, 2, ROWS_X, ROWS_Y, NZ)
    return pl.pallas_call(
        finish_kernel,
        in_specs=[
            pl.BlockSpec(memory_space=pltpu.SMEM),
            pl.BlockSpec(memory_space=pl.ANY),
            pl.BlockSpec(memory_space=pl.ANY),
            pl.BlockSpec(memory_space=pl.ANY),
            pl.BlockSpec(memory_space=pltpu.VMEM),
        ],
        out_specs=pl.BlockSpec(memory_space=pl.ANY),
        out_shape=jax.ShapeDtypeStruct(block, jnp.float32),
        scratch_shapes=[
            pltpu.VMEM(back.shape, jnp.float32),
            pltpu.VMEM(more.shape, jnp.float32),
            pltpu.VMEM(block, jnp.float32),
            pltpu.VMEM(block, jnp.float32),
            pltpu.SemaphoreType.DMA((2, ROWS_X)),
            pltpu.SemaphoreType.DMA((2,)),
        ],
        compiler_params=pltpu.CompilerParams(vmem_limit_bytes=vmem_bytes),
        name="finish",
    )(place, back, more, adjoint_hat, jnp.asarray(table))


def swap(chunks):
    return lax.all_to_all(chunks, ("wide", "narrow"), 0, 0, tiled=True)


def forward(tiles):
    return lax.ppermute(tiles, "narrow", [(LIGHT[0], HEAVY[0]), (LIGHT[1], HEAVY[1])])


def local(adjoint_hat, velocity_hat):
    place = jnp.stack([lax.axis_index("wide"), lax.axis_index("narrow")]).astype(jnp.int32)
    got = swap(synth_z(place, adjoint_hat, velocity_hat))
    back = swap(run_planes(got).reshape(DEVICES, TILES * ROWS_X, 128))
    more = forward(back[:, : 3 * ROWS_X])
    return finish(place, back, more, adjoint_hat)


def solution(mesh):
    in_specs = (P(None, None, "wide", "narrow", None), P(None, None, "wide", "narrow", None))
    out_specs = P(None, None, "wide", "narrow", None)
    return jax.shard_map(local, mesh=mesh, in_specs=in_specs, out_specs=out_specs, check_vma=False)
```

time: 222 us -> 227 us (1.023)
  blocking collectives: 0 us -> 168 us
  waiting for transfers between devices: 119 us -> 4.14 us
  starting transfers between devices: 35 us -> 1.29 us
  Pallas kernels: 63.7 us -> 51.8 us
  local copies, waits for them, and re-layouts: 3.3 us -> 0.11 us
    all_to_all x0 -> x2, blocking collectives: none -> 168 us  [swap(): return lax.all_to_all(chunks, ('wide', 'narrow'), 0, 0, tiled=True)]
    all_to_all x4 -> x0, waiting for transfers between devices: 116 us -> none  [swap(): return lax.all_to_all(chunks, ('wide', 'narrow'), 0, 0, tiled=True)]
    all_to_all x4 -> x0, starting transfers between devices: 32.5 us -> none  [swap(): return lax.all_to_all(chunks, ('wide', 'narrow'), 0, 0, tiled=True)]
    pallas_call x5 -> x3, Pallas kernels: 63.7 us -> 51.8 us  [the longest x1 23.3 us: run_planes(): pl.pallas_call(plane_kernel, grid=(2,), out_shape=jax.ShapeDtypeStruct(sh...]
  transfers between devices with their start and end apart: 6 -> 1, of which waited for: 5 -> 1; matrix products, arithmetic and copies ran while one was open for 1% -> 0% of each run, Pallas kernels for 18% -> 0%
where the time goes in v3:
time: 227 us; the launch traced here: 226 us
  blocking collectives  168 us (74%)
  Pallas kernels  51.8 us (23%)
  waiting for transfers between devices  4.14 us (2%)
    all_to_all x2, blocking collectives, swap(): return lax.all_to_all(chunks, ('wide', 'narrow'), 0, 0, tiled=True)  168 us
    pallas_call x1, Pallas kernels, run_planes(): pl.pallas_call(plane_kernel, grid=(2,), out_shape=jax.ShapeDtypeStruct(sh...  23.3 us
    pallas_call x1, Pallas kernels, synth_z(): pl.pallas_call(synth_z_kernel, in_specs=[pl.BlockSpec(memory_space=pltpu....  15.6 us
    pallas_call x1, Pallas kernels, finish(): pl.pallas_call(finish_kernel, in_specs=[pl.BlockSpec(memory_space=pltpu.S...  12.9 us
  transfers between devices with their start and end apart: 1, of which 1 were waited for; matrix products, arithmetic and copies ran while one was open for 0% of the time, Pallas kernels for 0%

profile of v3, /device:TPU:0, one launch (start us, length us, event | category | flops | bytes accessed | tf_op | source)
XLA Modules:
  0.0 226.4 jit_solution(5517550979672562363)
XLA Ops:
  0.0 0.6 pad_add_fusion.place_ref
  0.6 15.6 %synth_z.1 = f32[128,2,64,128]{3,2,1,0:T(8,128)} custom-call(s32[2]{0:T(128)} %pad_add_fusion.place_ref, f32[3,2,8,64,256]{4,3,2,1,0:T(8,128)} %adjoint_ref.3, f32[3,2,8,64,256]{4,3,2,1,0:T(8,128)} %velocity_ref.1, bf16[2,256,384]{2,1,0:T(8,128)(2,1)} %constant.21.clone.table_ref), custom_call_target="tpu_custom_call" | custom-call | tf_op jit(solution)/shard_map/synth_z/pallas_call | solution.py:197
  16.2 108.8 %all_to_all.10.got_ref = f32[128,2,64,128]{3,2,1,0:T(8,128)} all-to-all(f32[128,2,64,128]{3,2,1,0:T(8,128)} %synth_z.1), channel_id=1, replica_groups=mesh['narrow'=4,'wide'=32] {'wide','narrow'}, dimensions={0} | all-to-all | bytes 16777216 | tf_op jit(solution)/shard_map/all_to_all | solution.py:540
  125.0 23.3 %plane.1 = f32[32,4,56,128]{3,2,1,0:T(8,128)} custom-call(f32[128,2,64,128]{3,2,1,0:T(8,128)} %all_to_all.10.got_ref, bf16[2,2,256,256]{3,2,1,0:T(8,128)(2,1)} %constant.22.clone.sy_ref, bf16[2,2,256,256]{3,2,1,0:T(8,128)(2,1)} %constant.23.clone.sx_ref, bf16[2,2,176,256]{3,2,1,0:T(8,128)(2,1)} %constant.24.clone.ax_ref, ...), custom_call_target="tpu_custom_call" | custom-call | tf_op jit(solution)/shard_map/plane/pallas_call | solution.py:368
  148.3 59.5 %all_to_all.11.back_ref = f32[128,56,128]{2,1,0:T(8,128)S(1)} all-to-all(f32[128,56,128]{2,1,0:T(8,128)} %bitcast.3), channel_id=1, replica_groups=mesh['narrow'=4,'wide'=32] {'wide','narrow'}, dimensions={0} | all-to-all | bytes 7340032 | tf_op jit(solution)/shard_map/all_to_all | solution.py:540
  207.8 0.0 copy-start
  207.8 0.1 slice.4
  207.9 1.3 collective-permute-start
  209.2 4.1 %collective-permute-done.more_ref = f32[128,24,128]{2,1,0:T(8,128)} collective-permute-done((f32[128,24,128]{2,1,0:T(8,128)S(1)}, f32[128,24,128]{2,1,0:T(8,128)}, u32[]{:S(2)}, u32[]{:S(2)}) %collective-permute-start) | collective-permute-done | bytes 1572896 | tf_op jit(solution)/shard_map/ppermute | solution.py:544
  213.4 0.0 copy-done
  213.4 12.9 %finish.1 = f32[3,2,8,64,256]{4,3,2,1,0:T(8,128)} custom-call(s32[2]{0:T(128)} %pad_add_fusion.place_ref, f32[128,56,128]{2,1,0:T(8,128)} %copy-done, f32[128,24,128]{2,1,0:T(8,128)} %collective-permute-done.more_ref, f32[3,2,8,64,256]{4,3,2,1,0:T(8,128)} %adjoint_ref.3, bf16[2,384,256]{2,1,0:T(8,128)(2,1)} %constant.26.clone.table_ref), custom_call_target="tpu_custom_call" | custom-call | tf_op jit(solution)/shard_map/finish/pallas_call | solution.py:515
Async XLA Ops:
  207.8 5.5 %copy-start = (f32[128,56,128]{2,1,0:T(8,128)}, f32[128,56,128]{2,1,0:T(8,128)S(1)}, u32[]{:S(2)}) copy-start(f32[128,56,128]{2,1,0:T(8,128)S(1)} %all_to_all.11.back_ref) | copy-start | bytes 11010052
  207.9 5.4 %collective-permute-start = (f32[128,24,128]{2,1,0:T(8,128)S(1)}, f32[128,24,128]{2,1,0:T(8,128)}, u32[]{:S(2)}, u32[]{:S(2)}) collective-permute-start(f32[128,24,128]{2,1,0:T(8,128)S(1)} %slice.4), channel_id=1, source_target_pairs={{32,0},{64,96},{33,1},{65,97},{34,2},{66,98},{35,3},{67,99},{36,4}... | collective-permute-start | bytes 4718600 | tf_op jit(solution)/shard_map/ppermute | solution.py:544

commit v4 on v3

--- a/solution.py
+++ b/solution.py
@@ -143,10 +143,11 @@
         source, target = ((adjoint_ref, adj_ref), (velocity_ref, vel_ref))[which]
         return pltpu.make_async_copy(source.at[:, :, k], target.at[:, :, k], sems.at[which, k])
 
-    def store(k):
-        rows = pl.ds(k * SENT, SENT)
+    def store(k, plane):
         return pltpu.make_async_copy(
-            sent_ref.at[:, :, rows], out_ref.at[:, :, rows], sems.at[2, k]
+            sent_ref.at[k, plane],
+            out_ref.at[:, plane, pl.ds(k * SENT, SENT)],
+            sems.at[2 + plane, k],
         )
 
     for k in range(ROWS_X):
@@ -182,12 +183,14 @@
                 )
                 for f in range(2):
                     lanes = slice(128 * f, 128 * f + 128)
-                    sent_ref[:, plane, k * SENT + 2 * pair + f, :] = both[
+                    sent_ref[k, plane, :, 2 * pair + f, :] = both[
                         :128, lanes
                     ] + half_sign * pltpu.roll(both[128:, lanes], 64, 1)
-        store(k).start()
+        for plane in range(2):
+            store(k, plane).start()
     for k in range(ROWS_X):
-        store(k).wait()
+        for plane in range(2):
+            store(k, plane).wait()
 
 
 def synth_z(place, adjoint_hat, velocity_hat):
@@ -207,8 +210,8 @@
         scratch_shapes=[
             pltpu.VMEM(block, jnp.float32),
             pltpu.VMEM(block, jnp.float32),
-            pltpu.VMEM(shape, jnp.float32),
-            pltpu.SemaphoreType.DMA((3, ROWS_X)),
+            pltpu.VMEM((ROWS_X, 2, DEVICES, SENT, 128), jnp.float32),
+            pltpu.SemaphoreType.DMA((4, ROWS_X)),
         ],
         compiler_params=pltpu.CompilerParams(vmem_limit_bytes=vmem_bytes),
         name="synth_z",
@@ -381,62 +384,165 @@
     )(got, *[jnp.asarray(table) for table in tables])
 
 
+def take_kernel(back_ref, out_ref, sem):
+    copy = pltpu.make_async_copy(back_ref.at[:, pl.ds(0, 3 * ROWS_X)], out_ref, sem)
+    copy.start()
+    copy.wait()
+
+
+def take(back):
+    return pl.pallas_call(
+        take_kernel,
+        in_specs=[pl.BlockSpec(memory_space=pltpu.HBM)],
+        out_specs=pl.BlockSpec(memory_space=pltpu.HBM),
+        out_shape=jax.ShapeDtypeStruct((DEVICES, 3 * ROWS_X, 128), jnp.float32),
+        scratch_shapes=[pltpu.SemaphoreType.DMA],
+        name="take",
+    )(back)
+
+
+def span_of(got_ref, table_ref, k, *tiles):
+    spans = []
+    for plane, tile in enumerate(tiles):
+        upper, lower = split(got_ref[tile, :, k, :].T)
+        stacked = jnp.concatenate([upper, lower, upper], 1)
+        spans.append(dot(stacked, table_ref[plane], ((1,), (0,))))
+    return spans
+
+
+def unite(spans, real_rows, imag_rows):
+    parts = []
+    for span in spans:
+        real, imag = span[real_rows], span[imag_rows]
+        parts.append((real[:, :128] + imag[:, 128:], imag[:, :128] - real[:, 128:]))
+    (real_0, imag_0), (real_1, imag_1) = parts
+    return (
+        jnp.concatenate([real_0 + real_1, real_0 - real_1], 1),
+        jnp.concatenate([imag_0 + imag_1, imag_0 - imag_1], 1),
+    )
+
+
+def light_narrow(narrow):
+    return (narrow == LIGHT[0]) | (narrow == LIGHT[1])
+
+
+def begin_kernel(place_ref, back_ref, table_ref, part_ref, got_ref, new_ref, sems, whole_sems):
+    is_light = light_narrow(place_ref[1])
+
+    def store(k):
+        return pltpu.make_async_copy(new_ref.at[:, :, k], part_ref.at[:, :, k], sems.at[k])
+
+    pieces = [
+        pltpu.make_async_copy(
+            back_ref.at[:, pl.ds(tile * ROWS_X, ROWS_X)], got_ref.at[tile], whole_sems.at[tile]
+        )
+        for tile in range(TILES)
+    ]
+    for copy in pieces:
+        copy.start()
+    for copy in pieces:
+        copy.wait()
+
+    @pl.when(jnp.logical_not(is_light))
+    def _():
+        for k in range(ROWS_X):
+            for f in range(3):
+                spans = span_of(got_ref, table_ref, k, f, 3 + f)
+                real, imag = unite(spans, slice(0, 64), slice(64, 128))
+                new_ref[f, 0, k] = real
+                new_ref[f, 1, k] = imag
+            store(k).start()
+
+    @pl.when(is_light)
+    def _():
+        for k in range(ROWS_X):
+            tiles = [
+                span_of(got_ref, table_ref, k, 3, 5),
+                span_of(got_ref, table_ref, k, 4, 6),
+            ]
+            for f in range(BACK):
+                (tile, slot), (tile_i, slot_i) = divmod(2 * f, 5), divmod(2 * f + 1, 5)
+                real = [span[SLOT * slot : SLOT * slot + SLOT] for span in tiles[tile]]
+                imag = [span[SLOT * slot_i : SLOT * slot_i + SLOT] for span in tiles[tile_i]]
+                pairs = [jnp.concatenate([r, i], 0) for r, i in zip(real, imag)]
+                real, imag = unite(pairs, slice(0, SLOT), slice(SLOT, 2 * SLOT))
+                at = slice(SLOT * (f // 3), SLOT * (f // 3) + SLOT)
+                new_ref[f % 3, 0, k, at] = real
+                new_ref[f % 3, 1, k, at] = imag
+            store(k).start()
+
+    for k in range(ROWS_X):
+        store(k).wait()
+
+
+def begin(place, back):
+    table = tables_anal_z()
+    block = (3, 2, ROWS_X, ROWS_Y, NZ)
+    return pl.pallas_call(
+        begin_kernel,
+        in_specs=[
+            pl.BlockSpec(memory_space=pltpu.SMEM),
+            pl.BlockSpec(memory_space=pltpu.HBM),
+            pl.BlockSpec(memory_space=pltpu.VMEM),
+        ],
+        out_specs=pl.BlockSpec(memory_space=pltpu.HBM),
+        out_shape=jax.ShapeDtypeStruct(block, jnp.float32),
+        scratch_shapes=[
+            pltpu.VMEM((TILES, DEVICES, ROWS_X, 128), jnp.float32),
+            pltpu.VMEM(block, jnp.float32),
+            pltpu.SemaphoreType.DMA((ROWS_X,)),
+            pltpu.SemaphoreType.DMA((TILES,)),
+        ],
+        compiler_params=pltpu.CompilerParams(vmem_limit_bytes=vmem_bytes),
+        name="begin",
+    )(place, back, jnp.asarray(table))
+
+
 def finish_kernel(
     place_ref,
     back_ref,
     more_ref,
+    part_ref,
     adjoint_ref,
     table_ref,
     out_ref,
     got_ref,
-    fwd_ref,
+    mid_ref,
     old_ref,
     new_ref,
     sems,
     whole_sems,
 ):
     narrow = place_ref[1]
-    is_light = (narrow == LIGHT[0]) | (narrow == LIGHT[1])
-
-    def load(k):
-        return pltpu.make_async_copy(
-            adjoint_ref.at[:, :, k], old_ref.at[:, :, k], sems.at[0, k]
+    is_light = light_narrow(narrow)
+
+    def load(k, which):
+        source, target = ((adjoint_ref, old_ref), (part_ref, mid_ref))[which]
+        return pltpu.make_async_copy(source.at[:, :, k], target.at[:, :, k], sems.at[which, k])
+
+    def store(k):
+        return pltpu.make_async_copy(new_ref.at[:, :, k], out_ref.at[:, :, k], sems.at[2, k])
+
+    pieces = [
+        pltpu.make_async_copy(
+            more_ref.at[:, pl.ds(tile * ROWS_X, ROWS_X)], got_ref.at[tile], whole_sems.at[tile]
         )
-
-    def store(k):
-        return pltpu.make_async_copy(new_ref.at[:, :, k], out_ref.at[:, :, k], sems.at[1, k])
-
-    wholes = [
-        pltpu.make_async_copy(back_ref, got_ref, whole_sems.at[0]),
-        pltpu.make_async_copy(more_ref, fwd_ref, whole_sems.at[1]),
+        for tile in range(3)
     ]
-    for copy in wholes:
+    pieces.append(
+        pltpu.make_async_copy(
+            back_ref.at[:, pl.ds(6 * ROWS_X, ROWS_X)], got_ref.at[3], whole_sems.at[3]
+        )
+    )
+    for copy in pieces:
         copy.start()
     for k in range(ROWS_X):
-        load(k).start()
-    for copy in wholes:
+        load(k, 0).start()
+        load(k, 1).start()
+    for copy in pieces:
         copy.wait()
     number_z = signed(lax.broadcasted_iota(jnp.int32, (1, NZ), 1), NZ)
     kz = 2.0 * math.pi / NZ * number_z.astype(jnp.float32)
-
-    def span_of(k, first, second):
-        spans = []
-        for plane, (ref, tile) in enumerate((first, second)):
-            rows = ref[:, tile * ROWS_X + k, :]
-            upper, lower = split(rows.T)
-            spans.append(dot(jnp.concatenate([upper, lower, upper], 1), table_ref[plane], ((1,), (0,))))
-        return spans
-
-    def unite(spans, real_rows, imag_rows):
-        parts = []
-        for span in spans:
-            real, imag = span[real_rows], span[imag_rows]
-            parts.append((real[:, :128] + imag[:, 128:], imag[:, :128] - real[:, 128:]))
-        (real_0, imag_0), (real_1, imag_1) = parts
-        return (
-            jnp.concatenate([real_0 + real_1, real_0 - real_1], 1),
-            jnp.concatenate([imag_0 + imag_1, imag_0 - imag_1], 1),
-        )
 
     def emit(k, got, start, rows):
         number_x = place_ref[0] * ROWS_X + k
@@ -468,39 +574,33 @@
     @pl.when(jnp.logical_not(is_light))
     def _():
         for k in range(ROWS_X):
-            got = []
-            for f in range(BACK):
-                first = (got_ref, (0, 1, 2, 6)[f]) if f < 4 else (fwd_ref, 0)
-                second = (got_ref, 3 + f) if f < 3 else (fwd_ref, f - 2)
-                spans = span_of(k, first, second)
-                got.append(unite(spans, slice(0, 64), slice(64, 128)))
-            load(k).wait()
+            across = [
+                unite(span_of(got_ref, table_ref, k, first, second), slice(0, 64), slice(64, 128))
+                for first, second in ((3, 1), (0, 2))
+            ]
+            load(k, 0).wait()
+            load(k, 1).wait()
+            got = [(mid_ref[f, 0, k], mid_ref[f, 1, k]) for f in range(3)] + across
             emit(k, got, 0, ROWS_Y)
             store(k).start()
 
     @pl.when(is_light)
     def _():
+        number_y = lax.broadcasted_iota(jnp.int32, (ROWS_Y, 1), 0) + narrow * ROWS_Y
+        ky = 2.0 * math.pi / NY * signed(number_y, NY).astype(jnp.float32)
         for k in range(ROWS_X):
-            tiles = [
-                span_of(k, (got_ref, 3), (got_ref, 5)),
-                span_of(k, (got_ref, 4), (got_ref, 6)),
-            ]
             number_x = place_ref[0] * ROWS_X + k
             kx = 2.0 * math.pi / NX * number_x.astype(jnp.float32)
-            number_y = lax.broadcasted_iota(jnp.int32, (ROWS_Y, 1), 0) + narrow * ROWS_Y
-            ky = 2.0 * math.pi / NY * signed(number_y, NY).astype(jnp.float32)
             decay = jnp.exp(-viscous_rate * (kx * kx + ky * ky + kz * kz))
-            load(k).wait()
+            load(k, 0).wait()
+            load(k, 1).wait()
             for c in range(3):
                 for part in range(2):
                     new_ref[c, part, k] = decay * old_ref[c, part, k]
             got = []
             for f in range(BACK):
-                (tile, slot), (tile_i, slot_i) = divmod(2 * f, 5), divmod(2 * f + 1, 5)
-                real = [span[SLOT * slot : SLOT * slot + SLOT] for span in tiles[tile]]
-                imag = [span[SLOT * slot_i : SLOT * slot_i + SLOT] for span in tiles[tile_i]]
-                pairs = [jnp.concatenate([r, i], 0) for r, i in zip(real, imag)]
-                got.append(unite(pairs, slice(0, SLOT), slice(SLOT, 2 * SLOT)))
+                at = slice(SLOT * (f // 3), SLOT * (f // 3) + SLOT)
+                got.append((mid_ref[f % 3, 0, k, at], mid_ref[f % 3, 1, k, at]))
             start = pl.multiple_of(jnp.where(narrow == LIGHT[0], 0, LIGHT_ROW[1]), 8)
             emit(k, got, start, SLOT)
             store(k).start()
@@ -509,31 +609,32 @@
         store(k).wait()
 
 
-def finish(place, back, more, adjoint_hat):
+def finish(place, back, more, part, adjoint_hat):
     table = tables_anal_z()
     block = (3, 2, ROWS_X, ROWS_Y, NZ)
     return pl.pallas_call(
         finish_kernel,
         in_specs=[
             pl.BlockSpec(memory_space=pltpu.SMEM),
-            pl.BlockSpec(memory_space=pl.ANY),
-            pl.BlockSpec(memory_space=pl.ANY),
-            pl.BlockSpec(memory_space=pl.ANY),
+            pl.BlockSpec(memory_space=pltpu.HBM),
+            pl.BlockSpec(memory_space=pltpu.HBM),
+            pl.BlockSpec(memory_space=pltpu.HBM),
+            pl.BlockSpec(memory_space=pltpu.HBM),
             pl.BlockSpec(memory_space=pltpu.VMEM),
         ],
-        out_specs=pl.BlockSpec(memory_space=pl.ANY),
+        out_specs=pl.BlockSpec(memory_space=pltpu.HBM),
         out_shape=jax.ShapeDtypeStruct(block, jnp.float32),
         scratch_shapes=[
-            pltpu.VMEM(back.shape, jnp.float32),
-            pltpu.VMEM(more.shape, jnp.float32),
+            pltpu.VMEM((4, DEVICES, ROWS_X, 128), jnp.float32),
             pltpu.VMEM(block, jnp.float32),
             pltpu.VMEM(block, jnp.float32),
-            pltpu.SemaphoreType.DMA((2, ROWS_X)),
-            pltpu.SemaphoreType.DMA((2,)),
+            pltpu.VMEM(block, jnp.float32),
+            pltpu.SemaphoreType.DMA((3, ROWS_X)),
+            pltpu.SemaphoreType.DMA((4,)),
         ],
         compiler_params=pltpu.CompilerParams(vmem_limit_bytes=vmem_bytes),
         name="finish",
-    )(place, back, more, adjoint_hat, jnp.asarray(table))
+    )(place, back, more, part, adjoint_hat, jnp.asarray(table))
 
 
 def swap(chunks):
@@ -548,8 +649,9 @@
     place = jnp.stack([lax.axis_index("wide"), lax.axis_index("narrow")]).astype(jnp.int32)
     got = swap(synth_z(place, adjoint_hat, velocity_hat))
     back = swap(run_planes(got).reshape(DEVICES, TILES * ROWS_X, 128))
-    more = forward(back[:, : 3 * ROWS_X])
-    return finish(place, back, more, adjoint_hat)
+    more = pltpu.with_memory_space_constraint(forward(take(back)), pltpu.HBM)
+    part = begin(place, back)
+    return finish(place, back, more, part, adjoint_hat)
 
 
 def solution(mesh):

time: 227 us -> 273 us (1.20)
  Pallas kernels: 51.8 us -> 101 us
  waiting for transfers between devices: 4.14 us -> 0.01 us
    pallas_call x0 -> x2, Pallas kernels: none -> 55.2 us  [the longest x1 48.8 us: take(): pl.pallas_call(take_kernel, in_specs=[pl.BlockSpec(memory_space=pltpu.HBM...]
    ppermute x1, waiting for transfers between devices: 4.14 us -> 0.01 us  [forward(): lax.ppermute(tiles, 'narrow', [(LIGHT[0], HEAVY[0]), (LIGHT[1], HEAVY[1])])]
    pallas_call x1, Pallas kernels: 12.9 us -> 9.85 us  [finish(): pl.pallas_call(finish_kernel, in_specs=[pl.BlockSpec(memory_space=pltpu.S...]
    pallas_call x1, Pallas kernels: 15.6 us -> 12.7 us  [synth_z(): pl.pallas_call(synth_z_kernel, in_specs=[pl.BlockSpec(memory_space=pltpu....]
  transfers between devices with their start and end apart: 1 -> 1, of which waited for: 1 -> 0; matrix products, arithmetic and copies ran while one was open for 0% -> 0% of each run, Pallas kernels for 0% -> 2%
where the time goes in v4:
time: 273 us
  blocking collectives  168 us (62%)
  Pallas kernels  101 us (37%)
    all_to_all x2, blocking collectives, swap(): return lax.all_to_all(chunks, ('wide', 'narrow'), 0, 0, tiled=True)  168 us
    pallas_call x1, Pallas kernels, take(): pl.pallas_call(take_kernel, in_specs=[pl.BlockSpec(memory_space=pltpu.HBM...  48.8 us
    pallas_call x1, Pallas kernels, run_planes(): pl.pallas_call(plane_kernel, grid=(2,), out_shape=jax.ShapeDtypeStruct(sh...  23.4 us
    pallas_call x1, Pallas kernels, synth_z(): pl.pallas_call(synth_z_kernel, in_specs=[pl.BlockSpec(memory_space=pltpu....  12.7 us
    pallas_call x1, Pallas kernels, finish(): pl.pallas_call(finish_kernel, in_specs=[pl.BlockSpec(memory_space=pltpu.S...  9.85 us
    pallas_call x1, Pallas kernels, begin(): pl.pallas_call(begin_kernel, in_specs=[pl.BlockSpec(memory_space=pltpu.SM...  6.49 us
  transfers between devices with their start and end apart: 1, of which 0 were waited for; matrix products, arithmetic and copies ran while one was open for 0% of the time, Pallas kernels for 2%

profile of v4, /device:TPU:0, one launch (start us, length us, event | category | flops | bytes accessed | tf_op | source)
XLA Modules:
  0.0 272.9 jit_solution(696641997799939734)
XLA Ops:
  0.0 0.6 pad_add_fusion.place_ref
  0.6 12.7 %synth_z.1 = f32[128,2,64,128]{3,2,1,0:T(8,128)} custom-call(s32[2]{0:T(128)} %pad_add_fusion.place_ref, f32[3,2,8,64,256]{4,3,2,1,0:T(8,128)} %adjoint_ref.3, f32[3,2,8,64,256]{4,3,2,1,0:T(8,128)} %velocity_ref.1, bf16[2,256,384]{2,1,0:T(8,128)(2,1)} %constant.21.clone.table_ref), custom_call_target="tpu_custom_call" | custom-call | tf_op jit(solution)/shard_map/synth_z/pallas_call | solution.py:200
  13.4 108.8 %all_to_all.10.got_ref = f32[128,2,64,128]{3,2,1,0:T(8,128)} all-to-all(f32[128,2,64,128]{3,2,1,0:T(8,128)} %synth_z.1), channel_id=1, replica_groups=mesh['narrow'=4,'wide'=32] {'wide','narrow'}, dimensions={0} | all-to-all | bytes 16777216 | tf_op jit(solution)/shard_map/all_to_all | solution.py:641
  122.2 23.4 %plane.1 = f32[32,4,56,128]{3,2,1,0:T(8,128)} custom-call(f32[128,2,64,128]{3,2,1,0:T(8,128)} %all_to_all.10.got_ref, bf16[2,2,256,256]{3,2,1,0:T(8,128)(2,1)} %constant.22.clone.sy_ref, bf16[2,2,256,256]{3,2,1,0:T(8,128)(2,1)} %constant.23.clone.sx_ref, bf16[2,2,176,256]{3,2,1,0:T(8,128)(2,1)} %constant.24.clone.ax_ref, ...), custom_call_target="tpu_custom_call" | custom-call | tf_op jit(solution)/shard_map/plane/pallas_call | solution.py:371
  145.6 59.6 %all_to_all.11.back_ref = f32[128,56,128]{2,1,0:T(8,128)} all-to-all(f32[128,56,128]{2,1,0:T(8,128)} %bitcast.3), channel_id=1, replica_groups=mesh['narrow'=4,'wide'=32] {'wide','narrow'}, dimensions={0} | all-to-all | bytes 7340032 | tf_op jit(solution)/shard_map/all_to_all | solution.py:641
  205.1 48.8 %take.1 = f32[128,24,128]{2,1,0:T(8,128)} custom-call(f32[128,56,128]{2,1,0:T(8,128)} %all_to_all.11.back_ref), custom_call_target="tpu_custom_call" | custom-call | tf_op jit(solution)/shard_map/take/pallas_call | solution.py:394
  253.9 1.3 collective-permute-start
  255.2 6.5 %begin.1.part_ref = f32[3,2,8,64,256]{4,3,2,1,0:T(8,128)} custom-call(s32[2]{0:T(128)} %pad_add_fusion.place_ref, f32[128,56,128]{2,1,0:T(8,128)} %all_to_all.11.back_ref, bf16[2,384,256]{2,1,0:T(8,128)(2,1)} %constant.26.clone.table_ref), custom_call_target="tpu_custom_call" | custom-call | tf_op jit(solution)/shard_map/begin/pallas_call | solution.py:481
  261.7 0.0 collective-permute-done.more_ref
  261.7 0.0 copy-start
  261.7 1.1 copy-done
  262.8 9.9 %finish.1 = f32[3,2,8,64,256]{4,3,2,1,0:T(8,128)} custom-call(s32[2]{0:T(128)} %pad_add_fusion.place_ref, f32[128,56,128]{2,1,0:T(8,128)} %all_to_all.11.back_ref, f32[128,24,128]{2,1,0:T(8,128)} %copy-done, f32[3,2,8,64,256]{4,3,2,1,0:T(8,128)} %begin.1.part_ref, f32[3,2,8,64,256]{4,3,2,1,0:T(8,128)} %adjoint_ref.3, ...), custom_call_target="tpu_custom_call" | custom-call | tf_op jit(solution)/shard_map/finish/pallas_call | solution.py:615
Async XLA Ops:
  253.9 7.8 %collective-permute-start = (f32[128,24,128]{2,1,0:T(8,128)}, f32[128,24,128]{2,1,0:T(8,128)S(1)}, u32[]{:S(2)}, u32[]{:S(2)}) collective-permute-start(f32[128,24,128]{2,1,0:T(8,128)} %take.1), channel_id=1, source_target_pairs={{32,0},{64,96},{33,1},{65,97},{34,2},{66,98},{35,3},{67,99},{36,4}... | collective-permute-start | bytes 4718600 | tf_op jit(solution)/shard_map/ppermute | solution.py:645
  261.7 1.1 copy-start

commit v5 on v3

--- a/solution.py
+++ b/solution.py
@@ -27,7 +27,6 @@
 LIGHT = (1, 2)
 LIGHT_ROW = (0, 40)
 SLOT = 24
-TILES = 7
 
 section_step = 0.25
 viscous_rate = 0.05
@@ -137,16 +136,15 @@
 
 
 def synth_z_kernel(
-    place_ref, adjoint_ref, velocity_ref, table_ref, out_ref, adj_ref, vel_ref, sent_ref, sems
+    plane, place_ref, adjoint_ref, velocity_ref, table_ref, out_ref, adj_ref, vel_ref, sent_ref, sems
 ):
     def load(k, which):
         source, target = ((adjoint_ref, adj_ref), (velocity_ref, vel_ref))[which]
         return pltpu.make_async_copy(source.at[:, :, k], target.at[:, :, k], sems.at[which, k])
 
     def store(k):
-        rows = pl.ds(k * SENT, SENT)
         return pltpu.make_async_copy(
-            sent_ref.at[:, :, rows], out_ref.at[:, :, rows], sems.at[2, k]
+            sent_ref.at[k], out_ref.at[:, pl.ds(k * SENT, SENT)], sems.at[2, k]
         )
 
     for k in range(ROWS_X):
@@ -169,33 +167,28 @@
         for pair in range(SENT // 2):
             rows = [part for field in fields[2 * pair : 2 * pair + 2] for part in field]
             value = jnp.concatenate(rows, 0)
-            for plane in range(2):
-                if plane == 0:
-                    merged = value[:, :128] + value[:, 128:]
-                else:
-                    merged = value[:, :128] - value[:, 128:]
-                upper, lower = split(merged)
-                both = dot(
-                    table_ref[plane],
-                    jnp.concatenate([upper, lower, upper], 1),
-                    ((1,), (1,)),
-                )
-                for f in range(2):
-                    lanes = slice(128 * f, 128 * f + 128)
-                    sent_ref[:, plane, k * SENT + 2 * pair + f, :] = both[
-                        :128, lanes
-                    ] + half_sign * pltpu.roll(both[128:, lanes], 64, 1)
+            if plane == 0:
+                merged = value[:, :128] + value[:, 128:]
+            else:
+                merged = value[:, :128] - value[:, 128:]
+            upper, lower = split(merged)
+            stacked = jnp.concatenate([upper, lower, upper], 1)
+            both = dot(table_ref[...], stacked, ((1,), (1,)))
+            for f in range(2):
+                lanes = slice(128 * f, 128 * f + 128)
+                turned = pltpu.roll(both[128:, lanes], 64, 1)
+                sent_ref[k, :, 2 * pair + f, :] = both[:128, lanes] + half_sign * turned
         store(k).start()
     for k in range(ROWS_X):
         store(k).wait()
 
 
-def synth_z(place, adjoint_hat, velocity_hat):
-    table = tables_synth_z()
-    shape = (DEVICES, 2, ROWS_X * SENT, 128)
+def synth_z(place, adjoint_hat, velocity_hat, plane):
+    table = tables_synth_z()[plane]
+    shape = (DEVICES, ROWS_X * SENT, 128)
     block = (3, 2, ROWS_X, ROWS_Y, NZ)
     return pl.pallas_call(
-        synth_z_kernel,
+        functools.partial(synth_z_kernel, plane),
         in_specs=[
             pl.BlockSpec(memory_space=pltpu.SMEM),
             pl.BlockSpec(memory_space=pl.ANY),
@@ -207,7 +200,7 @@
         scratch_shapes=[
             pltpu.VMEM(block, jnp.float32),
             pltpu.VMEM(block, jnp.float32),
-            pltpu.VMEM(shape, jnp.float32),
+            pltpu.VMEM((ROWS_X, DEVICES, SENT, 128), jnp.float32),
             pltpu.SemaphoreType.DMA((3, ROWS_X)),
         ],
         compiler_params=pltpu.CompilerParams(vmem_limit_bytes=vmem_bytes),
@@ -215,8 +208,12 @@
     )(place, adjoint_hat, velocity_hat, jnp.asarray(table))
 
 
-def plane_kernel(got_ref, sy_ref, sx_ref, ax_ref, ay_ref, out_ref, spec_ref, cell_ref):
-    plane = pl.program_id(0)
+def plane_kernel(plane, got_ref, sy_ref, sx_ref, ax_ref, ay_ref, *refs):
+    if plane == 0:
+        out_ref, rest_ref, spec_ref, cell_ref = refs
+    else:
+        rest_ref, out_ref, spec_ref, cell_ref = refs
+    chunk = ROWS_X * SENT
     half_sign = jnp.where(lax.broadcasted_iota(jnp.int32, (1, 128), 1) < 64, -1.0, 1.0)
     ky_lanes = []
     for n in range(NARROW):
@@ -232,7 +229,7 @@
     def rows_of(field, n):
         return jnp.concatenate(
             [
-                got_ref[w * NARROW + n, 0, pl.ds(field, ROWS_X, stride=SENT), :]
+                got_ref[pl.ds((w * NARROW + n) * chunk + field, ROWS_X, stride=SENT), :]
                 for w in range(WIDE)
             ],
             0,
@@ -262,7 +259,7 @@
         synth([rows_of(field, n) for n in range(NARROW)], field)
         return carry
 
-    lax.fori_loop(0, SENT, each_field, 0, unroll=True)
+    lax.fori_loop(0, SENT, each_field, 0)
     swirl = []
     for n in range(NARROW):
         across = kx_rows * rows_of(4, n) - ky_lanes[n] * rows_of(3, n)
@@ -311,12 +308,12 @@
     def times_i(value):
         return pltpu.roll(value, 64, 1) * half_sign
 
-    @pl.when(plane == 0)
-    def _():
-        out_ref[KEPT_W:] = jnp.zeros((WIDE - KEPT_W,) + out_ref.shape[1:], jnp.float32)
+    out_ref[KEPT_W:] = jnp.zeros((WIDE - KEPT_W,) + out_ref.shape[1:], jnp.float32)
+    if plane == 0:
+        rest_ref[KEPT_W:] = jnp.zeros((WIDE - KEPT_W,) + rest_ref.shape[1:], jnp.float32)
 
     def put(n, tile, value):
-        rows = pl.ds(pl.multiple_of(tile * ROWS_X, ROWS_X), ROWS_X)
+        rows = slice(tile * ROWS_X, tile * ROWS_X + ROWS_X)
         out_ref[:KEPT_W, n, rows, :] = value.reshape(KEPT_W, ROWS_X, 128)
 
     def values_of(n):
@@ -335,18 +332,12 @@
     for half in range(2):
         heavy, light = HEAVY[half], LIGHT[half]
         values = values_of(heavy)
-        for f in range(3):
-            put(heavy, 3 * plane + f, values[f])
-
-        @pl.when(plane == 0)
-        def _(heavy=heavy, value=values[3]):
-            put(heavy, 6, value)
-
-        @pl.when(plane == 1)
-        def _(light=light, value=values[3]):
-            put(light, 1, value)
-
-        put(light, 2 * plane, values[4])
+        direct = 3 if plane == 0 else 4
+        for f in range(BACK):
+            if f < direct:
+                put(heavy, f, values[f])
+            else:
+                put(light, f - direct if plane == 0 else 3, values[f])
         values = values_of(light)
         packed = []
         for tile in range(2):
@@ -358,85 +349,149 @@
                 )
                 value = jnp.where((lane >= SLOT * slot) & (lane < SLOT * slot + SLOT), moved, value)
             packed.append(value)
-        for tile in range(2):
-            put(light, 3 + 2 * plane + tile, packed[tile])
-
-
-def run_planes(got):
+        if plane == 0:
+            put(light, 2, packed[0])
+            rest_ref[:KEPT_W, half] = packed[1].reshape(KEPT_W, ROWS_X, 128)
+        else:
+            out_ref[:, light, 0:ROWS_X, :] = rest_ref[:, half]
+            put(light, 1, packed[0])
+            put(light, 2, packed[1])
+
+
+def run_plane(plane, got, rest=None):
     tables = [tables_synth_y(), tables_synth_x(), tables_anal_x(), tables_anal_y()]
-    shape = (WIDE, NARROW, TILES * ROWS_X, 128)
-    return pl.pallas_call(
-        plane_kernel,
-        grid=(2,),
-        out_shape=jax.ShapeDtypeStruct(shape, jnp.float32),
-        in_specs=[pl.BlockSpec((DEVICES, 1, ROWS_X * SENT, 128), lambda i: (0, i, 0, 0))]
-        + [pl.BlockSpec(table.shape, lambda i: (0, 0, 0, 0)) for table in tables],
-        out_specs=pl.BlockSpec(shape, lambda i: (0, 0, 0, 0)),
+    tiles = 3 + plane
+    out_shape = [jax.ShapeDtypeStruct((WIDE, NARROW, tiles * ROWS_X, 128), jnp.float32)]
+    operands = [got.reshape(DEVICES * ROWS_X * SENT, 128)] + [jnp.asarray(t) for t in tables]
+    if plane == 0:
+        out_shape.append(jax.ShapeDtypeStruct((WIDE, 2, ROWS_X, 128), jnp.float32))
+    else:
+        operands.append(rest)
+    outs = pl.pallas_call(
+        functools.partial(plane_kernel, plane),
+        out_shape=out_shape,
+        in_specs=[pl.BlockSpec(memory_space=pltpu.VMEM)] * len(operands),
+        out_specs=[pl.BlockSpec(memory_space=pltpu.VMEM)] * len(out_shape),
         scratch_shapes=[
             pltpu.VMEM((6, 2, KEPT_X, 256), jnp.float32),
             pltpu.VMEM((9, 2, 256, 256), jnp.float32),
         ],
         compiler_params=pltpu.CompilerParams(vmem_limit_bytes=vmem_bytes),
         name="plane",
-    )(got, *[jnp.asarray(table) for table in tables])
+    )(*operands)
+    return [outs[0].reshape(DEVICES, tiles * ROWS_X, 128)] + list(outs[1:])
+
+
+def span_of(rows, table):
+    upper, lower = split(rows.T)
+    return dot(jnp.concatenate([upper, lower, upper], 1), table, ((1,), (0,)))
+
+
+def unite(span, real_rows, imag_rows):
+    real, imag = span[real_rows], span[imag_rows]
+    return real[:, :128] + imag[:, 128:], imag[:, :128] - real[:, 128:]
+
+
+def mirror(first, second):
+    return tuple(
+        jnp.concatenate([one + two, one - two], 1) for one, two in zip(first, second)
+    )
+
+
+def light_narrow(narrow):
+    return (narrow == LIGHT[0]) | (narrow == LIGHT[1])
+
+
+def tile_copies(source_ref, first, count, target_ref, at, sems):
+    return [
+        pltpu.make_async_copy(
+            source_ref.at[:, pl.ds((first + tile) * ROWS_X, ROWS_X)],
+            target_ref.at[at + tile],
+            sems.at[at + tile],
+        )
+        for tile in range(count)
+    ]
+
+
+def begin_kernel(
+    place_ref, back_ref, more_ref, table_ref, part_ref, got_ref, new_ref, sems, whole_sems
+):
+    def store(k):
+        return pltpu.make_async_copy(new_ref.at[:, :, k], part_ref.at[:, :, k], sems.at[k])
+
+    @pl.when(jnp.logical_not(light_narrow(place_ref[1])))
+    def _():
+        pieces = tile_copies(back_ref, 0, 3, got_ref, 0, whole_sems)
+        pieces += tile_copies(more_ref, 0, 2, got_ref, 3, whole_sems)
+        for copy in pieces:
+            copy.start()
+        for copy in pieces:
+            copy.wait()
+        for k in range(ROWS_X):
+            for f in range(BACK):
+                span = span_of(got_ref[f, :, k, :], table_ref[0])
+                real, imag = unite(span, slice(0, 64), slice(64, 128))
+                new_ref[f, 0, k] = real
+                new_ref[f, 1, k] = imag
+            store(k).start()
+        for k in range(ROWS_X):
+            store(k).wait()
+
+
+def begin(place, back, more):
+    table = tables_anal_z()
+    block = (BACK, 2, ROWS_X, ROWS_Y, 128)
+    return pl.pallas_call(
+        begin_kernel,
+        in_specs=[
+            pl.BlockSpec(memory_space=pltpu.SMEM),
+            pl.BlockSpec(memory_space=pltpu.HBM),
+            pl.BlockSpec(memory_space=pltpu.HBM),
+            pl.BlockSpec(memory_space=pltpu.VMEM),
+        ],
+        out_specs=pl.BlockSpec(memory_space=pltpu.HBM),
+        out_shape=jax.ShapeDtypeStruct(block, jnp.float32),
+        scratch_shapes=[
+            pltpu.VMEM((BACK, DEVICES, ROWS_X, 128), jnp.float32),
+            pltpu.VMEM(block, jnp.float32),
+            pltpu.SemaphoreType.DMA((ROWS_X,)),
+            pltpu.SemaphoreType.DMA((BACK,)),
+        ],
+        compiler_params=pltpu.CompilerParams(vmem_limit_bytes=vmem_bytes),
+        name="begin",
+    )(place, back, more, jnp.asarray(table))
 
 
 def finish_kernel(
     place_ref,
-    back_ref,
+    back0_ref,
+    back1_ref,
     more_ref,
+    part_ref,
     adjoint_ref,
     table_ref,
     out_ref,
     got_ref,
-    fwd_ref,
+    mid_ref,
     old_ref,
     new_ref,
     sems,
     whole_sems,
 ):
     narrow = place_ref[1]
-    is_light = (narrow == LIGHT[0]) | (narrow == LIGHT[1])
+    is_light = light_narrow(narrow)
 
     def load(k):
-        return pltpu.make_async_copy(
-            adjoint_ref.at[:, :, k], old_ref.at[:, :, k], sems.at[0, k]
-        )
+        return pltpu.make_async_copy(adjoint_ref.at[:, :, k], old_ref.at[:, :, k], sems.at[0, k])
+
+    def fetch(k):
+        return pltpu.make_async_copy(part_ref.at[:, :, k], mid_ref.at[:, :, k], sems.at[2, k])
 
     def store(k):
         return pltpu.make_async_copy(new_ref.at[:, :, k], out_ref.at[:, :, k], sems.at[1, k])
 
-    wholes = [
-        pltpu.make_async_copy(back_ref, got_ref, whole_sems.at[0]),
-        pltpu.make_async_copy(more_ref, fwd_ref, whole_sems.at[1]),
-    ]
-    for copy in wholes:
-        copy.start()
-    for k in range(ROWS_X):
-        load(k).start()
-    for copy in wholes:
-        copy.wait()
     number_z = signed(lax.broadcasted_iota(jnp.int32, (1, NZ), 1), NZ)
     kz = 2.0 * math.pi / NZ * number_z.astype(jnp.float32)
-
-    def span_of(k, first, second):
-        spans = []
-        for plane, (ref, tile) in enumerate((first, second)):
-            rows = ref[:, tile * ROWS_X + k, :]
-            upper, lower = split(rows.T)
-            spans.append(dot(jnp.concatenate([upper, lower, upper], 1), table_ref[plane], ((1,), (0,))))
-        return spans
-
-    def unite(spans, real_rows, imag_rows):
-        parts = []
-        for span in spans:
-            real, imag = span[real_rows], span[imag_rows]
-            parts.append((real[:, :128] + imag[:, 128:], imag[:, :128] - real[:, 128:]))
-        (real_0, imag_0), (real_1, imag_1) = parts
-        return (
-            jnp.concatenate([real_0 + real_1, real_0 - real_1], 1),
-            jnp.concatenate([imag_0 + imag_1, imag_0 - imag_1], 1),
-        )
 
     def emit(k, got, start, rows):
         number_x = place_ref[0] * ROWS_X + k
@@ -467,40 +522,69 @@
 
     @pl.when(jnp.logical_not(is_light))
     def _():
+        pieces = tile_copies(back1_ref, 0, 4, got_ref, 0, whole_sems)
+        pieces += tile_copies(more_ref, 0, 1, got_ref, 4, whole_sems)
+        for copy in pieces:
+            copy.start()
         for k in range(ROWS_X):
+            fetch(k).start()
+            load(k).start()
+        for copy in pieces:
+            copy.wait()
+        for k in range(ROWS_X):
+            fetch(k).wait()
             got = []
             for f in range(BACK):
-                first = (got_ref, (0, 1, 2, 6)[f]) if f < 4 else (fwd_ref, 0)
-                second = (got_ref, 3 + f) if f < 3 else (fwd_ref, f - 2)
-                spans = span_of(k, first, second)
-                got.append(unite(spans, slice(0, 64), slice(64, 128)))
+                span = span_of(got_ref[f, :, k, :], table_ref[1])
+                second = unite(span, slice(0, 64), slice(64, 128))
+                got.append(mirror((mid_ref[f, 0, k], mid_ref[f, 1, k]), second))
             load(k).wait()
             emit(k, got, 0, ROWS_Y)
             store(k).start()
 
     @pl.when(is_light)
     def _():
+        pieces = tile_copies(back1_ref, 0, 3, got_ref, 0, whole_sems)
+        pieces += tile_copies(back0_ref, 2, 1, got_ref, 3, whole_sems)
+        for copy in pieces:
+            copy.start()
         for k in range(ROWS_X):
-            tiles = [
-                span_of(k, (got_ref, 3), (got_ref, 5)),
-                span_of(k, (got_ref, 4), (got_ref, 6)),
+            load(k).start()
+        for copy in pieces:
+            copy.wait()
+        number_y = lax.broadcasted_iota(jnp.int32, (ROWS_Y, 1), 0) + narrow * ROWS_Y
+        ky = 2.0 * math.pi / NY * signed(number_y, NY).astype(jnp.float32)
+        for k in range(ROWS_X):
+            spans = [
+                [
+                    span_of(got_ref[tile, :, k, :], table_ref[plane])
+                    for plane, tile in enumerate(tiles)
+                ]
+                for tiles in ((3, 1), (0, 2))
             ]
+
+            def item(index, plane):
+                tile, slot = divmod(index, 5)
+                return spans[tile][plane][SLOT * slot : SLOT * slot + SLOT]
+
+            got = []
+            for f in range(BACK):
+                halves_of = [
+                    unite(
+                        jnp.concatenate([item(2 * f, plane), item(2 * f + 1, plane)], 0),
+                        slice(0, SLOT),
+                        slice(SLOT, 2 * SLOT),
+                    )
+                    for plane in range(2)
+                ]
+                got.append(mirror(*halves_of))
             number_x = place_ref[0] * ROWS_X + k
             kx = 2.0 * math.pi / NX * number_x.astype(jnp.float32)
-            number_y = lax.broadcasted_iota(jnp.int32, (ROWS_Y, 1), 0) + narrow * ROWS_Y
-            ky = 2.0 * math.pi / NY * signed(number_y, NY).astype(jnp.float32)
             decay = jnp.exp(-viscous_rate * (kx * kx + ky * ky + kz * kz))
             load(k).wait()
             for c in range(3):
                 for part in range(2):
                     new_ref[c, part, k] = decay * old_ref[c, part, k]
-            got = []
-            for f in range(BACK):
-                (tile, slot), (tile_i, slot_i) = divmod(2 * f, 5), divmod(2 * f + 1, 5)
-                real = [span[SLOT * slot : SLOT * slot + SLOT] for span in tiles[tile]]
-                imag = [span[SLOT * slot_i : SLOT * slot_i + SLOT] for span in tiles[tile_i]]
-                pairs = [jnp.concatenate([r, i], 0) for r, i in zip(real, imag)]
-                got.append(unite(pairs, slice(0, SLOT), slice(SLOT, 2 * SLOT)))
             start = pl.multiple_of(jnp.where(narrow == LIGHT[0], 0, LIGHT_ROW[1]), 8)
             emit(k, got, start, SLOT)
             store(k).start()
@@ -509,31 +593,27 @@
         store(k).wait()
 
 
-def finish(place, back, more, adjoint_hat):
+def finish(place, arrays, adjoint_hat):
     table = tables_anal_z()
     block = (3, 2, ROWS_X, ROWS_Y, NZ)
     return pl.pallas_call(
         finish_kernel,
-        in_specs=[
-            pl.BlockSpec(memory_space=pltpu.SMEM),
-            pl.BlockSpec(memory_space=pl.ANY),
-            pl.BlockSpec(memory_space=pl.ANY),
-            pl.BlockSpec(memory_space=pl.ANY),
-            pl.BlockSpec(memory_space=pltpu.VMEM),
-        ],
-        out_specs=pl.BlockSpec(memory_space=pl.ANY),
+        in_specs=[pl.BlockSpec(memory_space=pltpu.SMEM)]
+        + [pl.BlockSpec(memory_space=pltpu.HBM)] * 5
+        + [pl.BlockSpec(memory_space=pltpu.VMEM)],
+        out_specs=pl.BlockSpec(memory_space=pltpu.HBM),
         out_shape=jax.ShapeDtypeStruct(block, jnp.float32),
         scratch_shapes=[
-            pltpu.VMEM(back.shape, jnp.float32),
-            pltpu.VMEM(more.shape, jnp.float32),
+            pltpu.VMEM((BACK, DEVICES, ROWS_X, 128), jnp.float32),
+            pltpu.VMEM((BACK, 2, ROWS_X, ROWS_Y, 128), jnp.float32),
             pltpu.VMEM(block, jnp.float32),
             pltpu.VMEM(block, jnp.float32),
-            pltpu.SemaphoreType.DMA((2, ROWS_X)),
-            pltpu.SemaphoreType.DMA((2,)),
+            pltpu.SemaphoreType.DMA((3, ROWS_X)),
+            pltpu.SemaphoreType.DMA((BACK,)),
         ],
         compiler_params=pltpu.CompilerParams(vmem_limit_bytes=vmem_bytes),
         name="finish",
-    )(place, back, more, adjoint_hat, jnp.asarray(table))
+    )(place, *arrays, adjoint_hat, jnp.asarray(table))
 
 
 def swap(chunks):
@@ -546,10 +626,16 @@
 
 def local(adjoint_hat, velocity_hat):
     place = jnp.stack([lax.axis_index("wide"), lax.axis_index("narrow")]).astype(jnp.int32)
-    got = swap(synth_z(place, adjoint_hat, velocity_hat))
-    back = swap(run_planes(got).reshape(DEVICES, TILES * ROWS_X, 128))
-    more = forward(back[:, : 3 * ROWS_X])
-    return finish(place, back, more, adjoint_hat)
+    got = [swap(synth_z(place, adjoint_hat, velocity_hat, plane)) for plane in range(2)]
+    out0, rest = run_plane(0, got[0])
+    back0 = swap(out0)
+    (out1,) = run_plane(1, got[1], rest)
+    back1 = swap(out1)
+    more0 = forward(back0[:, : 2 * ROWS_X])
+    part = begin(place, back0, more0)
+    back1, part = lax.optimization_barrier((back1, part))
+    more1 = forward(back1[:, 3 * ROWS_X :])
+    return finish(place, [back0, back1, more1, part], adjoint_hat)
 
 
 def solution(mesh):

time: 227 us -> 217 us (0.956)
  blocking collectives: 168 us -> 0 us
  waiting for transfers between devices: 4.14 us -> 115 us
  starting transfers between devices: 1.29 us -> 35.1 us
  Pallas kernels: 51.8 us -> 62.7 us
  local copies, waits for them, and re-layouts: 0.11 us -> 2.95 us
    all_to_all x2 -> x0, blocking collectives: 168 us -> none  [swap(): return lax.all_to_all(chunks, ('wide', 'narrow'), 0, 0, tiled=True)]
    all_to_all x0 -> x4, waiting for transfers between devices: none -> 109 us  [swap(): return lax.all_to_all(chunks, ('wide', 'narrow'), 0, 0, tiled=True)]
    all_to_all x0 -> x4, starting transfers between devices: none -> 32.5 us  [swap(): return lax.all_to_all(chunks, ('wide', 'narrow'), 0, 0, tiled=True)]
    pallas_call x2 -> x5, Pallas kernels: 38.9 us -> 52.6 us  [the longest x2 29.1 us: run_plane(): pl.pallas_call(functools.partial(plane_kernel, plane), out_shape=out_shap...]
    pallas_call x1, Pallas kernels: 12.9 us -> 10.1 us  [finish(): pl.pallas_call(finish_kernel, in_specs=[pl.BlockSpec(memory_space=pltpu.S...]
    ppermute x1 -> x2, waiting for transfers between devices: 4.14 us -> 5.76 us  [forward(): lax.ppermute(tiles, 'narrow', [(LIGHT[0], HEAVY[0]), (LIGHT[1], HEAVY[1])])]
  transfers between devices with their start and end apart: 1 -> 6, of which waited for: 1 -> 6; matrix products, arithmetic and copies ran while one was open for 0% -> 0% of each run, Pallas kernels for 0% -> 20%
where the time goes in v5:
time: 217 us; the launch traced here: 216 us
  waiting for transfers between devices  115 us (53%)
  Pallas kernels  62.7 us (29%)
  starting transfers between devices  35.1 us (16%)
  local copies, waits for them, and re-layouts  2.95 us (1%)
    all_to_all x4, waiting for transfers between devices, swap(): return lax.all_to_all(chunks, ('wide', 'narrow'), 0, 0, tiled=True)  109 us
    all_to_all x4, starting transfers between devices, swap(): return lax.all_to_all(chunks, ('wide', 'narrow'), 0, 0, tiled=True)  32.5 us
    pallas_call x2, Pallas kernels, run_plane(): pl.pallas_call(functools.partial(plane_kernel, plane), out_shape=out_shap...  29.1 us
    pallas_call x2, Pallas kernels, synth_z(): pl.pallas_call(functools.partial(synth_z_kernel, plane), in_specs=[pl.Blo...  17.6 us
    pallas_call x1, Pallas kernels, finish(): pl.pallas_call(finish_kernel, in_specs=[pl.BlockSpec(memory_space=pltpu.S...  10.1 us
    pallas_call x1, Pallas kernels, begin(): pl.pallas_call(begin_kernel, in_specs=[pl.BlockSpec(memory_space=pltpu.SM...  5.85 us
    ppermute x2, waiting for transfers between devices, forward(): lax.ppermute(tiles, 'narrow', [(LIGHT[0], HEAVY[0]), (LIGHT[1], HEAVY[1])])  5.76 us
  transfers between devices with their start and end apart: 6, of which 6 were waited for; matrix products, arithmetic and copies ran while one was open for 0% of the time, Pallas kernels for 20%

profile of v5, /device:TPU:0, one launch (start us, length us, event | category | flops | bytes accessed | tf_op | source)
XLA Modules:
  0.0 216.3 jit_solution(11137542594705654622)
XLA Ops:
  0.0 0.6 pad_add_fusion.place_ref
  0.6 8.8 %synth_z.2 = f32[128,64,128]{2,1,0:T(8,128)} custom-call(s32[2]{0:T(128)} %pad_add_fusion.place_ref, f32[3,2,8,64,256]{4,3,2,1,0:T(8,128)} %adjoint_ref.5, f32[3,2,8,64,256]{4,3,2,1,0:T(8,128)} %velocity_ref.3, bf16[256,384]{1,0:T(8,128)(2,1)} %constant.23.clone.table_ref), custom_call_target="tpu_custom_call" | custom-call | tf_op jit(solution)/shard_map/synth_z/pallas_call | solution.py:190
  9.4 11.7 %all-to-all-start = ((f32[128,64,128]{2,1,0:T(8,128)}), f32[128,64,128]{2,1,0:T(8,128)}, u32[]{:S(2)}, u32[]{:S(2)}) async-start(f32[128,64,128]{2,1,0:T(8,128)} %synth_z.2), calls=%async_computation | async-start | bytes 8388608 | tf_op jit(solution)/shard_map/all_to_all | solution.py:620
  21.1 8.8 %synth_z.3 = f32[128,64,128]{2,1,0:T(8,128)} custom-call(s32[2]{0:T(128)} %pad_add_fusion.place_ref, f32[3,2,8,64,256]{4,3,2,1,0:T(8,128)} %adjoint_ref.5, f32[3,2,8,64,256]{4,3,2,1,0:T(8,128)} %velocity_ref.3, bf16[256,384]{1,0:T(8,128)(2,1)} %constant.24.clone.table_ref), custom_call_target="tpu_custom_call" | custom-call | tf_op jit(solution)/shard_map/synth_z/pallas_call | solution.py:190
  29.9 43.3 %all-to-all-done = f32[128,64,128]{2,1,0:T(8,128)} async-done(((f32[128,64,128]{2,1,0:T(8,128)}), f32[128,64,128]{2,1,0:T(8,128)}, u32[]{:S(2)}, u32[]{:S(2)}) %all-to-all-start) | async-done | bytes 4194336 | tf_op jit(solution)/shard_map/all_to_all | solution.py:620
  73.2 7.8 %all-to-all-start.2 = ((f32[128,64,128]{2,1,0:T(8,128)}), f32[128,64,128]{2,1,0:T(8,128)}, u32[]{:S(2)}, u32[]{:S(2)}) async-start(f32[128,64,128]{2,1,0:T(8,128)} %synth_z.3), calls=%async_computation.2 | async-start | bytes 8388608 | tf_op jit(solution)/shard_map/all_to_all | solution.py:620
  81.0 14.5 %plane.2 = (f32[32,4,24,128]{3,2,1,0:T(8,128)}, f32[32,2,8,128]{3,2,1,0:T(8,128)}) custom-call(f32[8192,128]{1,0:T(8,128)} %bitcast.2.got_ref, bf16[2,2,256,256]{3,2,1,0:T(8,128)(2,1)} %constant.25.clone.sy_ref, bf16[2,2,256,256]{3,2,1,0:T(8,128)(2,1)} %constant.26.clone.sx_ref, bf16[2,2,176,256]{3,2,1,0:T(8,128)(2,1)} %constant.27.clone.ax_ref, ...), custom_call_target="tpu_custom_call" | custom-call | tf_op jit(solution)/shard_map/plane/pallas_call | solution.py:370
  95.5 37.6 %all-to-all-done.2 = f32[128,64,128]{2,1,0:T(8,128)} async-done(((f32[128,64,128]{2,1,0:T(8,128)}), f32[128,64,128]{2,1,0:T(8,128)}, u32[]{:S(2)}, u32[]{:S(2)}) %all-to-all-start.2) | async-done | bytes 4194336 | tf_op jit(solution)/shard_map/all_to_all | solution.py:620
  133.1 7.2 %all-to-all-start.1 = ((f32[128,24,128]{2,1,0:T(8,128)}), f32[128,24,128]{2,1,0:T(8,128)S(1)}, u32[]{:S(2)}, u32[]{:S(2)}) async-start(f32[128,24,128]{2,1,0:T(8,128)} %bitcast.7), calls=%async_computation.1 | async-start | bytes 3145728 | tf_op jit(solution)/shard_map/all_to_all | solution.py:620
  140.3 14.6 %plane.3 = f32[32,4,32,128]{3,2,1,0:T(8,128)} custom-call(f32[8192,128]{1,0:T(8,128)} %bitcast.4.got_ref, bf16[2,2,256,256]{3,2,1,0:T(8,128)(2,1)} %constant.25.clone.sy_ref, bf16[2,2,256,256]{3,2,1,0:T(8,128)(2,1)} %constant.26.clone.sx_ref, bf16[2,2,176,256]{3,2,1,0:T(8,128)(2,1)} %constant.27.clone.ax_ref, ...), custom_call_target="tpu_custom_call" | custom-call | tf_op jit(solution)/shard_map/plane/pallas_call | solution.py:370
  155.0 9.9 %all-to-all-done.1.back_ref.back0_ref = f32[128,24,128]{2,1,0:T(8,128)S(1)} async-done(((f32[128,24,128]{2,1,0:T(8,128)}), f32[128,24,128]{2,1,0:T(8,128)S(1)}, u32[]{:S(2)}, u32[]{:S(2)}) %all-to-all-start.1) | async-done | bytes 1572896 | tf_op jit(solution)/shard_map/all_to_all | solution.py:620
  164.8 0.0 copy-start
  164.8 5.8 %all-to-all-start.3 = ((f32[128,32,128]{2,1,0:T(8,128)}), f32[128,32,128]{2,1,0:T(8,128)}, u32[]{:S(2)}, u32[]{:S(2)}) async-start(f32[128,32,128]{2,1,0:T(8,128)} %bitcast.6), calls=%async_computation.3 | async-start | bytes 4194304 | tf_op jit(solution)/shard_map/all_to_all | solution.py:620
  170.6 0.1 slice.8
  170.7 0.0 copy-done
  170.7 1.3 collective-permute-start
  172.0 3.3 %collective-permute-done.more_ref = f32[128,16,128]{2,1,0:T(8,128)S(1)} collective-permute-done((f32[128,16,128]{2,1,0:T(8,128)S(1)}, f32[128,16,128]{2,1,0:T(8,128)S(1)}, u32[]{:S(2)}, u32[]{:S(2)}) %collective-permute-start) | collective-permute-done | bytes 1048608 | tf_op jit(solution)/shard_map/ppermute | solution.py:624
  175.3 0.0 copy-start.1
  175.3 1.0 copy-done.1
  176.3 5.9 %begin.1.part_ref = f32[5,2,8,64,128]{4,3,2,1,0:T(8,128)} custom-call(s32[2]{0:T(128)} %pad_add_fusion.place_ref, f32[128,24,128]{2,1,0:T(8,128)} %copy-done, f32[128,16,128]{2,1,0:T(8,128)} %copy-done.1, bf16[2,384,256]{2,1,0:T(8,128)(2,1)} %constant.29.clone.table_ref), custom_call_target="tpu_custom_call" | custom-call | tf_op jit(solution)/shard_map/begin/pallas_call | solution.py:444
  182.1 18.2 %all-to-all-done.3.back1_ref = f32[128,32,128]{2,1,0:T(8,128)} async-done(((f32[128,32,128]{2,1,0:T(8,128)}), f32[128,32,128]{2,1,0:T(8,128)}, u32[]{:S(2)}, u32[]{:S(2)}) %all-to-all-start.3) | async-done | bytes 2097184 | tf_op jit(solution)/shard_map/all_to_all | solution.py:620
  200.3 1.1 slice.7
  201.4 1.3 collective-permute-start.1
  202.7 2.5 %collective-permute-done.1.more_ref = f32[128,8,128]{2,1,0:T(8,128)S(1)} collective-permute-done((f32[128,8,128]{2,1,0:T(8,128)S(1)}, f32[128,8,128]{2,1,0:T(8,128)S(1)}, u32[]{:S(2)}, u32[]{:S(2)}) %collective-permute-start.1) | collective-permute-done | bytes 524320 | tf_op jit(solution)/shard_map/ppermute | solution.py:624
  205.2 0.0 copy-start.2
  205.2 0.8 copy-done.2
  206.0 10.1 %finish.1 = f32[3,2,8,64,256]{4,3,2,1,0:T(8,128)} custom-call(s32[2]{0:T(128)} %pad_add_fusion.place_ref, f32[128,24,128]{2,1,0:T(8,128)} %copy-done, f32[128,32,128]{2,1,0:T(8,128)} %all-to-all-done.3.back1_ref, f32[128,8,128]{2,1,0:T(8,128)} %copy-done.2, f32[5,2,8,64,128]{4,3,2,1,0:T(8,128)} %begin.1.part_ref, f32[3,2,8,64,256]{4,3,2,1,0:T(8,128)} %adjoint_ref.5, ...), custom_call_target="tpu_custom_call" | custom-call | tf_op jit(solution)/shard_map/finish/pallas_call | solution.py:599
Async XLA Ops:
  9.4 63.8 %all-to-all-start = ((f32[128,64,128]{2,1,0:T(8,128)}), f32[128,64,128]{2,1,0:T(8,128)}, u32[]{:S(2)}, u32[]{:S(2)}) async-start(f32[128,64,128]{2,1,0:T(8,128)} %synth_z.2), calls=%async_computation | async-start | bytes 8388608 | tf_op jit(solution)/shard_map/all_to_all | solution.py:620
  73.2 59.9 %all-to-all-start.2 = ((f32[128,64,128]{2,1,0:T(8,128)}), f32[128,64,128]{2,1,0:T(8,128)}, u32[]{:S(2)}, u32[]{:S(2)}) async-start(f32[128,64,128]{2,1,0:T(8,128)} %synth_z.3), calls=%async_computation.2 | async-start | bytes 8388608 | tf_op jit(solution)/shard_map/all_to_all | solution.py:620
  133.1 31.7 %all-to-all-start.1 = ((f32[128,24,128]{2,1,0:T(8,128)}), f32[128,24,128]{2,1,0:T(8,128)S(1)}, u32[]{:S(2)}, u32[]{:S(2)}) async-start(f32[128,24,128]{2,1,0:T(8,128)} %bitcast.7), calls=%async_computation.1 | async-start | bytes 3145728 | tf_op jit(solution)/shard_map/all_to_all | solution.py:620
  164.8 5.9 %copy-start = (f32[128,24,128]{2,1,0:T(8,128)}, f32[128,24,128]{2,1,0:T(8,128)S(1)}, u32[]{:S(2)}) copy-start(f32[128,24,128]{2,1,0:T(8,128)S(1)} %all-to-all-done.1.back_ref.back0_ref) | copy-start | bytes 4718596
  164.8 35.5 %all-to-all-start.3 = ((f32[128,32,128]{2,1,0:T(8,128)}), f32[128,32,128]{2,1,0:T(8,128)}, u32[]{:S(2)}, u32[]{:S(2)}) async-start(f32[128,32,128]{2,1,0:T(8,128)} %bitcast.6), calls=%async_computation.3 | async-start | bytes 4194304 | tf_op jit(solution)/shard_map/all_to_all | solution.py:620
  170.7 4.6 %collective-permute-start = (f32[128,16,128]{2,1,0:T(8,128)S(1)}, f32[128,16,128]{2,1,0:T(8,128)S(1)}, u32[]{:S(2)}, u32[]{:S(2)}) collective-permute-start(f32[128,16,128]{2,1,0:T(8,128)S(1)} %slice.8), channel_id=1, source_target_pairs={{32,0},{64,96},{33,1},{65,97},{34,2},{66,98},{35,3},{67,99},{36,4}... | collective-permute-start | bytes 3145736 | tf_op jit(solution)/shard_map/ppermute | solution.py:624
  175.3 1.0 copy-start.1
  201.4 3.8 %collective-permute-start.1 = (f32[128,8,128]{2,1,0:T(8,128)S(1)}, f32[128,8,128]{2,1,0:T(8,128)S(1)}, u32[]{:S(2)}, u32[]{:S(2)}) collective-permute-start(f32[128,8,128]{2,1,0:T(8,128)S(1)} %slice.7), channel_id=1, source_target_pairs={{32,0},{64,96},{33,1},{65,97},{34,2},{66,98},{35,3},{67,99},{36,4}... | collective-permute-start | bytes 1572872 | tf_op jit(solution)/shard_map/ppermute | solution.py:624
  205.2 0.8 copy-start.2

commit v6 on v5

--- a/solution.py
+++ b/solution.py
@@ -136,7 +136,7 @@
 
 
 def synth_z_kernel(
-    plane, place_ref, adjoint_ref, velocity_ref, table_ref, out_ref, adj_ref, vel_ref, sent_ref, sems
+    plane, adjoint_ref, velocity_ref, table_ref, out_ref, adj_ref, vel_ref, sent_ref, sems
 ):
     def load(k, which):
         source, target = ((adjoint_ref, adj_ref), (velocity_ref, vel_ref))[which]
@@ -150,12 +150,12 @@
     for k in range(ROWS_X):
         for which in range(2):
             load(k, which).start()
-    ky = wave_y(place_ref[1] * ROWS_Y, (ROWS_Y, 1), 0)
+    ky = wave_y(lax.axis_index("narrow") * ROWS_Y, (ROWS_Y, 1), 0)
     kz = wave_z((1, NZ), 1)
     half_sign = jnp.where(lax.broadcasted_iota(jnp.int32, (1, 128), 1) < 64, -1.0, 1.0)
 
     for k in range(ROWS_X):
-        number_x = place_ref[0] * ROWS_X + k
+        number_x = lax.axis_index("wide") * ROWS_X + k
         kx = 2.0 * math.pi / NX * number_x.astype(jnp.float32)
         for which in range(2):
             load(k, which).wait()
@@ -183,14 +183,13 @@
         store(k).wait()
 
 
-def synth_z(place, adjoint_hat, velocity_hat, plane):
+def synth_z(adjoint_hat, velocity_hat, plane):
     table = tables_synth_z()[plane]
     shape = (DEVICES, ROWS_X * SENT, 128)
     block = (3, 2, ROWS_X, ROWS_Y, NZ)
     return pl.pallas_call(
         functools.partial(synth_z_kernel, plane),
         in_specs=[
-            pl.BlockSpec(memory_space=pltpu.SMEM),
             pl.BlockSpec(memory_space=pl.ANY),
             pl.BlockSpec(memory_space=pl.ANY),
             pl.BlockSpec(memory_space=pltpu.VMEM),
@@ -205,7 +204,7 @@
         ],
         compiler_params=pltpu.CompilerParams(vmem_limit_bytes=vmem_bytes),
         name="synth_z",
-    )(place, adjoint_hat, velocity_hat, jnp.asarray(table))
+    )(adjoint_hat, velocity_hat, jnp.asarray(table))
 
 
 def plane_kernel(plane, got_ref, sy_ref, sx_ref, ax_ref, ay_ref, *refs):
@@ -382,9 +381,10 @@
     return [outs[0].reshape(DEVICES, tiles * ROWS_X, 128)] + list(outs[1:])
 
 
-def span_of(rows, table):
-    upper, lower = split(rows.T)
-    return dot(jnp.concatenate([upper, lower, upper], 1), table, ((1,), (0,)))
+def spans_of(tiles, table):
+    upper, lower = split(jnp.concatenate([rows.T for rows in tiles], 0))
+    span = dot(jnp.concatenate([upper, lower, upper], 1), table, ((1,), (0,)))
+    return [span[128 * at : 128 * at + 128] for at in range(len(tiles))]
 
 
 def unite(span, real_rows, imag_rows):
@@ -414,12 +414,12 @@
 
 
 def begin_kernel(
-    place_ref, back_ref, more_ref, table_ref, part_ref, got_ref, new_ref, sems, whole_sems
+    back_ref, more_ref, table_ref, part_ref, got_ref, new_ref, sems, whole_sems
 ):
     def store(k):
         return pltpu.make_async_copy(new_ref.at[:, :, k], part_ref.at[:, :, k], sems.at[k])
 
-    @pl.when(jnp.logical_not(light_narrow(place_ref[1])))
+    @pl.when(jnp.logical_not(light_narrow(lax.axis_index("narrow"))))
     def _():
         pieces = tile_copies(back_ref, 0, 3, got_ref, 0, whole_sems)
         pieces += tile_copies(more_ref, 0, 2, got_ref, 3, whole_sems)
@@ -428,8 +428,8 @@
         for copy in pieces:
             copy.wait()
         for k in range(ROWS_X):
-            for f in range(BACK):
-                span = span_of(got_ref[f, :, k, :], table_ref[0])
+            spans = spans_of([got_ref[f, :, k, :] for f in range(BACK)], table_ref[0])
+            for f, span in enumerate(spans):
                 real, imag = unite(span, slice(0, 64), slice(64, 128))
                 new_ref[f, 0, k] = real
                 new_ref[f, 1, k] = imag
@@ -438,13 +438,12 @@
             store(k).wait()
 
 
-def begin(place, back, more):
+def begin(back, more):
     table = tables_anal_z()
     block = (BACK, 2, ROWS_X, ROWS_Y, 128)
     return pl.pallas_call(
         begin_kernel,
         in_specs=[
-            pl.BlockSpec(memory_space=pltpu.SMEM),
             pl.BlockSpec(memory_space=pltpu.HBM),
             pl.BlockSpec(memory_space=pltpu.HBM),
             pl.BlockSpec(memory_space=pltpu.VMEM),
@@ -459,11 +458,10 @@
         ],
         compiler_params=pltpu.CompilerParams(vmem_limit_bytes=vmem_bytes),
         name="begin",
-    )(place, back, more, jnp.asarray(table))
+    )(back, more, jnp.asarray(table))
 
 
 def finish_kernel(
-    place_ref,
     back0_ref,
     back1_ref,
     more_ref,
@@ -475,10 +473,11 @@
     mid_ref,
     old_ref,
     new_ref,
+    factor_ref,
     sems,
     whole_sems,
 ):
-    narrow = place_ref[1]
+    wide, narrow = lax.axis_index("wide"), lax.axis_index("narrow")
     is_light = light_narrow(narrow)
 
     def load(k):
@@ -493,31 +492,44 @@
     number_z = signed(lax.broadcasted_iota(jnp.int32, (1, NZ), 1), NZ)
     kz = 2.0 * math.pi / NZ * number_z.astype(jnp.float32)
 
+    number_y = signed(
+        lax.broadcasted_iota(jnp.int32, (ROWS_Y, 1), 0) + narrow * ROWS_Y, NY
+    )
+    all_ky = 2.0 * math.pi / NY * number_y.astype(jnp.float32)
+
+    def wave_x(k):
+        number_x = wide * ROWS_X + k
+        return number_x, 2.0 * math.pi / NX * number_x.astype(jnp.float32)
+
+    def prepare():
+        keep_yz = (3 * jnp.abs(number_y) < NY) & (3 * jnp.abs(number_z) < NZ)
+        scale_yz = keep_yz.astype(jnp.float32) * section_step
+        square_yz = all_ky * all_ky + kz * kz
+        for k in range(ROWS_X):
+            number_x, kx = wave_x(k)
+            ksquare = kx * kx + square_yz
+            decay = jnp.exp(-viscous_rate * ksquare)
+            factor_ref[0, k] = 1.0 / (ksquare + (ksquare == 0).astype(jnp.float32))
+            factor_ref[1, k] = decay
+            factor_ref[2, k] = scale_yz * (3 * number_x < NX).astype(jnp.float32) * decay
+
     def emit(k, got, start, rows):
-        number_x = place_ref[0] * ROWS_X + k
-        kx = 2.0 * math.pi / NX * number_x.astype(jnp.float32)
-        number_y = lax.broadcasted_iota(jnp.int32, (rows, 1), 0) + start + narrow * ROWS_Y
-        number_y = signed(number_y, NY)
-        ky = 2.0 * math.pi / NY * number_y.astype(jnp.float32)
+        at = pl.ds(start, rows)
+        kx = wave_x(k)[1]
+        row = lax.broadcasted_iota(jnp.int32, (rows, 1), 0) + start + narrow * ROWS_Y
+        ky = 2.0 * math.pi / NY * signed(row, NY).astype(jnp.float32)
         conv = [
             (got[0][0] + kz * got[4][1], got[0][1] - kz * got[4][0]),
             (got[1][0] - kz * got[3][1], got[1][1] + kz * got[3][0]),
             got[2],
         ]
-        keep = (
-            (3 * number_x < NX) & (3 * jnp.abs(number_y) < NY) & (3 * jnp.abs(number_z) < NZ)
-        ).astype(jnp.float32)
-        ksquare = kx * kx + ky * ky + kz * kz
-        inverse = 1.0 / (ksquare + (ksquare == 0).astype(jnp.float32))
-        decay = jnp.exp(-viscous_rate * ksquare)
+        inverse, decay, gain = [factor_ref[which, k, at, :] for which in range(3)]
         waves = (kx, ky, kz)
         for part in range(2):
             along = (kx * conv[0][part] + ky * conv[1][part] + kz * conv[2][part]) * inverse
             for c in range(3):
-                projected = keep * (conv[c][part] - waves[c] * along)
-                old = old_ref[c, part, k, pl.ds(start, rows), :]
-                new_ref[c, part, k, pl.ds(start, rows), :] = decay * (
-                    old + section_step * projected
+                new_ref[c, part, k, at, :] = decay * old_ref[c, part, k, at, :] + gain * (
+                    conv[c][part] - waves[c] * along
                 )
 
     @pl.when(jnp.logical_not(is_light))
@@ -529,13 +541,14 @@
         for k in range(ROWS_X):
             fetch(k).start()
             load(k).start()
+        prepare()
         for copy in pieces:
             copy.wait()
         for k in range(ROWS_X):
             fetch(k).wait()
             got = []
-            for f in range(BACK):
-                span = span_of(got_ref[f, :, k, :], table_ref[1])
+            spans = spans_of([got_ref[f, :, k, :] for f in range(BACK)], table_ref[1])
+            for f, span in enumerate(spans):
                 second = unite(span, slice(0, 64), slice(64, 128))
                 got.append(mirror((mid_ref[f, 0, k], mid_ref[f, 1, k]), second))
             load(k).wait()
@@ -550,22 +563,18 @@
             copy.start()
         for k in range(ROWS_X):
             load(k).start()
+        prepare()
         for copy in pieces:
             copy.wait()
-        number_y = lax.broadcasted_iota(jnp.int32, (ROWS_Y, 1), 0) + narrow * ROWS_Y
-        ky = 2.0 * math.pi / NY * signed(number_y, NY).astype(jnp.float32)
         for k in range(ROWS_X):
-            spans = [
-                [
-                    span_of(got_ref[tile, :, k, :], table_ref[plane])
-                    for plane, tile in enumerate(tiles)
-                ]
-                for tiles in ((3, 1), (0, 2))
+            by_plane = [
+                spans_of([got_ref[tile, :, k, :] for tile in tiles], table_ref[plane])
+                for plane, tiles in enumerate(((3, 0), (1, 2)))
             ]
 
             def item(index, plane):
                 tile, slot = divmod(index, 5)
-                return spans[tile][plane][SLOT * slot : SLOT * slot + SLOT]
+                return by_plane[plane][tile][SLOT * slot : SLOT * slot + SLOT]
 
             got = []
             for f in range(BACK):
@@ -578,13 +587,10 @@
                     for plane in range(2)
                 ]
                 got.append(mirror(*halves_of))
-            number_x = place_ref[0] * ROWS_X + k
-            kx = 2.0 * math.pi / NX * number_x.astype(jnp.float32)
-            decay = jnp.exp(-viscous_rate * (kx * kx + ky * ky + kz * kz))
             load(k).wait()
             for c in range(3):
                 for part in range(2):
-                    new_ref[c, part, k] = decay * old_ref[c, part, k]
+                    new_ref[c, part, k] = factor_ref[1, k] * old_ref[c, part, k]
             start = pl.multiple_of(jnp.where(narrow == LIGHT[0], 0, LIGHT_ROW[1]), 8)
             emit(k, got, start, SLOT)
             store(k).start()
@@ -593,13 +599,12 @@
         store(k).wait()
 
 
-def finish(place, arrays, adjoint_hat):
+def finish(arrays, adjoint_hat):
     table = tables_anal_z()
     block = (3, 2, ROWS_X, ROWS_Y, NZ)
     return pl.pallas_call(
         finish_kernel,
-        in_specs=[pl.BlockSpec(memory_space=pltpu.SMEM)]
-        + [pl.BlockSpec(memory_space=pltpu.HBM)] * 5
+        in_specs=[pl.BlockSpec(memory_space=pltpu.HBM)] * 5
         + [pl.BlockSpec(memory_space=pltpu.VMEM)],
         out_specs=pl.BlockSpec(memory_space=pltpu.HBM),
         out_shape=jax.ShapeDtypeStruct(block, jnp.float32),
@@ -608,12 +613,13 @@
             pltpu.VMEM((BACK, 2, ROWS_X, ROWS_Y, 128), jnp.float32),
             pltpu.VMEM(block, jnp.float32),
             pltpu.VMEM(block, jnp.float32),
+            pltpu.VMEM((3, ROWS_X, ROWS_Y, NZ), jnp.float32),
             pltpu.SemaphoreType.DMA((3, ROWS_X)),
             pltpu.SemaphoreType.DMA((BACK,)),
         ],
         compiler_params=pltpu.CompilerParams(vmem_limit_bytes=vmem_bytes),
         name="finish",
-    )(place, *arrays, adjoint_hat, jnp.asarray(table))
+    )(*arrays, adjoint_hat, jnp.asarray(table))
 
 
 def swap(chunks):
@@ -625,17 +631,16 @@
 
 
 def local(adjoint_hat, velocity_hat):
-    place = jnp.stack([lax.axis_index("wide"), lax.axis_index("narrow")]).astype(jnp.int32)
-    got = [swap(synth_z(place, adjoint_hat, velocity_hat, plane)) for plane in range(2)]
+    got = [swap(synth_z(adjoint_hat, velocity_hat, plane)) for plane in range(2)]
     out0, rest = run_plane(0, got[0])
     back0 = swap(out0)
     (out1,) = run_plane(1, got[1], rest)
     back1 = swap(out1)
     more0 = forward(back0[:, : 2 * ROWS_X])
-    part = begin(place, back0, more0)
+    part = begin(back0, more0)
     back1, part = lax.optimization_barrier((back1, part))
     more1 = forward(back1[:, 3 * ROWS_X :])
-    return finish(place, [back0, back1, more1, part], adjoint_hat)
+    return finish([back0, back1, more1, part], adjoint_hat)
 
 
 def solution(mesh):

time: 217 us -> 217 us (level)
  no operation moved by 1% of the time
where the time goes in v6:
time: 217 us; the launch traced here: 216 us
  waiting for transfers between devices  115 us (53%)
  Pallas kernels  63.4 us (29%)
  starting transfers between devices  35.1 us (16%)
  local copies, waits for them, and re-layouts  2.95 us (1%)
    all_to_all x4, waiting for transfers between devices, swap(): return lax.all_to_all(chunks, ('wide', 'narrow'), 0, 0, tiled=True)  109 us
    all_to_all x4, starting transfers between devices, swap(): return lax.all_to_all(chunks, ('wide', 'narrow'), 0, 0, tiled=True)  32.5 us
    pallas_call x2, Pallas kernels, run_plane(): pl.pallas_call(functools.partial(plane_kernel, plane), out_shape=out_shap...  29.1 us
    pallas_call x2, Pallas kernels, synth_z(): pl.pallas_call(functools.partial(synth_z_kernel, plane), in_specs=[pl.Blo...  17.6 us
    pallas_call x1, Pallas kernels, finish(): pl.pallas_call(finish_kernel, in_specs=[pl.BlockSpec(memory_space=pltpu.H...  10.6 us
    pallas_call x1, Pallas kernels, begin(): pl.pallas_call(begin_kernel, in_specs=[pl.BlockSpec(memory_space=pltpu.HB...  5.99 us
    ppermute x2, waiting for transfers between devices, forward(): lax.ppermute(tiles, 'narrow', [(LIGHT[0], HEAVY[0]), (LIGHT[1], HEAVY[1])])  5.76 us
  transfers between devices with their start and end apart: 6, of which 6 were waited for; matrix products, arithmetic and copies ran while one was open for 0% of the time, Pallas kernels for 20%

profile of v6, /device:TPU:0, one launch (start us, length us, event | category | flops | bytes accessed | tf_op | source)
XLA Modules:
  0.0 216.2 jit_solution(11789419459795776331)
XLA Ops:
  0.0 8.8 %synth_z.2 = f32[128,64,128]{2,1,0:T(8,128)} custom-call(f32[3,2,8,64,256]{4,3,2,1,0:T(8,128)} %adjoint_ref.5, f32[3,2,8,64,256]{4,3,2,1,0:T(8,128)} %velocity_ref.3, bf16[256,384]{1,0:T(8,128)(2,1)} %constant.14.clone.table_ref), custom_call_target="tpu_custom_call" | custom-call | tf_op jit(solution)/shard_map/synth_z/pallas_call | solution.py:190
  8.8 11.7 %all-to-all-start = ((f32[128,64,128]{2,1,0:T(8,128)}), f32[128,64,128]{2,1,0:T(8,128)}, u32[]{:S(2)}, u32[]{:S(2)}) async-start(f32[128,64,128]{2,1,0:T(8,128)} %synth_z.2), calls=%async_computation | async-start | bytes 8388608 | tf_op jit(solution)/shard_map/all_to_all | solution.py:626
  20.5 8.8 %synth_z.3 = f32[128,64,128]{2,1,0:T(8,128)} custom-call(f32[3,2,8,64,256]{4,3,2,1,0:T(8,128)} %adjoint_ref.5, f32[3,2,8,64,256]{4,3,2,1,0:T(8,128)} %velocity_ref.3, bf16[256,384]{1,0:T(8,128)(2,1)} %constant.15.clone.table_ref), custom_call_target="tpu_custom_call" | custom-call | tf_op jit(solution)/shard_map/synth_z/pallas_call | solution.py:190
  29.3 43.3 %all-to-all-done = f32[128,64,128]{2,1,0:T(8,128)} async-done(((f32[128,64,128]{2,1,0:T(8,128)}), f32[128,64,128]{2,1,0:T(8,128)}, u32[]{:S(2)}, u32[]{:S(2)}) %all-to-all-start) | async-done | bytes 4194336 | tf_op jit(solution)/shard_map/all_to_all | solution.py:626
  72.6 7.8 %all-to-all-start.2 = ((f32[128,64,128]{2,1,0:T(8,128)}), f32[128,64,128]{2,1,0:T(8,128)}, u32[]{:S(2)}, u32[]{:S(2)}) async-start(f32[128,64,128]{2,1,0:T(8,128)} %synth_z.3), calls=%async_computation.2 | async-start | bytes 8388608 | tf_op jit(solution)/shard_map/all_to_all | solution.py:626
  80.4 14.5 %plane.2 = (f32[32,4,24,128]{3,2,1,0:T(8,128)}, f32[32,2,8,128]{3,2,1,0:T(8,128)}) custom-call(f32[8192,128]{1,0:T(8,128)} %bitcast.got_ref, bf16[2,2,256,256]{3,2,1,0:T(8,128)(2,1)} %constant.16.clone.sy_ref, bf16[2,2,256,256]{3,2,1,0:T(8,128)(2,1)} %constant.17.clone.sx_ref, bf16[2,2,176,256]{3,2,1,0:T(8,128)(2,1)} %constant.18.clone.ax_ref, ...), custom_call_target="tpu_custom_call" | custom-call | tf_op jit(solution)/shard_map/plane/pallas_call | solution.py:369
  94.9 37.6 %all-to-all-done.2 = f32[128,64,128]{2,1,0:T(8,128)} async-done(((f32[128,64,128]{2,1,0:T(8,128)}), f32[128,64,128]{2,1,0:T(8,128)}, u32[]{:S(2)}, u32[]{:S(2)}) %all-to-all-start.2) | async-done | bytes 4194336 | tf_op jit(solution)/shard_map/all_to_all | solution.py:626
  132.5 7.2 %all-to-all-start.1 = ((f32[128,24,128]{2,1,0:T(8,128)}), f32[128,24,128]{2,1,0:T(8,128)S(1)}, u32[]{:S(2)}, u32[]{:S(2)}) async-start(f32[128,24,128]{2,1,0:T(8,128)} %bitcast.5), calls=%async_computation.1 | async-start | bytes 3145728 | tf_op jit(solution)/shard_map/all_to_all | solution.py:626
  139.7 14.6 %plane.3 = f32[32,4,32,128]{3,2,1,0:T(8,128)} custom-call(f32[8192,128]{1,0:T(8,128)} %bitcast.2.got_ref, bf16[2,2,256,256]{3,2,1,0:T(8,128)(2,1)} %constant.16.clone.sy_ref, bf16[2,2,256,256]{3,2,1,0:T(8,128)(2,1)} %constant.17.clone.sx_ref, bf16[2,2,176,256]{3,2,1,0:T(8,128)(2,1)} %constant.18.clone.ax_ref, ...), custom_call_target="tpu_custom_call" | custom-call | tf_op jit(solution)/shard_map/plane/pallas_call | solution.py:369
  154.4 9.9 %all-to-all-done.1.back_ref.back0_ref = f32[128,24,128]{2,1,0:T(8,128)S(1)} async-done(((f32[128,24,128]{2,1,0:T(8,128)}), f32[128,24,128]{2,1,0:T(8,128)S(1)}, u32[]{:S(2)}, u32[]{:S(2)}) %all-to-all-start.1) | async-done | bytes 1572896 | tf_op jit(solution)/shard_map/all_to_all | solution.py:626
  164.2 0.0 copy-start
  164.2 5.8 %all-to-all-start.3 = ((f32[128,32,128]{2,1,0:T(8,128)}), f32[128,32,128]{2,1,0:T(8,128)}, u32[]{:S(2)}, u32[]{:S(2)}) async-start(f32[128,32,128]{2,1,0:T(8,128)} %bitcast.4), calls=%async_computation.3 | async-start | bytes 4194304 | tf_op jit(solution)/shard_map/all_to_all | solution.py:626
  170.0 0.1 slice.8
  170.1 0.0 copy-done
  170.1 1.3 collective-permute-start
  171.4 3.3 %collective-permute-done.more_ref = f32[128,16,128]{2,1,0:T(8,128)S(1)} collective-permute-done((f32[128,16,128]{2,1,0:T(8,128)S(1)}, f32[128,16,128]{2,1,0:T(8,128)S(1)}, u32[]{:S(2)}, u32[]{:S(2)}) %collective-permute-start) | collective-permute-done | bytes 1048608 | tf_op jit(solution)/shard_map/ppermute | solution.py:630
  174.7 0.0 copy-start.1
  174.7 1.0 copy-done.1
  175.7 6.0 %begin.1.part_ref = f32[5,2,8,64,128]{4,3,2,1,0:T(8,128)} custom-call(f32[128,24,128]{2,1,0:T(8,128)} %copy-done, f32[128,16,128]{2,1,0:T(8,128)} %copy-done.1, bf16[2,384,256]{2,1,0:T(8,128)(2,1)} %constant.20.clone.table_ref), custom_call_target="tpu_custom_call" | custom-call | tf_op jit(solution)/shard_map/begin/pallas_call | solution.py:444
  181.7 18.1 %all-to-all-done.3.back1_ref = f32[128,32,128]{2,1,0:T(8,128)} async-done(((f32[128,32,128]{2,1,0:T(8,128)}), f32[128,32,128]{2,1,0:T(8,128)}, u32[]{:S(2)}, u32[]{:S(2)}) %all-to-all-start.3) | async-done | bytes 2097184 | tf_op jit(solution)/shard_map/all_to_all | solution.py:626
  199.8 1.1 slice.7
  200.8 1.3 collective-permute-start.1
  202.1 2.5 %collective-permute-done.1.more_ref = f32[128,8,128]{2,1,0:T(8,128)S(1)} collective-permute-done((f32[128,8,128]{2,1,0:T(8,128)S(1)}, f32[128,8,128]{2,1,0:T(8,128)S(1)}, u32[]{:S(2)}, u32[]{:S(2)}) %collective-permute-start.1) | collective-permute-done | bytes 524320 | tf_op jit(solution)/shard_map/ppermute | solution.py:630
  204.6 0.0 copy-start.2
  204.6 0.8 copy-done.2
  205.4 10.6 %finish.1 = f32[3,2,8,64,256]{4,3,2,1,0:T(8,128)} custom-call(f32[128,24,128]{2,1,0:T(8,128)} %copy-done, f32[128,32,128]{2,1,0:T(8,128)} %all-to-all-done.3.back1_ref, f32[128,8,128]{2,1,0:T(8,128)} %copy-done.2, f32[5,2,8,64,128]{4,3,2,1,0:T(8,128)} %begin.1.part_ref, f32[3,2,8,64,256]{4,3,2,1,0:T(8,128)} %adjoint_ref.5, ...), custom_call_target="tpu_custom_call" | custom-call | tf_op jit(solution)/shard_map/finish/pallas_call | solution.py:605
Async XLA Ops:
  8.8 63.8 %all-to-all-start = ((f32[128,64,128]{2,1,0:T(8,128)}), f32[128,64,128]{2,1,0:T(8,128)}, u32[]{:S(2)}, u32[]{:S(2)}) async-start(f32[128,64,128]{2,1,0:T(8,128)} %synth_z.2), calls=%async_computation | async-start | bytes 8388608 | tf_op jit(solution)/shard_map/all_to_all | solution.py:626
  72.6 59.9 %all-to-all-start.2 = ((f32[128,64,128]{2,1,0:T(8,128)}), f32[128,64,128]{2,1,0:T(8,128)}, u32[]{:S(2)}, u32[]{:S(2)}) async-start(f32[128,64,128]{2,1,0:T(8,128)} %synth_z.3), calls=%async_computation.2 | async-start | bytes 8388608 | tf_op jit(solution)/shard_map/all_to_all | solution.py:626
  132.5 31.7 %all-to-all-start.1 = ((f32[128,24,128]{2,1,0:T(8,128)}), f32[128,24,128]{2,1,0:T(8,128)S(1)}, u32[]{:S(2)}, u32[]{:S(2)}) async-start(f32[128,24,128]{2,1,0:T(8,128)} %bitcast.5), calls=%async_computation.1 | async-start | bytes 3145728 | tf_op jit(solution)/shard_map/all_to_all | solution.py:626
  164.2 5.9 %copy-start = (f32[128,24,128]{2,1,0:T(8,128)}, f32[128,24,128]{2,1,0:T(8,128)S(1)}, u32[]{:S(2)}) copy-start(f32[128,24,128]{2,1,0:T(8,128)S(1)} %all-to-all-done.1.back_ref.back0_ref) | copy-start | bytes 4718596
  164.2 35.5 %all-to-all-start.3 = ((f32[128,32,128]{2,1,0:T(8,128)}), f32[128,32,128]{2,1,0:T(8,128)}, u32[]{:S(2)}, u32[]{:S(2)}) async-start(f32[128,32,128]{2,1,0:T(8,128)} %bitcast.4), calls=%async_computation.3 | async-start | bytes 4194304 | tf_op jit(solution)/shard_map/all_to_all | solution.py:626
  170.1 4.6 %collective-permute-start = (f32[128,16,128]{2,1,0:T(8,128)S(1)}, f32[128,16,128]{2,1,0:T(8,128)S(1)}, u32[]{:S(2)}, u32[]{:S(2)}) collective-permute-start(f32[128,16,128]{2,1,0:T(8,128)S(1)} %slice.8), channel_id=1, source_target_pairs={{32,0},{64,96},{33,1},{65,97},{34,2},{66,98},{35,3},{67,99},{36,4}... | collective-permute-start | bytes 3145736 | tf_op jit(solution)/shard_map/ppermute | solution.py:630
  174.7 1.0 copy-start.1
  200.8 3.8 %collective-permute-start.1 = (f32[128,8,128]{2,1,0:T(8,128)S(1)}, f32[128,8,128]{2,1,0:T(8,128)S(1)}, u32[]{:S(2)}, u32[]{:S(2)}) collective-permute-start(f32[128,8,128]{2,1,0:T(8,128)S(1)} %slice.7), channel_id=1, source_target_pairs={{32,0},{64,96},{33,1},{65,97},{34,2},{66,98},{35,3},{67,99},{36,4}... | collective-permute-start | bytes 1572872 | tf_op jit(solution)/shard_map/ppermute | solution.py:630
  204.6 0.8 copy-start.2

commit v7 on v6

--- a/solution.py
+++ b/solution.py
@@ -31,6 +31,7 @@
 section_step = 0.25
 viscous_rate = 0.05
 vmem_bytes = 60 * 1024 * 1024
+finish_bytes = 24 * 1024 * 1024
 
 
 def halves(table):
@@ -456,9 +457,13 @@
             pltpu.SemaphoreType.DMA((ROWS_X,)),
             pltpu.SemaphoreType.DMA((BACK,)),
         ],
-        compiler_params=pltpu.CompilerParams(vmem_limit_bytes=vmem_bytes),
+        compiler_params=pltpu.CompilerParams(vmem_limit_bytes=finish_bytes),
         name="begin",
     )(back, more, jnp.asarray(table))
+
+
+def in_vmem(array):
+    return pltpu.with_memory_space_constraint(array, pltpu.VMEM)
 
 
 def finish_kernel(
@@ -469,25 +474,15 @@
     adjoint_ref,
     table_ref,
     out_ref,
-    got_ref,
-    mid_ref,
-    old_ref,
     new_ref,
     factor_ref,
     sems,
-    whole_sems,
 ):
     wide, narrow = lax.axis_index("wide"), lax.axis_index("narrow")
     is_light = light_narrow(narrow)
 
-    def load(k):
-        return pltpu.make_async_copy(adjoint_ref.at[:, :, k], old_ref.at[:, :, k], sems.at[0, k])
-
-    def fetch(k):
-        return pltpu.make_async_copy(part_ref.at[:, :, k], mid_ref.at[:, :, k], sems.at[2, k])
-
     def store(k):
-        return pltpu.make_async_copy(new_ref.at[:, :, k], out_ref.at[:, :, k], sems.at[1, k])
+        return pltpu.make_async_copy(new_ref.at[:, :, k], out_ref.at[:, :, k], sems.at[k])
 
     number_z = signed(lax.broadcasted_iota(jnp.int32, (1, NZ), 1), NZ)
     kz = 2.0 * math.pi / NZ * number_z.astype(jnp.float32)
@@ -528,48 +523,34 @@
         for part in range(2):
             along = (kx * conv[0][part] + ky * conv[1][part] + kz * conv[2][part]) * inverse
             for c in range(3):
-                new_ref[c, part, k, at, :] = decay * old_ref[c, part, k, at, :] + gain * (
+                new_ref[c, part, k, at, :] = decay * adjoint_ref[c, part, k, at, :] + gain * (
                     conv[c][part] - waves[c] * along
                 )
 
     @pl.when(jnp.logical_not(is_light))
     def _():
-        pieces = tile_copies(back1_ref, 0, 4, got_ref, 0, whole_sems)
-        pieces += tile_copies(more_ref, 0, 1, got_ref, 4, whole_sems)
-        for copy in pieces:
-            copy.start()
+        prepare()
         for k in range(ROWS_X):
-            fetch(k).start()
-            load(k).start()
-        prepare()
-        for copy in pieces:
-            copy.wait()
-        for k in range(ROWS_X):
-            fetch(k).wait()
             got = []
-            spans = spans_of([got_ref[f, :, k, :] for f in range(BACK)], table_ref[1])
+            spans = spans_of(
+                [back1_ref[:, f * ROWS_X + k, :] for f in range(4)] + [more_ref[:, k, :]],
+                table_ref[1],
+            )
             for f, span in enumerate(spans):
                 second = unite(span, slice(0, 64), slice(64, 128))
-                got.append(mirror((mid_ref[f, 0, k], mid_ref[f, 1, k]), second))
-            load(k).wait()
+                got.append(mirror((part_ref[f, 0, k], part_ref[f, 1, k]), second))
             emit(k, got, 0, ROWS_Y)
             store(k).start()
 
     @pl.when(is_light)
     def _():
-        pieces = tile_copies(back1_ref, 0, 3, got_ref, 0, whole_sems)
-        pieces += tile_copies(back0_ref, 2, 1, got_ref, 3, whole_sems)
-        for copy in pieces:
-            copy.start()
-        for k in range(ROWS_X):
-            load(k).start()
         prepare()
-        for copy in pieces:
-            copy.wait()
         for k in range(ROWS_X):
             by_plane = [
-                spans_of([got_ref[tile, :, k, :] for tile in tiles], table_ref[plane])
-                for plane, tiles in enumerate(((3, 0), (1, 2)))
+                spans_of([ref[:, tile * ROWS_X + k, :] for ref, tile in tiles], table_ref[plane])
+                for plane, tiles in enumerate(
+                    (((back0_ref, 2), (back1_ref, 0)), ((back1_ref, 1), (back1_ref, 2)))
+                )
             ]
 
             def item(index, plane):
@@ -587,10 +568,9 @@
                     for plane in range(2)
                 ]
                 got.append(mirror(*halves_of))
-            load(k).wait()
             for c in range(3):
                 for part in range(2):
-                    new_ref[c, part, k] = factor_ref[1, k] * old_ref[c, part, k]
+                    new_ref[c, part, k] = factor_ref[1, k] * adjoint_ref[c, part, k]
             start = pl.multiple_of(jnp.where(narrow == LIGHT[0], 0, LIGHT_ROW[1]), 8)
             emit(k, got, start, SLOT)
             store(k).start()
@@ -604,22 +584,17 @@
     block = (3, 2, ROWS_X, ROWS_Y, NZ)
     return pl.pallas_call(
         finish_kernel,
-        in_specs=[pl.BlockSpec(memory_space=pltpu.HBM)] * 5
-        + [pl.BlockSpec(memory_space=pltpu.VMEM)],
+        in_specs=[pl.BlockSpec(memory_space=pltpu.VMEM)] * 6,
         out_specs=pl.BlockSpec(memory_space=pltpu.HBM),
         out_shape=jax.ShapeDtypeStruct(block, jnp.float32),
         scratch_shapes=[
-            pltpu.VMEM((BACK, DEVICES, ROWS_X, 128), jnp.float32),
-            pltpu.VMEM((BACK, 2, ROWS_X, ROWS_Y, 128), jnp.float32),
-            pltpu.VMEM(block, jnp.float32),
             pltpu.VMEM(block, jnp.float32),
             pltpu.VMEM((3, ROWS_X, ROWS_Y, NZ), jnp.float32),
-            pltpu.SemaphoreType.DMA((3, ROWS_X)),
-            pltpu.SemaphoreType.DMA((BACK,)),
+            pltpu.SemaphoreType.DMA((ROWS_X,)),
         ],
-        compiler_params=pltpu.CompilerParams(vmem_limit_bytes=vmem_bytes),
+        compiler_params=pltpu.CompilerParams(vmem_limit_bytes=finish_bytes),
         name="finish",
-    )(*arrays, adjoint_hat, jnp.asarray(table))
+    )(*[in_vmem(array) for array in (*arrays, adjoint_hat)], jnp.asarray(table))
 
 
 def swap(chunks):

time: 217 us -> 215 us (level)
  Pallas kernels: 63.4 us -> 57.7 us
  local copies, waits for them, and re-layouts: 2.95 us -> 7.21 us
    pallas_call x1, Pallas kernels: 10.6 us -> 6.11 us  [finish(): pl.pallas_call(finish_kernel, in_specs=[pl.BlockSpec(memory_space=pltpu.V...]
    unnamed x6 -> x14, local copies, waits for them, and re-layouts: 1.8 us -> 6.06 us
where the time goes in v7:
time: 215 us; the launch traced here: 214 us
  waiting for transfers between devices  114 us (53%)
  Pallas kernels  57.7 us (27%)
  starting transfers between devices  35.4 us (16%)
  local copies, waits for them, and re-layouts  7.21 us (3%)
    all_to_all x4, waiting for transfers between devices, swap(): return lax.all_to_all(chunks, ('wide', 'narrow'), 0, 0, tiled=True)  108 us
    all_to_all x4, starting transfers between devices, swap(): return lax.all_to_all(chunks, ('wide', 'narrow'), 0, 0, tiled=True)  32.6 us
    pallas_call x2, Pallas kernels, run_plane(): pl.pallas_call(functools.partial(plane_kernel, plane), out_shape=out_shap...  29.1 us
    pallas_call x2, Pallas kernels, synth_z(): pl.pallas_call(functools.partial(synth_z_kernel, plane), in_specs=[pl.Blo...  17.6 us
    pallas_call x1, Pallas kernels, finish(): pl.pallas_call(finish_kernel, in_specs=[pl.BlockSpec(memory_space=pltpu.V...  6.11 us
    unnamed x14, local copies, waits for them, and re-layouts  6.06 us
    ppermute x2, waiting for transfers between devices, forward(): lax.ppermute(tiles, 'narrow', [(LIGHT[0], HEAVY[0]), (LIGHT[1], HEAVY[1])])  5.76 us
    pallas_call x1, Pallas kernels, begin(): pl.pallas_call(begin_kernel, in_specs=[pl.BlockSpec(memory_space=pltpu.HB...  4.87 us
  transfers between devices with their start and end apart: 6, of which 6 were waited for; matrix products, arithmetic and copies ran while one was open for 0% of the time, Pallas kernels for 20%

profile of v7, /device:TPU:0, one launch (start us, length us, event | category | flops | bytes accessed | tf_op | source)
XLA Modules:
  0.0 214.2 jit_solution(17391348028184132500)
XLA Ops:
  0.0 8.8 %synth_z.2 = f32[128,64,128]{2,1,0:T(8,128)} custom-call(f32[3,2,8,64,256]{4,3,2,1,0:T(8,128)} %adjoint_ref.5, f32[3,2,8,64,256]{4,3,2,1,0:T(8,128)} %velocity_ref.3, bf16[256,384]{1,0:T(8,128)(2,1)} %constant.14.clone.table_ref), custom_call_target="tpu_custom_call" | custom-call | tf_op jit(solution)/shard_map/synth_z/pallas_call | solution.py:191
  8.8 11.7 %all-to-all-start = ((f32[128,64,128]{2,1,0:T(8,128)}), f32[128,64,128]{2,1,0:T(8,128)}, u32[]{:S(2)}, u32[]{:S(2)}) async-start(f32[128,64,128]{2,1,0:T(8,128)} %synth_z.2), calls=%async_computation | async-start | bytes 8388608 | tf_op jit(solution)/shard_map/all_to_all | solution.py:601
  20.5 8.8 %synth_z.3 = f32[128,64,128]{2,1,0:T(8,128)} custom-call(f32[3,2,8,64,256]{4,3,2,1,0:T(8,128)} %adjoint_ref.5, f32[3,2,8,64,256]{4,3,2,1,0:T(8,128)} %velocity_ref.3, bf16[256,384]{1,0:T(8,128)(2,1)} %constant.15.clone.table_ref), custom_call_target="tpu_custom_call" | custom-call | tf_op jit(solution)/shard_map/synth_z/pallas_call | solution.py:191
  29.3 43.3 %all-to-all-done = f32[128,64,128]{2,1,0:T(8,128)} async-done(((f32[128,64,128]{2,1,0:T(8,128)}), f32[128,64,128]{2,1,0:T(8,128)}, u32[]{:S(2)}, u32[]{:S(2)}) %all-to-all-start) | async-done | bytes 4194336 | tf_op jit(solution)/shard_map/all_to_all | solution.py:601
  72.6 7.8 %all-to-all-start.2 = ((f32[128,64,128]{2,1,0:T(8,128)}), f32[128,64,128]{2,1,0:T(8,128)}, u32[]{:S(2)}, u32[]{:S(2)}) async-start(f32[128,64,128]{2,1,0:T(8,128)} %synth_z.3), calls=%async_computation.2 | async-start | bytes 8388608 | tf_op jit(solution)/shard_map/all_to_all | solution.py:601
  80.4 14.5 %plane.2 = (f32[32,4,24,128]{3,2,1,0:T(8,128)}, f32[32,2,8,128]{3,2,1,0:T(8,128)}) custom-call(f32[8192,128]{1,0:T(8,128)} %bitcast.got_ref, bf16[2,2,256,256]{3,2,1,0:T(8,128)(2,1)} %constant.16.clone.sy_ref, bf16[2,2,256,256]{3,2,1,0:T(8,128)(2,1)} %constant.17.clone.sx_ref, bf16[2,2,176,256]{3,2,1,0:T(8,128)(2,1)} %constant.18.clone.ax_ref, ...), custom_call_target="tpu_custom_call" | custom-call | tf_op jit(solution)/shard_map/plane/pallas_call | solution.py:370
  94.9 37.7 %all-to-all-done.2 = f32[128,64,128]{2,1,0:T(8,128)} async-done(((f32[128,64,128]{2,1,0:T(8,128)}), f32[128,64,128]{2,1,0:T(8,128)}, u32[]{:S(2)}, u32[]{:S(2)}) %all-to-all-start.2) | async-done | bytes 4194336 | tf_op jit(solution)/shard_map/all_to_all | solution.py:601
  132.5 7.2 %all-to-all-start.1 = ((f32[128,24,128]{2,1,0:T(8,128)}), f32[128,24,128]{2,1,0:T(8,128)S(1)}, u32[]{:S(2)}, u32[]{:S(2)}) async-start(f32[128,24,128]{2,1,0:T(8,128)} %bitcast.5), calls=%async_computation.1 | async-start | bytes 3145728 | tf_op jit(solution)/shard_map/all_to_all | solution.py:601
  139.8 14.7 %plane.3 = f32[32,4,32,128]{3,2,1,0:T(8,128)} custom-call(f32[8192,128]{1,0:T(8,128)} %bitcast.2.got_ref, bf16[2,2,256,256]{3,2,1,0:T(8,128)(2,1)} %constant.16.clone.sy_ref, bf16[2,2,256,256]{3,2,1,0:T(8,128)(2,1)} %constant.17.clone.sx_ref, bf16[2,2,176,256]{3,2,1,0:T(8,128)(2,1)} %constant.18.clone.ax_ref, ...), custom_call_target="tpu_custom_call" | custom-call | tf_op jit(solution)/shard_map/plane/pallas_call | solution.py:370
  154.4 9.8 %all-to-all-done.1.back_ref.back0_ref = f32[128,24,128]{2,1,0:T(8,128)S(1)} async-done(((f32[128,24,128]{2,1,0:T(8,128)}), f32[128,24,128]{2,1,0:T(8,128)S(1)}, u32[]{:S(2)}, u32[]{:S(2)}) %all-to-all-start.1) | async-done | bytes 1572896 | tf_op jit(solution)/shard_map/all_to_all | solution.py:601
  164.3 0.0 copy-start.1
  164.3 0.0 copy-start.6
  164.3 5.9 %all-to-all-start.3 = ((f32[128,32,128]{2,1,0:T(8,128)}), f32[128,32,128]{2,1,0:T(8,128)}, u32[]{:S(2)}, u32[]{:S(2)}) async-start(f32[128,32,128]{2,1,0:T(8,128)} %bitcast.4), calls=%async_computation.3 | async-start | bytes 4194304 | tf_op jit(solution)/shard_map/all_to_all | solution.py:601
  170.2 0.0 copy-done.1
  170.2 0.1 slice.8
  170.3 0.0 copy-start
  170.3 1.6 collective-permute-start
  171.9 3.3 %collective-permute-done.more_ref = f32[128,16,128]{2,1,0:T(8,128)S(1)} collective-permute-done((f32[128,16,128]{2,1,0:T(8,128)S(1)}, f32[128,16,128]{2,1,0:T(8,128)S(1)}, u32[]{:S(2)}, u32[]{:S(2)}) %collective-permute-start) | collective-permute-done | bytes 1048608 | tf_op jit(solution)/shard_map/ppermute | solution.py:605
  175.1 0.0 copy-done.6
  175.1 0.0 copy-start.2
  175.1 1.4 copy-done.2
  176.5 4.9 %begin.1.part_ref = f32[5,2,8,64,128]{4,3,2,1,0:T(8,128)S(1)} custom-call(f32[128,24,128]{2,1,0:T(8,128)S(1)} %copy-done.2, f32[128,16,128]{2,1,0:T(8,128)S(1)} %collective-permute-done.more_ref, bf16[2,384,256]{2,1,0:T(8,128)(2,1)S(1)} %copy-done.6), custom_call_target="tpu_custom_call" | custom-call | tf_op jit(solution)/shard_map/begin/pallas_call | solution.py:445
  181.4 0.0 copy-start.4
  181.4 1.5 copy-done.4
  182.9 17.0 %all-to-all-done.3.back1_ref = f32[128,32,128]{2,1,0:T(8,128)} async-done(((f32[128,32,128]{2,1,0:T(8,128)}), f32[128,32,128]{2,1,0:T(8,128)}, u32[]{:S(2)}, u32[]{:S(2)}) %all-to-all-start.3) | async-done | bytes 2097184 | tf_op jit(solution)/shard_map/all_to_all | solution.py:601
  199.9 1.1 slice.7
  201.0 1.3 collective-permute-start.1
  202.3 2.5 %collective-permute-done.1.more_ref = f32[128,8,128]{2,1,0:T(8,128)S(1)} collective-permute-done((f32[128,8,128]{2,1,0:T(8,128)S(1)}, f32[128,8,128]{2,1,0:T(8,128)S(1)}, u32[]{:S(2)}, u32[]{:S(2)}) %collective-permute-start.1) | collective-permute-done | bytes 524320 | tf_op jit(solution)/shard_map/ppermute | solution.py:605
  204.8 0.0 copy-done
  204.8 0.0 copy-start.3
  204.8 1.4 copy-done.3
  206.2 0.0 copy-start.5
  206.2 1.7 copy-done.5
  208.0 6.1 %finish.1 = f32[3,2,8,64,256]{4,3,2,1,0:T(8,128)} custom-call(f32[128,24,128]{2,1,0:T(8,128)S(1)} %copy-done.3, f32[128,32,128]{2,1,0:T(8,128)} %all-to-all-done.3.back1_ref, f32[128,8,128]{2,1,0:T(8,128)S(1)} %collective-permute-done.1.more_ref, f32[5,2,8,64,128]{4,3,2,1,0:T(8,128)S(1)} %copy-done.5, f32[3,2,8,64,256]{4,3,2,1,0:T(8,128)S(1)} %copy-done, ...), custom_call_target="tpu_custom_call" | custom-call | tf_op jit(solution)/shard_map/finish/pallas_call | solution.py:585
Async XLA Ops:
  8.8 63.8 %all-to-all-start = ((f32[128,64,128]{2,1,0:T(8,128)}), f32[128,64,128]{2,1,0:T(8,128)}, u32[]{:S(2)}, u32[]{:S(2)}) async-start(f32[128,64,128]{2,1,0:T(8,128)} %synth_z.2), calls=%async_computation | async-start | bytes 8388608 | tf_op jit(solution)/shard_map/all_to_all | solution.py:601
  72.6 59.9 %all-to-all-start.2 = ((f32[128,64,128]{2,1,0:T(8,128)}), f32[128,64,128]{2,1,0:T(8,128)}, u32[]{:S(2)}, u32[]{:S(2)}) async-start(f32[128,64,128]{2,1,0:T(8,128)} %synth_z.3), calls=%async_computation.2 | async-start | bytes 8388608 | tf_op jit(solution)/shard_map/all_to_all | solution.py:601
  132.5 31.7 %all-to-all-start.1 = ((f32[128,24,128]{2,1,0:T(8,128)}), f32[128,24,128]{2,1,0:T(8,128)S(1)}, u32[]{:S(2)}, u32[]{:S(2)}) async-start(f32[128,24,128]{2,1,0:T(8,128)} %bitcast.5), calls=%async_computation.1 | async-start | bytes 3145728 | tf_op jit(solution)/shard_map/all_to_all | solution.py:601
  164.3 5.9 %copy-start.1 = (f32[128,24,128]{2,1,0:T(8,128)}, f32[128,24,128]{2,1,0:T(8,128)S(1)}, u32[]{:S(2)}) copy-start(f32[128,24,128]{2,1,0:T(8,128)S(1)} %all-to-all-done.1.back_ref.back0_ref) | copy-start | bytes 4718596
  164.3 10.8 %copy-start.6 = (bf16[2,384,256]{2,1,0:T(8,128)(2,1)S(1)}, bf16[2,384,256]{2,1,0:T(8,128)(2,1)}, u32[]{:S(2)}) copy-start(bf16[2,384,256]{2,1,0:T(8,128)(2,1)} %constant.20.clone.table_ref) | copy-start | bytes 1179652
  164.3 35.7 %all-to-all-start.3 = ((f32[128,32,128]{2,1,0:T(8,128)}), f32[128,32,128]{2,1,0:T(8,128)}, u32[]{:S(2)}, u32[]{:S(2)}) async-start(f32[128,32,128]{2,1,0:T(8,128)} %bitcast.4), calls=%async_computation.3 | async-start | bytes 4194304 | tf_op jit(solution)/shard_map/all_to_all | solution.py:601
  170.3 34.5 %copy-start = (f32[3,2,8,64,256]{4,3,2,1,0:T(8,128)S(1)}, f32[3,2,8,64,256]{4,3,2,1,0:T(8,128)}, u32[]{:S(2)}) copy-start(f32[3,2,8,64,256]{4,3,2,1,0:T(8,128)} %adjoint_ref.5) | copy-start | bytes 9437188
  170.3 4.8 %collective-permute-start = (f32[128,16,128]{2,1,0:T(8,128)S(1)}, f32[128,16,128]{2,1,0:T(8,128)S(1)}, u32[]{:S(2)}, u32[]{:S(2)}) collective-permute-start(f32[128,16,128]{2,1,0:T(8,128)S(1)} %slice.8), channel_id=1, source_target_pairs={{32,0},{64,96},{33,1},{65,97},{34,2},{66,98},{35,3},{67,99},{36,4}... | collective-permute-start | bytes 3145736 | tf_op jit(solution)/shard_map/ppermute | solution.py:605
  175.1 1.4 copy-start.2
  181.4 1.5 copy-start.4
  201.0 3.8 %collective-permute-start.1 = (f32[128,8,128]{2,1,0:T(8,128)S(1)}, f32[128,8,128]{2,1,0:T(8,128)S(1)}, u32[]{:S(2)}, u32[]{:S(2)}) collective-permute-start(f32[128,8,128]{2,1,0:T(8,128)S(1)} %slice.7), channel_id=1, source_target_pairs={{32,0},{64,96},{33,1},{65,97},{34,2},{66,98},{35,3},{67,99},{36,4}... | collective-permute-start | bytes 1572872 | tf_op jit(solution)/shard_map/ppermute | solution.py:605
  204.8 1.4 copy-start.3
  206.2 1.7 copy-start.5

commit v8 on v7

--- a/solution.py
+++ b/solution.py
@@ -158,8 +158,10 @@
     for k in range(ROWS_X):
         number_x = lax.axis_index("wide") * ROWS_X + k
         kx = 2.0 * math.pi / NX * number_x.astype(jnp.float32)
-        for which in range(2):
-            load(k, which).wait()
+        if k % 4 == 0:
+            for near in range(k, k + 4):
+                for which in range(2):
+                    load(near, which).wait()
         vel = [[vel_ref[c, part, k] for part in range(2)] for c in range(3)]
         fields = [(adj_ref[c, 0, k], adj_ref[c, 1, k]) for c in range(3)]
         fields += [(vel[c][0], vel[c][1]) for c in range(3)]
@@ -462,6 +464,10 @@
     )(back, more, jnp.asarray(table))
 
 
+def in_hbm(array):
+    return pltpu.with_memory_space_constraint(array, pltpu.HBM)
+
+
 def in_vmem(array):
     return pltpu.with_memory_space_constraint(array, pltpu.VMEM)
 
@@ -476,10 +482,20 @@
     out_ref,
     new_ref,
     factor_ref,
+    mid_ref,
+    tile_ref,
     sems,
+    mid_sems,
 ):
     wide, narrow = lax.axis_index("wide"), lax.axis_index("narrow")
     is_light = light_narrow(narrow)
+
+    def fetch(k):
+        return pltpu.make_async_copy(part_ref.at[:, :, k], mid_ref.at[:, :, k], mid_sems.at[k])
+
+    tile_copy = pltpu.make_async_copy(
+        back0_ref.at[:, pl.ds(2 * ROWS_X, ROWS_X)], tile_ref, mid_sems.at[0]
+    )
 
     def store(k):
         return pltpu.make_async_copy(new_ref.at[:, :, k], out_ref.at[:, :, k], sems.at[k])
@@ -529,6 +545,8 @@
 
     @pl.when(jnp.logical_not(is_light))
     def _():
+        for k in range(ROWS_X):
+            fetch(k).start()
         prepare()
         for k in range(ROWS_X):
             got = []
@@ -536,20 +554,23 @@
                 [back1_ref[:, f * ROWS_X + k, :] for f in range(4)] + [more_ref[:, k, :]],
                 table_ref[1],
             )
+            fetch(k).wait()
             for f, span in enumerate(spans):
                 second = unite(span, slice(0, 64), slice(64, 128))
-                got.append(mirror((part_ref[f, 0, k], part_ref[f, 1, k]), second))
+                got.append(mirror((mid_ref[f, 0, k], mid_ref[f, 1, k]), second))
             emit(k, got, 0, ROWS_Y)
             store(k).start()
 
     @pl.when(is_light)
     def _():
+        tile_copy.start()
         prepare()
+        tile_copy.wait()
         for k in range(ROWS_X):
             by_plane = [
                 spans_of([ref[:, tile * ROWS_X + k, :] for ref, tile in tiles], table_ref[plane])
                 for plane, tiles in enumerate(
-                    (((back0_ref, 2), (back1_ref, 0)), ((back1_ref, 1), (back1_ref, 2)))
+                    (((tile_ref, 0), (back1_ref, 0)), ((back1_ref, 1), (back1_ref, 2)))
                 )
             ]
 
@@ -579,22 +600,39 @@
         store(k).wait()
 
 
-def finish(arrays, adjoint_hat):
+def finish(back0, back1, more, part, adjoint_hat):
     table = tables_anal_z()
     block = (3, 2, ROWS_X, ROWS_Y, NZ)
     return pl.pallas_call(
         finish_kernel,
-        in_specs=[pl.BlockSpec(memory_space=pltpu.VMEM)] * 6,
+        in_specs=[
+            pl.BlockSpec(memory_space=pltpu.HBM),
+            pl.BlockSpec(memory_space=pltpu.VMEM),
+            pl.BlockSpec(memory_space=pltpu.VMEM),
+            pl.BlockSpec(memory_space=pltpu.HBM),
+            pl.BlockSpec(memory_space=pltpu.VMEM),
+            pl.BlockSpec(memory_space=pltpu.VMEM),
+        ],
         out_specs=pl.BlockSpec(memory_space=pltpu.HBM),
         out_shape=jax.ShapeDtypeStruct(block, jnp.float32),
         scratch_shapes=[
             pltpu.VMEM(block, jnp.float32),
             pltpu.VMEM((3, ROWS_X, ROWS_Y, NZ), jnp.float32),
+            pltpu.VMEM((BACK, 2, ROWS_X, ROWS_Y, 128), jnp.float32),
+            pltpu.VMEM((DEVICES, ROWS_X, 128), jnp.float32),
+            pltpu.SemaphoreType.DMA((ROWS_X,)),
             pltpu.SemaphoreType.DMA((ROWS_X,)),
         ],
         compiler_params=pltpu.CompilerParams(vmem_limit_bytes=finish_bytes),
         name="finish",
-    )(*[in_vmem(array) for array in (*arrays, adjoint_hat)], jnp.asarray(table))
+    )(
+        in_hbm(back0),
+        in_vmem(back1),
+        in_vmem(more),
+        in_hbm(part),
+        in_vmem(adjoint_hat),
+        jnp.asarray(table),
+    )
 
 
 def swap(chunks):
@@ -615,7 +653,7 @@
     part = begin(back0, more0)
     back1, part = lax.optimization_barrier((back1, part))
     more1 = forward(back1[:, 3 * ROWS_X :])
-    return finish([back0, back1, more1, part], adjoint_hat)
+    return finish(back0, back1, more1, part, adjoint_hat)
 
 
 def solution(mesh):

time: 215 us -> 214 us (level)
  local copies, waits for them, and re-layouts: 7.21 us -> 4.06 us
    pallas_call x1, Pallas kernels: 6.11 us -> 9.46 us  [finish(): pl.pallas_call(finish_kernel, in_specs=[pl.BlockSpec(memory_space=pltpu.H...]
    unnamed x14 -> x10, local copies, waits for them, and re-layouts: 6.06 us -> 2.91 us
where the time goes in v8:
time: 214 us
  waiting for transfers between devices  114 us (53%)
  Pallas kernels  59.8 us (28%)
  starting transfers between devices  35.6 us (17%)
  local copies, waits for them, and re-layouts  4.06 us (2%)
    all_to_all x4, waiting for transfers between devices, swap(): return lax.all_to_all(chunks, ('wide', 'narrow'), 0, 0, tiled=True)  108 us
    all_to_all x4, starting transfers between devices, swap(): return lax.all_to_all(chunks, ('wide', 'narrow'), 0, 0, tiled=True)  32.8 us
    pallas_call x2, Pallas kernels, run_plane(): pl.pallas_call(functools.partial(plane_kernel, plane), out_shape=out_shap...  29.1 us
    pallas_call x2, Pallas kernels, synth_z(): pl.pallas_call(functools.partial(synth_z_kernel, plane), in_specs=[pl.Blo...  16.3 us
    pallas_call x1, Pallas kernels, finish(): pl.pallas_call(finish_kernel, in_specs=[pl.BlockSpec(memory_space=pltpu.H...  9.46 us
    ppermute x2, waiting for transfers between devices, forward(): lax.ppermute(tiles, 'narrow', [(LIGHT[0], HEAVY[0]), (LIGHT[1], HEAVY[1])])  5.76 us
    pallas_call x1, Pallas kernels, begin(): pl.pallas_call(begin_kernel, in_specs=[pl.BlockSpec(memory_space=pltpu.HB...  4.87 us
  transfers between devices with their start and end apart: 6, of which 6 were waited for; matrix products, arithmetic and copies ran while one was open for 0% of the time, Pallas kernels for 20%

profile of v8, /device:TPU:0, one launch (start us, length us, event | category | flops | bytes accessed | tf_op | source)
XLA Modules:
  0.0 213.8 jit_solution(13210374027488324538)
XLA Ops:
  0.0 8.1 %synth_z.2 = f32[128,64,128]{2,1,0:T(8,128)} custom-call(f32[3,2,8,64,256]{4,3,2,1,0:T(8,128)} %adjoint_ref.5, f32[3,2,8,64,256]{4,3,2,1,0:T(8,128)} %velocity_ref.3, bf16[256,384]{1,0:T(8,128)(2,1)} %constant.14.clone.table_ref), custom_call_target="tpu_custom_call" | custom-call | tf_op jit(solution)/shard_map/synth_z/pallas_call | solution.py:193
  8.1 11.7 %all-to-all-start = ((f32[128,64,128]{2,1,0:T(8,128)}), f32[128,64,128]{2,1,0:T(8,128)}, u32[]{:S(2)}, u32[]{:S(2)}) async-start(f32[128,64,128]{2,1,0:T(8,128)} %synth_z.2), calls=%async_computation | async-start | bytes 8388608 | tf_op jit(solution)/shard_map/all_to_all | solution.py:639
  19.8 8.2 %synth_z.3 = f32[128,64,128]{2,1,0:T(8,128)} custom-call(f32[3,2,8,64,256]{4,3,2,1,0:T(8,128)} %adjoint_ref.5, f32[3,2,8,64,256]{4,3,2,1,0:T(8,128)} %velocity_ref.3, bf16[256,384]{1,0:T(8,128)(2,1)} %constant.15.clone.table_ref), custom_call_target="tpu_custom_call" | custom-call | tf_op jit(solution)/shard_map/synth_z/pallas_call | solution.py:193
  28.0 43.9 %all-to-all-done = f32[128,64,128]{2,1,0:T(8,128)} async-done(((f32[128,64,128]{2,1,0:T(8,128)}), f32[128,64,128]{2,1,0:T(8,128)}, u32[]{:S(2)}, u32[]{:S(2)}) %all-to-all-start) | async-done | bytes 4194336 | tf_op jit(solution)/shard_map/all_to_all | solution.py:639
  71.9 7.9 %all-to-all-start.2 = ((f32[128,64,128]{2,1,0:T(8,128)}), f32[128,64,128]{2,1,0:T(8,128)}, u32[]{:S(2)}, u32[]{:S(2)}) async-start(f32[128,64,128]{2,1,0:T(8,128)} %synth_z.3), calls=%async_computation.2 | async-start | bytes 8388608 | tf_op jit(solution)/shard_map/all_to_all | solution.py:639
  79.9 14.5 %plane.2 = (f32[32,4,24,128]{3,2,1,0:T(8,128)}, f32[32,2,8,128]{3,2,1,0:T(8,128)}) custom-call(f32[8192,128]{1,0:T(8,128)} %bitcast.got_ref, bf16[2,2,256,256]{3,2,1,0:T(8,128)(2,1)} %constant.16.clone.sy_ref, bf16[2,2,256,256]{3,2,1,0:T(8,128)(2,1)} %constant.17.clone.sx_ref, bf16[2,2,176,256]{3,2,1,0:T(8,128)(2,1)} %constant.18.clone.ax_ref, ...), custom_call_target="tpu_custom_call" | custom-call | tf_op jit(solution)/shard_map/plane/pallas_call | solution.py:372
  94.4 37.4 %all-to-all-done.2 = f32[128,64,128]{2,1,0:T(8,128)} async-done(((f32[128,64,128]{2,1,0:T(8,128)}), f32[128,64,128]{2,1,0:T(8,128)}, u32[]{:S(2)}, u32[]{:S(2)}) %all-to-all-start.2) | async-done | bytes 4194336 | tf_op jit(solution)/shard_map/all_to_all | solution.py:639
  131.8 7.2 %all-to-all-start.1 = ((f32[128,24,128]{2,1,0:T(8,128)}), f32[128,24,128]{2,1,0:T(8,128)S(1)}, u32[]{:S(2)}, u32[]{:S(2)}) async-start(f32[128,24,128]{2,1,0:T(8,128)} %bitcast.5), calls=%async_computation.1 | async-start | bytes 3145728 | tf_op jit(solution)/shard_map/all_to_all | solution.py:639
  139.1 14.6 %plane.3 = f32[32,4,32,128]{3,2,1,0:T(8,128)} custom-call(f32[8192,128]{1,0:T(8,128)} %bitcast.2.got_ref, bf16[2,2,256,256]{3,2,1,0:T(8,128)(2,1)} %constant.16.clone.sy_ref, bf16[2,2,256,256]{3,2,1,0:T(8,128)(2,1)} %constant.17.clone.sx_ref, bf16[2,2,176,256]{3,2,1,0:T(8,128)(2,1)} %constant.18.clone.ax_ref, ...), custom_call_target="tpu_custom_call" | custom-call | tf_op jit(solution)/shard_map/plane/pallas_call | solution.py:372
  153.7 9.8 %all-to-all-done.1.back_ref.back0_ref = f32[128,24,128]{2,1,0:T(8,128)S(1)} async-done(((f32[128,24,128]{2,1,0:T(8,128)}), f32[128,24,128]{2,1,0:T(8,128)S(1)}, u32[]{:S(2)}, u32[]{:S(2)}) %all-to-all-start.1) | async-done | bytes 1572896 | tf_op jit(solution)/shard_map/all_to_all | solution.py:639
  163.6 0.0 copy-start.1
  163.6 0.0 copy-start.4
  163.6 5.9 %all-to-all-start.3 = ((f32[128,32,128]{2,1,0:T(8,128)}), f32[128,32,128]{2,1,0:T(8,128)}, u32[]{:S(2)}, u32[]{:S(2)}) async-start(f32[128,32,128]{2,1,0:T(8,128)} %bitcast.4), calls=%async_computation.3 | async-start | bytes 4194304 | tf_op jit(solution)/shard_map/all_to_all | solution.py:639
  169.5 0.0 copy-done.1
  169.5 0.1 slice.8
  169.6 0.0 copy-start
  169.6 1.6 collective-permute-start
  171.2 3.3 %collective-permute-done.more_ref = f32[128,16,128]{2,1,0:T(8,128)S(1)} collective-permute-done((f32[128,16,128]{2,1,0:T(8,128)S(1)}, f32[128,16,128]{2,1,0:T(8,128)S(1)}, u32[]{:S(2)}, u32[]{:S(2)}) %collective-permute-start) | collective-permute-done | bytes 1048608 | tf_op jit(solution)/shard_map/ppermute | solution.py:643
  174.4 0.0 copy-done.4
  174.4 0.0 copy-start.2
  174.4 1.4 copy-done.2
  175.8 4.9 %begin.1.part_ref = f32[5,2,8,64,128]{4,3,2,1,0:T(8,128)S(1)} custom-call(f32[128,24,128]{2,1,0:T(8,128)S(1)} %copy-done.2, f32[128,16,128]{2,1,0:T(8,128)S(1)} %collective-permute-done.more_ref, bf16[2,384,256]{2,1,0:T(8,128)(2,1)S(1)} %copy-done.4), custom_call_target="tpu_custom_call" | custom-call | tf_op jit(solution)/shard_map/begin/pallas_call | solution.py:447
  180.7 0.0 copy-start.3
  180.7 1.5 copy-done.3
  182.2 17.0 %all-to-all-done.3.back1_ref = f32[128,32,128]{2,1,0:T(8,128)} async-done(((f32[128,32,128]{2,1,0:T(8,128)}), f32[128,32,128]{2,1,0:T(8,128)}, u32[]{:S(2)}, u32[]{:S(2)}) %all-to-all-start.3) | async-done | bytes 2097184 | tf_op jit(solution)/shard_map/all_to_all | solution.py:639
  199.2 1.1 slice.7
  200.3 1.3 collective-permute-start.1
  201.6 2.5 %collective-permute-done.1.more_ref = f32[128,8,128]{2,1,0:T(8,128)S(1)} collective-permute-done((f32[128,8,128]{2,1,0:T(8,128)S(1)}, f32[128,8,128]{2,1,0:T(8,128)S(1)}, u32[]{:S(2)}, u32[]{:S(2)}) %collective-permute-start.1) | collective-permute-done | bytes 524320 | tf_op jit(solution)/shard_map/ppermute | solution.py:643
  204.1 0.0 copy-done
  204.1 9.5 %finish.1 = f32[3,2,8,64,256]{4,3,2,1,0:T(8,128)} custom-call(f32[128,24,128]{2,1,0:T(8,128)} %copy-done.1, f32[128,32,128]{2,1,0:T(8,128)} %all-to-all-done.3.back1_ref, f32[128,8,128]{2,1,0:T(8,128)S(1)} %collective-permute-done.1.more_ref, f32[5,2,8,64,128]{4,3,2,1,0:T(8,128)} %copy-done.3, f32[3,2,8,64,256]{4,3,2,1,0:T(8,128)S(1)} %copy-done, ...), custom_call_target="tpu_custom_call" | custom-call | tf_op jit(solution)/shard_map/finish/pallas_call | solution.py:606
Async XLA Ops:
  8.1 63.8 %all-to-all-start = ((f32[128,64,128]{2,1,0:T(8,128)}), f32[128,64,128]{2,1,0:T(8,128)}, u32[]{:S(2)}, u32[]{:S(2)}) async-start(f32[128,64,128]{2,1,0:T(8,128)} %synth_z.2), calls=%async_computation | async-start | bytes 8388608 | tf_op jit(solution)/shard_map/all_to_all | solution.py:639
  71.9 59.9 %all-to-all-start.2 = ((f32[128,64,128]{2,1,0:T(8,128)}), f32[128,64,128]{2,1,0:T(8,128)}, u32[]{:S(2)}, u32[]{:S(2)}) async-start(f32[128,64,128]{2,1,0:T(8,128)} %synth_z.3), calls=%async_computation.2 | async-start | bytes 8388608 | tf_op jit(solution)/shard_map/all_to_all | solution.py:639
  131.8 31.7 %all-to-all-start.1 = ((f32[128,24,128]{2,1,0:T(8,128)}), f32[128,24,128]{2,1,0:T(8,128)S(1)}, u32[]{:S(2)}, u32[]{:S(2)}) async-start(f32[128,24,128]{2,1,0:T(8,128)} %bitcast.5), calls=%async_computation.1 | async-start | bytes 3145728 | tf_op jit(solution)/shard_map/all_to_all | solution.py:639
  163.6 5.9 %copy-start.1 = (f32[128,24,128]{2,1,0:T(8,128)}, f32[128,24,128]{2,1,0:T(8,128)S(1)}, u32[]{:S(2)}) copy-start(f32[128,24,128]{2,1,0:T(8,128)S(1)} %all-to-all-done.1.back_ref.back0_ref) | copy-start | bytes 4718596
  163.6 10.9 %copy-start.4 = (bf16[2,384,256]{2,1,0:T(8,128)(2,1)S(1)}, bf16[2,384,256]{2,1,0:T(8,128)(2,1)}, u32[]{:S(2)}) copy-start(bf16[2,384,256]{2,1,0:T(8,128)(2,1)} %constant.20.clone.table_ref) | copy-start | bytes 1179652
  163.6 35.7 %all-to-all-start.3 = ((f32[128,32,128]{2,1,0:T(8,128)}), f32[128,32,128]{2,1,0:T(8,128)}, u32[]{:S(2)}, u32[]{:S(2)}) async-start(f32[128,32,128]{2,1,0:T(8,128)} %bitcast.4), calls=%async_computation.3 | async-start | bytes 4194304 | tf_op jit(solution)/shard_map/all_to_all | solution.py:639
  169.6 34.5 %copy-start = (f32[3,2,8,64,256]{4,3,2,1,0:T(8,128)S(1)}, f32[3,2,8,64,256]{4,3,2,1,0:T(8,128)}, u32[]{:S(2)}) copy-start(f32[3,2,8,64,256]{4,3,2,1,0:T(8,128)} %adjoint_ref.5) | copy-start | bytes 9437188
  169.6 4.8 %collective-permute-start = (f32[128,16,128]{2,1,0:T(8,128)S(1)}, f32[128,16,128]{2,1,0:T(8,128)S(1)}, u32[]{:S(2)}, u32[]{:S(2)}) collective-permute-start(f32[128,16,128]{2,1,0:T(8,128)S(1)} %slice.8), channel_id=1, source_target_pairs={{32,0},{64,96},{33,1},{65,97},{34,2},{66,98},{35,3},{67,99},{36,4}... | collective-permute-start | bytes 3145736 | tf_op jit(solution)/shard_map/ppermute | solution.py:643
  174.4 1.4 copy-start.2
  180.7 1.5 copy-start.3
  200.3 3.8 %collective-permute-start.1 = (f32[128,8,128]{2,1,0:T(8,128)S(1)}, f32[128,8,128]{2,1,0:T(8,128)S(1)}, u32[]{:S(2)}, u32[]{:S(2)}) collective-permute-start(f32[128,8,128]{2,1,0:T(8,128)S(1)} %slice.7), channel_id=1, source_target_pairs={{32,0},{64,96},{33,1},{65,97},{34,2},{66,98},{35,3},{67,99},{36,4}... | collective-permute-start | bytes 1572872 | tf_op jit(solution)/shard_map/ppermute | solution.py:643

commit v9 on v8

--- a/solution.py
+++ b/solution.py
@@ -420,7 +420,7 @@
     back_ref, more_ref, table_ref, part_ref, got_ref, new_ref, sems, whole_sems
 ):
     def store(k):
-        return pltpu.make_async_copy(new_ref.at[:, :, k], part_ref.at[:, :, k], sems.at[k])
+        return pltpu.make_async_copy(new_ref.at[k], part_ref.at[k], sems.at[k])
 
     @pl.when(jnp.logical_not(light_narrow(lax.axis_index("narrow"))))
     def _():
@@ -434,8 +434,8 @@
             spans = spans_of([got_ref[f, :, k, :] for f in range(BACK)], table_ref[0])
             for f, span in enumerate(spans):
                 real, imag = unite(span, slice(0, 64), slice(64, 128))
-                new_ref[f, 0, k] = real
-                new_ref[f, 1, k] = imag
+                new_ref[k, f, 0] = real
+                new_ref[k, f, 1] = imag
             store(k).start()
         for k in range(ROWS_X):
             store(k).wait()
@@ -443,7 +443,7 @@
 
 def begin(back, more):
     table = tables_anal_z()
-    block = (BACK, 2, ROWS_X, ROWS_Y, 128)
+    block = (ROWS_X, BACK, 2, ROWS_Y, 128)
     return pl.pallas_call(
         begin_kernel,
         in_specs=[
@@ -484,14 +484,16 @@
     factor_ref,
     mid_ref,
     tile_ref,
+    got_ref,
     sems,
     mid_sems,
+    tile_sems,
 ):
     wide, narrow = lax.axis_index("wide"), lax.axis_index("narrow")
     is_light = light_narrow(narrow)
 
     def fetch(k):
-        return pltpu.make_async_copy(part_ref.at[:, :, k], mid_ref.at[:, :, k], mid_sems.at[k])
+        return pltpu.make_async_copy(part_ref.at[k], mid_ref.at[k], mid_sems.at[k])
 
     tile_copy = pltpu.make_async_copy(
         back0_ref.at[:, pl.ds(2 * ROWS_X, ROWS_X)], tile_ref, mid_sems.at[0]
@@ -545,32 +547,43 @@
 
     @pl.when(jnp.logical_not(is_light))
     def _():
+        pieces = tile_copies(back1_ref, 0, 4, got_ref, 0, tile_sems)
+        for copy in pieces:
+            copy.start()
         for k in range(ROWS_X):
             fetch(k).start()
         prepare()
+        for copy in pieces:
+            copy.wait()
         for k in range(ROWS_X):
             got = []
             spans = spans_of(
-                [back1_ref[:, f * ROWS_X + k, :] for f in range(4)] + [more_ref[:, k, :]],
+                [got_ref[f, :, k, :] for f in range(4)] + [more_ref[:, k, :]],
                 table_ref[1],
             )
             fetch(k).wait()
             for f, span in enumerate(spans):
                 second = unite(span, slice(0, 64), slice(64, 128))
-                got.append(mirror((mid_ref[f, 0, k], mid_ref[f, 1, k]), second))
+                got.append(mirror((mid_ref[k, f, 0], mid_ref[k, f, 1]), second))
             emit(k, got, 0, ROWS_Y)
             store(k).start()
 
     @pl.when(is_light)
     def _():
-        tile_copy.start()
+        pieces = tile_copies(back1_ref, 0, 3, got_ref, 0, tile_sems) + [tile_copy]
+        for copy in pieces:
+            copy.start()
         prepare()
-        tile_copy.wait()
+        for copy in pieces:
+            copy.wait()
         for k in range(ROWS_X):
             by_plane = [
-                spans_of([ref[:, tile * ROWS_X + k, :] for ref, tile in tiles], table_ref[plane])
-                for plane, tiles in enumerate(
-                    (((tile_ref, 0), (back1_ref, 0)), ((back1_ref, 1), (back1_ref, 2)))
+                spans_of(rows, table_ref[plane])
+                for plane, rows in enumerate(
+                    (
+                        (tile_ref[:, k, :], got_ref[0, :, k, :]),
+                        (got_ref[1, :, k, :], got_ref[2, :, k, :]),
+                    )
                 )
             ]
 
@@ -607,7 +620,7 @@
         finish_kernel,
         in_specs=[
             pl.BlockSpec(memory_space=pltpu.HBM),
-            pl.BlockSpec(memory_space=pltpu.VMEM),
+            pl.BlockSpec(memory_space=pltpu.HBM),
             pl.BlockSpec(memory_space=pltpu.VMEM),
             pl.BlockSpec(memory_space=pltpu.HBM),
             pl.BlockSpec(memory_space=pltpu.VMEM),
@@ -618,16 +631,18 @@
         scratch_shapes=[
             pltpu.VMEM(block, jnp.float32),
             pltpu.VMEM((3, ROWS_X, ROWS_Y, NZ), jnp.float32),
-            pltpu.VMEM((BACK, 2, ROWS_X, ROWS_Y, 128), jnp.float32),
+            pltpu.VMEM((ROWS_X, BACK, 2, ROWS_Y, 128), jnp.float32),
             pltpu.VMEM((DEVICES, ROWS_X, 128), jnp.float32),
+            pltpu.VMEM((4, DEVICES, ROWS_X, 128), jnp.float32),
             pltpu.SemaphoreType.DMA((ROWS_X,)),
             pltpu.SemaphoreType.DMA((ROWS_X,)),
+            pltpu.SemaphoreType.DMA((4,)),
         ],
         compiler_params=pltpu.CompilerParams(vmem_limit_bytes=finish_bytes),
         name="finish",
     )(
         in_hbm(back0),
-        in_vmem(back1),
+        in_hbm(back1),
         in_vmem(more),
         in_hbm(part),
         in_vmem(adjoint_hat),

time: 214 us -> 213 us (level)
  no operation moved by 1% of the time
where the time goes in v9:
time: 213 us
  waiting for transfers between devices  113 us (53%)
  Pallas kernels  59.4 us (28%)
  starting transfers between devices  35.6 us (17%)
  local copies, waits for them, and re-layouts  4.06 us (2%)
    all_to_all x4, waiting for transfers between devices, swap(): return lax.all_to_all(chunks, ('wide', 'narrow'), 0, 0, tiled=True)  108 us
    all_to_all x4, starting transfers between devices, swap(): return lax.all_to_all(chunks, ('wide', 'narrow'), 0, 0, tiled=True)  32.8 us
    pallas_call x2, Pallas kernels, run_plane(): pl.pallas_call(functools.partial(plane_kernel, plane), out_shape=out_shap...  29.1 us
    pallas_call x2, Pallas kernels, synth_z(): pl.pallas_call(functools.partial(synth_z_kernel, plane), in_specs=[pl.Blo...  16.3 us
    pallas_call x1, Pallas kernels, finish(): pl.pallas_call(finish_kernel, in_specs=[pl.BlockSpec(memory_space=pltpu.H...  8.45 us
    ppermute x2, waiting for transfers between devices, forward(): lax.ppermute(tiles, 'narrow', [(LIGHT[0], HEAVY[0]), (LIGHT[1], HEAVY[1])])  5.76 us
    pallas_call x1, Pallas kernels, begin(): pl.pallas_call(begin_kernel, in_specs=[pl.BlockSpec(memory_space=pltpu.HB...  5.47 us
  transfers between devices with their start and end apart: 6, of which 6 were waited for; matrix products, arithmetic and copies ran while one was open for 0% of the time, Pallas kernels for 20%

profile of v9, /device:TPU:0, one launch (start us, length us, event | category | flops | bytes accessed | tf_op | source)
XLA Modules:
  0.0 212.7 jit_solution(10242021684673502123)
XLA Ops:
  0.0 8.1 %synth_z.2 = f32[128,64,128]{2,1,0:T(8,128)} custom-call(f32[3,2,8,64,256]{4,3,2,1,0:T(8,128)} %adjoint_ref.5, f32[3,2,8,64,256]{4,3,2,1,0:T(8,128)} %velocity_ref.3, bf16[256,384]{1,0:T(8,128)(2,1)} %constant.14.clone.table_ref), custom_call_target="tpu_custom_call" | custom-call | tf_op jit(solution)/shard_map/synth_z/pallas_call | solution.py:193
  8.1 11.7 %all-to-all-start = ((f32[128,64,128]{2,1,0:T(8,128)}), f32[128,64,128]{2,1,0:T(8,128)}, u32[]{:S(2)}, u32[]{:S(2)}) async-start(f32[128,64,128]{2,1,0:T(8,128)} %synth_z.2), calls=%async_computation | async-start | bytes 8388608 | tf_op jit(solution)/shard_map/all_to_all | solution.py:654
  19.8 8.2 %synth_z.3 = f32[128,64,128]{2,1,0:T(8,128)} custom-call(f32[3,2,8,64,256]{4,3,2,1,0:T(8,128)} %adjoint_ref.5, f32[3,2,8,64,256]{4,3,2,1,0:T(8,128)} %velocity_ref.3, bf16[256,384]{1,0:T(8,128)(2,1)} %constant.15.clone.table_ref), custom_call_target="tpu_custom_call" | custom-call | tf_op jit(solution)/shard_map/synth_z/pallas_call | solution.py:193
  28.0 43.9 %all-to-all-done = f32[128,64,128]{2,1,0:T(8,128)} async-done(((f32[128,64,128]{2,1,0:T(8,128)}), f32[128,64,128]{2,1,0:T(8,128)}, u32[]{:S(2)}, u32[]{:S(2)}) %all-to-all-start) | async-done | bytes 4194336 | tf_op jit(solution)/shard_map/all_to_all | solution.py:654
  71.9 7.9 %all-to-all-start.2 = ((f32[128,64,128]{2,1,0:T(8,128)}), f32[128,64,128]{2,1,0:T(8,128)}, u32[]{:S(2)}, u32[]{:S(2)}) async-start(f32[128,64,128]{2,1,0:T(8,128)} %synth_z.3), calls=%async_computation.2 | async-start | bytes 8388608 | tf_op jit(solution)/shard_map/all_to_all | solution.py:654
  79.9 14.5 %plane.2 = (f32[32,4,24,128]{3,2,1,0:T(8,128)}, f32[32,2,8,128]{3,2,1,0:T(8,128)}) custom-call(f32[8192,128]{1,0:T(8,128)} %bitcast.got_ref, bf16[2,2,256,256]{3,2,1,0:T(8,128)(2,1)} %constant.16.clone.sy_ref, bf16[2,2,256,256]{3,2,1,0:T(8,128)(2,1)} %constant.17.clone.sx_ref, bf16[2,2,176,256]{3,2,1,0:T(8,128)(2,1)} %constant.18.clone.ax_ref, ...), custom_call_target="tpu_custom_call" | custom-call | tf_op jit(solution)/shard_map/plane/pallas_call | solution.py:372
  94.4 37.4 %all-to-all-done.2 = f32[128,64,128]{2,1,0:T(8,128)} async-done(((f32[128,64,128]{2,1,0:T(8,128)}), f32[128,64,128]{2,1,0:T(8,128)}, u32[]{:S(2)}, u32[]{:S(2)}) %all-to-all-start.2) | async-done | bytes 4194336 | tf_op jit(solution)/shard_map/all_to_all | solution.py:654
  131.8 7.2 %all-to-all-start.1 = ((f32[128,24,128]{2,1,0:T(8,128)}), f32[128,24,128]{2,1,0:T(8,128)S(1)}, u32[]{:S(2)}, u32[]{:S(2)}) async-start(f32[128,24,128]{2,1,0:T(8,128)} %bitcast.5), calls=%async_computation.1 | async-start | bytes 3145728 | tf_op jit(solution)/shard_map/all_to_all | solution.py:654
  139.1 14.6 %plane.3 = f32[32,4,32,128]{3,2,1,0:T(8,128)} custom-call(f32[8192,128]{1,0:T(8,128)} %bitcast.2.got_ref, bf16[2,2,256,256]{3,2,1,0:T(8,128)(2,1)} %constant.16.clone.sy_ref, bf16[2,2,256,256]{3,2,1,0:T(8,128)(2,1)} %constant.17.clone.sx_ref, bf16[2,2,176,256]{3,2,1,0:T(8,128)(2,1)} %constant.18.clone.ax_ref, ...), custom_call_target="tpu_custom_call" | custom-call | tf_op jit(solution)/shard_map/plane/pallas_call | solution.py:372
  153.7 9.8 %all-to-all-done.1.back_ref.back0_ref = f32[128,24,128]{2,1,0:T(8,128)S(1)} async-done(((f32[128,24,128]{2,1,0:T(8,128)}), f32[128,24,128]{2,1,0:T(8,128)S(1)}, u32[]{:S(2)}, u32[]{:S(2)}) %all-to-all-start.1) | async-done | bytes 1572896 | tf_op jit(solution)/shard_map/all_to_all | solution.py:654
  163.6 0.0 copy-start.1
  163.6 0.0 copy-start.4
  163.6 5.9 %all-to-all-start.3 = ((f32[128,32,128]{2,1,0:T(8,128)}), f32[128,32,128]{2,1,0:T(8,128)}, u32[]{:S(2)}, u32[]{:S(2)}) async-start(f32[128,32,128]{2,1,0:T(8,128)} %bitcast.4), calls=%async_computation.3 | async-start | bytes 4194304 | tf_op jit(solution)/shard_map/all_to_all | solution.py:654
  169.5 0.0 copy-done.1
  169.5 0.1 slice.8
  169.6 0.0 copy-start
  169.6 1.6 collective-permute-start
  171.2 3.3 %collective-permute-done.more_ref = f32[128,16,128]{2,1,0:T(8,128)S(1)} collective-permute-done((f32[128,16,128]{2,1,0:T(8,128)S(1)}, f32[128,16,128]{2,1,0:T(8,128)S(1)}, u32[]{:S(2)}, u32[]{:S(2)}) %collective-permute-start) | collective-permute-done | bytes 1048608 | tf_op jit(solution)/shard_map/ppermute | solution.py:658
  174.4 0.0 copy-done.4
  174.4 0.0 copy-start.2
  174.4 1.4 copy-done.2
  175.8 5.5 %begin.1.part_ref = f32[8,5,2,64,128]{4,3,2,1,0:T(8,128)S(1)} custom-call(f32[128,24,128]{2,1,0:T(8,128)S(1)} %copy-done.2, f32[128,16,128]{2,1,0:T(8,128)S(1)} %collective-permute-done.more_ref, bf16[2,384,256]{2,1,0:T(8,128)(2,1)S(1)} %copy-done.4), custom_call_target="tpu_custom_call" | custom-call | tf_op jit(solution)/shard_map/begin/pallas_call | solution.py:447
  181.3 0.0 copy-start.3
  181.3 1.5 copy-done.3
  182.8 16.4 %all-to-all-done.3.back1_ref = f32[128,32,128]{2,1,0:T(8,128)} async-done(((f32[128,32,128]{2,1,0:T(8,128)}), f32[128,32,128]{2,1,0:T(8,128)}, u32[]{:S(2)}, u32[]{:S(2)}) %all-to-all-start.3) | async-done | bytes 2097184 | tf_op jit(solution)/shard_map/all_to_all | solution.py:654
  199.2 1.1 slice.7
  200.3 1.3 collective-permute-start.1
  201.6 2.5 %collective-permute-done.1.more_ref = f32[128,8,128]{2,1,0:T(8,128)S(1)} collective-permute-done((f32[128,8,128]{2,1,0:T(8,128)S(1)}, f32[128,8,128]{2,1,0:T(8,128)S(1)}, u32[]{:S(2)}, u32[]{:S(2)}) %collective-permute-start.1) | collective-permute-done | bytes 524320 | tf_op jit(solution)/shard_map/ppermute | solution.py:658
  204.1 0.0 copy-done
  204.1 8.4 %finish.1 = f32[3,2,8,64,256]{4,3,2,1,0:T(8,128)} custom-call(f32[128,24,128]{2,1,0:T(8,128)} %copy-done.1, f32[128,32,128]{2,1,0:T(8,128)} %all-to-all-done.3.back1_ref, f32[128,8,128]{2,1,0:T(8,128)S(1)} %collective-permute-done.1.more_ref, f32[8,5,2,64,128]{4,3,2,1,0:T(8,128)} %copy-done.3, f32[3,2,8,64,256]{4,3,2,1,0:T(8,128)S(1)} %copy-done, ...), custom_call_target="tpu_custom_call" | custom-call | tf_op jit(solution)/shard_map/finish/pallas_call | solution.py:619
Async XLA Ops:
  8.1 63.8 %all-to-all-start = ((f32[128,64,128]{2,1,0:T(8,128)}), f32[128,64,128]{2,1,0:T(8,128)}, u32[]{:S(2)}, u32[]{:S(2)}) async-start(f32[128,64,128]{2,1,0:T(8,128)} %synth_z.2), calls=%async_computation | async-start | bytes 8388608 | tf_op jit(solution)/shard_map/all_to_all | solution.py:654
  71.9 59.9 %all-to-all-start.2 = ((f32[128,64,128]{2,1,0:T(8,128)}), f32[128,64,128]{2,1,0:T(8,128)}, u32[]{:S(2)}, u32[]{:S(2)}) async-start(f32[128,64,128]{2,1,0:T(8,128)} %synth_z.3), calls=%async_computation.2 | async-start | bytes 8388608 | tf_op jit(solution)/shard_map/all_to_all | solution.py:654
  131.8 31.7 %all-to-all-start.1 = ((f32[128,24,128]{2,1,0:T(8,128)}), f32[128,24,128]{2,1,0:T(8,128)S(1)}, u32[]{:S(2)}, u32[]{:S(2)}) async-start(f32[128,24,128]{2,1,0:T(8,128)} %bitcast.5), calls=%async_computation.1 | async-start | bytes 3145728 | tf_op jit(solution)/shard_map/all_to_all | solution.py:654
  163.6 5.9 %copy-start.1 = (f32[128,24,128]{2,1,0:T(8,128)}, f32[128,24,128]{2,1,0:T(8,128)S(1)}, u32[]{:S(2)}) copy-start(f32[128,24,128]{2,1,0:T(8,128)S(1)} %all-to-all-done.1.back_ref.back0_ref) | copy-start | bytes 4718596
  163.6 10.9 %copy-start.4 = (bf16[2,384,256]{2,1,0:T(8,128)(2,1)S(1)}, bf16[2,384,256]{2,1,0:T(8,128)(2,1)}, u32[]{:S(2)}) copy-start(bf16[2,384,256]{2,1,0:T(8,128)(2,1)} %constant.20.clone.table_ref) | copy-start | bytes 1179652
  163.6 35.7 %all-to-all-start.3 = ((f32[128,32,128]{2,1,0:T(8,128)}), f32[128,32,128]{2,1,0:T(8,128)}, u32[]{:S(2)}, u32[]{:S(2)}) async-start(f32[128,32,128]{2,1,0:T(8,128)} %bitcast.4), calls=%async_computation.3 | async-start | bytes 4194304 | tf_op jit(solution)/shard_map/all_to_all | solution.py:654
  169.6 34.5 %copy-start = (f32[3,2,8,64,256]{4,3,2,1,0:T(8,128)S(1)}, f32[3,2,8,64,256]{4,3,2,1,0:T(8,128)}, u32[]{:S(2)}) copy-start(f32[3,2,8,64,256]{4,3,2,1,0:T(8,128)} %adjoint_ref.5) | copy-start | bytes 9437188
  169.6 4.8 %collective-permute-start = (f32[128,16,128]{2,1,0:T(8,128)S(1)}, f32[128,16,128]{2,1,0:T(8,128)S(1)}, u32[]{:S(2)}, u32[]{:S(2)}) collective-permute-start(f32[128,16,128]{2,1,0:T(8,128)S(1)} %slice.8), channel_id=1, source_target_pairs={{32,0},{64,96},{33,1},{65,97},{34,2},{66,98},{35,3},{67,99},{36,4}... | collective-permute-start | bytes 3145736 | tf_op jit(solution)/shard_map/ppermute | solution.py:658
  174.4 1.4 copy-start.2
  181.3 1.5 copy-start.3
  200.3 3.8 %collective-permute-start.1 = (f32[128,8,128]{2,1,0:T(8,128)S(1)}, f32[128,8,128]{2,1,0:T(8,128)S(1)}, u32[]{:S(2)}, u32[]{:S(2)}) collective-permute-start(f32[128,8,128]{2,1,0:T(8,128)S(1)} %slice.7), channel_id=1, source_target_pairs={{32,0},{64,96},{33,1},{65,97},{34,2},{66,98},{35,3},{67,99},{36,4}... | collective-permute-start | bytes 1572872 | tf_op jit(solution)/shard_map/ppermute | solution.py:658

commit v10 on v9

--- a/solution.py
+++ b/solution.py
@@ -27,6 +27,7 @@
 LIGHT = (1, 2)
 LIGHT_ROW = (0, 40)
 SLOT = 24
+WAITS = {0: 1, 1: 4, 4: 8}
 
 section_step = 0.25
 viscous_rate = 0.05
@@ -137,7 +138,7 @@
 
 
 def synth_z_kernel(
-    plane, adjoint_ref, velocity_ref, table_ref, out_ref, adj_ref, vel_ref, sent_ref, sems
+    plane, adjoint_ref, velocity_ref, table_ref, out_ref, adj_ref, vel_ref, turn_ref, sent_ref, sems
 ):
     def load(k, which):
         source, target = ((adjoint_ref, adj_ref), (velocity_ref, vel_ref))[which]
@@ -148,9 +149,12 @@
             sent_ref.at[k], out_ref.at[:, pl.ds(k * SENT, SENT)], sems.at[2, k]
         )
 
+    turn_copy = pltpu.make_async_copy(table_ref, turn_ref, sems.at[3, 0])
     for k in range(ROWS_X):
         for which in range(2):
             load(k, which).start()
+        if k == 0:
+            turn_copy.start()
     ky = wave_y(lax.axis_index("narrow") * ROWS_Y, (ROWS_Y, 1), 0)
     kz = wave_z((1, NZ), 1)
     half_sign = jnp.where(lax.broadcasted_iota(jnp.int32, (1, 128), 1) < 64, -1.0, 1.0)
@@ -158,8 +162,10 @@
     for k in range(ROWS_X):
         number_x = lax.axis_index("wide") * ROWS_X + k
         kx = 2.0 * math.pi / NX * number_x.astype(jnp.float32)
-        if k % 4 == 0:
-            for near in range(k, k + 4):
+        if k == 0:
+            turn_copy.wait()
+        if k in WAITS:
+            for near in range(k, WAITS[k]):
                 for which in range(2):
                     load(near, which).wait()
         vel = [[vel_ref[c, part, k] for part in range(2)] for c in range(3)]
@@ -176,7 +182,7 @@
                 merged = value[:, :128] - value[:, 128:]
             upper, lower = split(merged)
             stacked = jnp.concatenate([upper, lower, upper], 1)
-            both = dot(table_ref[...], stacked, ((1,), (1,)))
+            both = dot(turn_ref[...], stacked, ((1,), (1,)))
             for f in range(2):
                 lanes = slice(128 * f, 128 * f + 128)
                 turned = pltpu.roll(both[128:, lanes], 64, 1)
@@ -195,15 +201,16 @@
         in_specs=[
             pl.BlockSpec(memory_space=pl.ANY),
             pl.BlockSpec(memory_space=pl.ANY),
-            pl.BlockSpec(memory_space=pltpu.VMEM),
+            pl.BlockSpec(memory_space=pl.ANY),
         ],
         out_specs=pl.BlockSpec(memory_space=pl.ANY),
         out_shape=jax.ShapeDtypeStruct(shape, jnp.float32),
         scratch_shapes=[
             pltpu.VMEM(block, jnp.float32),
             pltpu.VMEM(block, jnp.float32),
+            pltpu.VMEM(table.shape, jnp.bfloat16),
             pltpu.VMEM((ROWS_X, DEVICES, SENT, 128), jnp.float32),
-            pltpu.SemaphoreType.DMA((3, ROWS_X)),
+            pltpu.SemaphoreType.DMA((4, ROWS_X)),
         ],
         compiler_params=pltpu.CompilerParams(vmem_limit_bytes=vmem_bytes),
         name="synth_z",
@@ -561,7 +568,9 @@
                 [got_ref[f, :, k, :] for f in range(4)] + [more_ref[:, k, :]],
                 table_ref[1],
             )
-            fetch(k).wait()
+            if k in (0, 2):
+                for near in range(k, 2 if k == 0 else ROWS_X):
+                    fetch(near).wait()
             for f, span in enumerate(spans):
                 second = unite(span, slice(0, 64), slice(64, 128))
                 got.append(mirror((mid_ref[k, f, 0], mid_ref[k, f, 1]), second))

time: 213 us -> 210 us (0.986)
  Pallas kernels: 59.4 us -> 55.2 us
    pallas_call x2, Pallas kernels: 16.3 us -> 13.7 us  [synth_z(): pl.pallas_call(functools.partial(synth_z_kernel, plane), in_specs=[pl.Blo...]
where the time goes in v10:
time: 210 us
  waiting for transfers between devices  115 us (55%)
  Pallas kernels  55.2 us (26%)
  starting transfers between devices  35.6 us (17%)
  local copies, waits for them, and re-layouts  4.06 us (2%)
    all_to_all x4, waiting for transfers between devices, swap(): return lax.all_to_all(chunks, ('wide', 'narrow'), 0, 0, tiled=True)  109 us
    all_to_all x4, starting transfers between devices, swap(): return lax.all_to_all(chunks, ('wide', 'narrow'), 0, 0, tiled=True)  32.8 us
    pallas_call x2, Pallas kernels, run_plane(): pl.pallas_call(functools.partial(plane_kernel, plane), out_shape=out_shap...  29.1 us
    pallas_call x2, Pallas kernels, synth_z(): pl.pallas_call(functools.partial(synth_z_kernel, plane), in_specs=[pl.Blo...  13.7 us
    pallas_call x1, Pallas kernels, finish(): pl.pallas_call(finish_kernel, in_specs=[pl.BlockSpec(memory_space=pltpu.H...  6.9 us
    ppermute x2, waiting for transfers between devices, forward(): lax.ppermute(tiles, 'narrow', [(LIGHT[0], HEAVY[0]), (LIGHT[1], HEAVY[1])])  5.76 us
    pallas_call x1, Pallas kernels, begin(): pl.pallas_call(begin_kernel, in_specs=[pl.BlockSpec(memory_space=pltpu.HB...  5.47 us
  transfers between devices with their start and end apart: 6, of which 6 were waited for; matrix products, arithmetic and copies ran while one was open for 0% of the time, Pallas kernels for 20%

profile of v10, /device:TPU:0, one launch (start us, length us, event | category | flops | bytes accessed | tf_op | source)
XLA Modules:
  0.0 209.9 jit_solution(6802043284124471675)
XLA Ops:
  0.0 6.8 %synth_z.2 = f32[128,64,128]{2,1,0:T(8,128)} custom-call(f32[3,2,8,64,256]{4,3,2,1,0:T(8,128)} %adjoint_ref.5, f32[3,2,8,64,256]{4,3,2,1,0:T(8,128)} %velocity_ref.3, bf16[256,384]{1,0:T(8,128)(2,1)} %constant.14.clone.table_ref), custom_call_target="tpu_custom_call" | custom-call | tf_op jit(solution)/shard_map/synth_z/pallas_call | solution.py:199
  6.8 11.7 %all-to-all-start = ((f32[128,64,128]{2,1,0:T(8,128)}), f32[128,64,128]{2,1,0:T(8,128)}, u32[]{:S(2)}, u32[]{:S(2)}) async-start(f32[128,64,128]{2,1,0:T(8,128)} %synth_z.2), calls=%async_computation | async-start | bytes 8388608 | tf_op jit(solution)/shard_map/all_to_all | solution.py:663
  18.5 6.9 %synth_z.3 = f32[128,64,128]{2,1,0:T(8,128)} custom-call(f32[3,2,8,64,256]{4,3,2,1,0:T(8,128)} %adjoint_ref.5, f32[3,2,8,64,256]{4,3,2,1,0:T(8,128)} %velocity_ref.3, bf16[256,384]{1,0:T(8,128)(2,1)} %constant.15.clone.table_ref), custom_call_target="tpu_custom_call" | custom-call | tf_op jit(solution)/shard_map/synth_z/pallas_call | solution.py:199
  25.4 45.2 %all-to-all-done = f32[128,64,128]{2,1,0:T(8,128)} async-done(((f32[128,64,128]{2,1,0:T(8,128)}), f32[128,64,128]{2,1,0:T(8,128)}, u32[]{:S(2)}, u32[]{:S(2)}) %all-to-all-start) | async-done | bytes 4194336 | tf_op jit(solution)/shard_map/all_to_all | solution.py:663
  70.6 7.9 %all-to-all-start.2 = ((f32[128,64,128]{2,1,0:T(8,128)}), f32[128,64,128]{2,1,0:T(8,128)}, u32[]{:S(2)}, u32[]{:S(2)}) async-start(f32[128,64,128]{2,1,0:T(8,128)} %synth_z.3), calls=%async_computation.2 | async-start | bytes 8388608 | tf_op jit(solution)/shard_map/all_to_all | solution.py:663
  78.6 14.5 %plane.2 = (f32[32,4,24,128]{3,2,1,0:T(8,128)}, f32[32,2,8,128]{3,2,1,0:T(8,128)}) custom-call(f32[8192,128]{1,0:T(8,128)} %bitcast.got_ref, bf16[2,2,256,256]{3,2,1,0:T(8,128)(2,1)} %constant.16.clone.sy_ref, bf16[2,2,256,256]{3,2,1,0:T(8,128)(2,1)} %constant.17.clone.sx_ref, bf16[2,2,176,256]{3,2,1,0:T(8,128)(2,1)} %constant.18.clone.ax_ref, ...), custom_call_target="tpu_custom_call" | custom-call | tf_op jit(solution)/shard_map/plane/pallas_call | solution.py:379
  93.1 37.4 %all-to-all-done.2 = f32[128,64,128]{2,1,0:T(8,128)} async-done(((f32[128,64,128]{2,1,0:T(8,128)}), f32[128,64,128]{2,1,0:T(8,128)}, u32[]{:S(2)}, u32[]{:S(2)}) %all-to-all-start.2) | async-done | bytes 4194336 | tf_op jit(solution)/shard_map/all_to_all | solution.py:663
  130.5 7.2 %all-to-all-start.1 = ((f32[128,24,128]{2,1,0:T(8,128)}), f32[128,24,128]{2,1,0:T(8,128)S(1)}, u32[]{:S(2)}, u32[]{:S(2)}) async-start(f32[128,24,128]{2,1,0:T(8,128)} %bitcast.5), calls=%async_computation.1 | async-start | bytes 3145728 | tf_op jit(solution)/shard_map/all_to_all | solution.py:663
  137.8 14.6 %plane.3 = f32[32,4,32,128]{3,2,1,0:T(8,128)} custom-call(f32[8192,128]{1,0:T(8,128)} %bitcast.2.got_ref, bf16[2,2,256,256]{3,2,1,0:T(8,128)(2,1)} %constant.16.clone.sy_ref, bf16[2,2,256,256]{3,2,1,0:T(8,128)(2,1)} %constant.17.clone.sx_ref, bf16[2,2,176,256]{3,2,1,0:T(8,128)(2,1)} %constant.18.clone.ax_ref, ...), custom_call_target="tpu_custom_call" | custom-call | tf_op jit(solution)/shard_map/plane/pallas_call | solution.py:379
  152.4 9.9 %all-to-all-done.1.back_ref.back0_ref = f32[128,24,128]{2,1,0:T(8,128)S(1)} async-done(((f32[128,24,128]{2,1,0:T(8,128)}), f32[128,24,128]{2,1,0:T(8,128)S(1)}, u32[]{:S(2)}, u32[]{:S(2)}) %all-to-all-start.1) | async-done | bytes 1572896 | tf_op jit(solution)/shard_map/all_to_all | solution.py:663
  162.3 0.0 copy-start.1
  162.3 0.0 copy-start.4
  162.3 5.9 %all-to-all-start.3 = ((f32[128,32,128]{2,1,0:T(8,128)}), f32[128,32,128]{2,1,0:T(8,128)}, u32[]{:S(2)}, u32[]{:S(2)}) async-start(f32[128,32,128]{2,1,0:T(8,128)} %bitcast.4), calls=%async_computation.3 | async-start | bytes 4194304 | tf_op jit(solution)/shard_map/all_to_all | solution.py:663
  168.2 0.0 copy-done.1
  168.2 0.1 slice.8
  168.3 0.0 copy-start
  168.3 1.6 collective-permute-start
  169.9 3.3 %collective-permute-done.more_ref = f32[128,16,128]{2,1,0:T(8,128)S(1)} collective-permute-done((f32[128,16,128]{2,1,0:T(8,128)S(1)}, f32[128,16,128]{2,1,0:T(8,128)S(1)}, u32[]{:S(2)}, u32[]{:S(2)}) %collective-permute-start) | collective-permute-done | bytes 1048608 | tf_op jit(solution)/shard_map/ppermute | solution.py:667
  173.1 0.0 copy-done.4
  173.1 0.0 copy-start.2
  173.1 1.4 copy-done.2
  174.5 5.5 %begin.1.part_ref = f32[8,5,2,64,128]{4,3,2,1,0:T(8,128)S(1)} custom-call(f32[128,24,128]{2,1,0:T(8,128)S(1)} %copy-done.2, f32[128,16,128]{2,1,0:T(8,128)S(1)} %collective-permute-done.more_ref, bf16[2,384,256]{2,1,0:T(8,128)(2,1)S(1)} %copy-done.4), custom_call_target="tpu_custom_call" | custom-call | tf_op jit(solution)/shard_map/begin/pallas_call | solution.py:454
  180.0 0.0 copy-start.3
  180.0 1.5 copy-done.3
  181.5 16.4 %all-to-all-done.3.back1_ref = f32[128,32,128]{2,1,0:T(8,128)} async-done(((f32[128,32,128]{2,1,0:T(8,128)}), f32[128,32,128]{2,1,0:T(8,128)}, u32[]{:S(2)}, u32[]{:S(2)}) %all-to-all-start.3) | async-done | bytes 2097184 | tf_op jit(solution)/shard_map/all_to_all | solution.py:663
  197.9 1.1 slice.7
  199.0 1.3 collective-permute-start.1
  200.3 2.5 %collective-permute-done.1.more_ref = f32[128,8,128]{2,1,0:T(8,128)S(1)} collective-permute-done((f32[128,8,128]{2,1,0:T(8,128)S(1)}, f32[128,8,128]{2,1,0:T(8,128)S(1)}, u32[]{:S(2)}, u32[]{:S(2)}) %collective-permute-start.1) | collective-permute-done | bytes 524320 | tf_op jit(solution)/shard_map/ppermute | solution.py:667
  202.8 0.0 copy-done
  202.8 6.9 %finish.1 = f32[3,2,8,64,256]{4,3,2,1,0:T(8,128)} custom-call(f32[128,24,128]{2,1,0:T(8,128)} %copy-done.1, f32[128,32,128]{2,1,0:T(8,128)} %all-to-all-done.3.back1_ref, f32[128,8,128]{2,1,0:T(8,128)S(1)} %collective-permute-done.1.more_ref, f32[8,5,2,64,128]{4,3,2,1,0:T(8,128)} %copy-done.3, f32[3,2,8,64,256]{4,3,2,1,0:T(8,128)S(1)} %copy-done, ...), custom_call_target="tpu_custom_call" | custom-call | tf_op jit(solution)/shard_map/finish/pallas_call | solution.py:628
Async XLA Ops:
  6.8 63.8 %all-to-all-start = ((f32[128,64,128]{2,1,0:T(8,128)}), f32[128,64,128]{2,1,0:T(8,128)}, u32[]{:S(2)}, u32[]{:S(2)}) async-start(f32[128,64,128]{2,1,0:T(8,128)} %synth_z.2), calls=%async_computation | async-start | bytes 8388608 | tf_op jit(solution)/shard_map/all_to_all | solution.py:663
  70.6 59.9 %all-to-all-start.2 = ((f32[128,64,128]{2,1,0:T(8,128)}), f32[128,64,128]{2,1,0:T(8,128)}, u32[]{:S(2)}, u32[]{:S(2)}) async-start(f32[128,64,128]{2,1,0:T(8,128)} %synth_z.3), calls=%async_computation.2 | async-start | bytes 8388608 | tf_op jit(solution)/shard_map/all_to_all | solution.py:663
  130.5 31.7 %all-to-all-start.1 = ((f32[128,24,128]{2,1,0:T(8,128)}), f32[128,24,128]{2,1,0:T(8,128)S(1)}, u32[]{:S(2)}, u32[]{:S(2)}) async-start(f32[128,24,128]{2,1,0:T(8,128)} %bitcast.5), calls=%async_computation.1 | async-start | bytes 3145728 | tf_op jit(solution)/shard_map/all_to_all | solution.py:663
  162.3 5.9 %copy-start.1 = (f32[128,24,128]{2,1,0:T(8,128)}, f32[128,24,128]{2,1,0:T(8,128)S(1)}, u32[]{:S(2)}) copy-start(f32[128,24,128]{2,1,0:T(8,128)S(1)} %all-to-all-done.1.back_ref.back0_ref) | copy-start | bytes 4718596
  162.3 10.9 %copy-start.4 = (bf16[2,384,256]{2,1,0:T(8,128)(2,1)S(1)}, bf16[2,384,256]{2,1,0:T(8,128)(2,1)}, u32[]{:S(2)}) copy-start(bf16[2,384,256]{2,1,0:T(8,128)(2,1)} %constant.20.clone.table_ref) | copy-start | bytes 1179652
  162.3 35.7 %all-to-all-start.3 = ((f32[128,32,128]{2,1,0:T(8,128)}), f32[128,32,128]{2,1,0:T(8,128)}, u32[]{:S(2)}, u32[]{:S(2)}) async-start(f32[128,32,128]{2,1,0:T(8,128)} %bitcast.4), calls=%async_computation.3 | async-start | bytes 4194304 | tf_op jit(solution)/shard_map/all_to_all | solution.py:663
  168.3 34.5 %copy-start = (f32[3,2,8,64,256]{4,3,2,1,0:T(8,128)S(1)}, f32[3,2,8,64,256]{4,3,2,1,0:T(8,128)}, u32[]{:S(2)}) copy-start(f32[3,2,8,64,256]{4,3,2,1,0:T(8,128)} %adjoint_ref.5) | copy-start | bytes 9437188
  168.3 4.8 %collective-permute-start = (f32[128,16,128]{2,1,0:T(8,128)S(1)}, f32[128,16,128]{2,1,0:T(8,128)S(1)}, u32[]{:S(2)}, u32[]{:S(2)}) collective-permute-start(f32[128,16,128]{2,1,0:T(8,128)S(1)} %slice.8), channel_id=1, source_target_pairs={{32,0},{64,96},{33,1},{65,97},{34,2},{66,98},{35,3},{67,99},{36,4}... | collective-permute-start | bytes 3145736 | tf_op jit(solution)/shard_map/ppermute | solution.py:667
  173.1 1.4 copy-start.2
  180.0 1.5 copy-start.3
  199.0 3.8 %collective-permute-start.1 = (f32[128,8,128]{2,1,0:T(8,128)S(1)}, f32[128,8,128]{2,1,0:T(8,128)S(1)}, u32[]{:S(2)}, u32[]{:S(2)}) collective-permute-start(f32[128,8,128]{2,1,0:T(8,128)S(1)} %slice.7), channel_id=1, source_target_pairs={{32,0},{64,96},{33,1},{65,97},{34,2},{66,98},{35,3},{67,99},{36,4}... | collective-permute-start | bytes 1572872 | tf_op jit(solution)/shard_map/ppermute | solution.py:667

commit v11 on v10

--- a/solution.py
+++ b/solution.py
@@ -27,7 +27,7 @@
 LIGHT = (1, 2)
 LIGHT_ROW = (0, 40)
 SLOT = 24
-WAITS = {0: 1, 1: 4, 4: 8}
+WAITS = {0: 1, 1: 3, 3: 8}
 
 section_step = 0.25
 viscous_rate = 0.05
@@ -568,8 +568,8 @@
                 [got_ref[f, :, k, :] for f in range(4)] + [more_ref[:, k, :]],
                 table_ref[1],
             )
-            if k in (0, 2):
-                for near in range(k, 2 if k == 0 else ROWS_X):
+            if k in (0, 1):
+                for near in range(k, 1 if k == 0 else ROWS_X):
                     fetch(near).wait()
             for f, span in enumerate(spans):
                 second = unite(span, slice(0, 64), slice(64, 128))

time: 210 us -> 211 us (level)
  no operation moved by 1% of the time
where the time goes in v11:
time: 211 us; the launch traced here: 210 us
  waiting for transfers between devices  115 us (55%)
  Pallas kernels  55.7 us (26%)
  starting transfers between devices  35.6 us (17%)
  local copies, waits for them, and re-layouts  4.06 us (2%)
    all_to_all x4, waiting for transfers between devices, swap(): return lax.all_to_all(chunks, ('wide', 'narrow'), 0, 0, tiled=True)  109 us
    all_to_all x4, starting transfers between devices, swap(): return lax.all_to_all(chunks, ('wide', 'narrow'), 0, 0, tiled=True)  32.8 us
    pallas_call x2, Pallas kernels, run_plane(): pl.pallas_call(functools.partial(plane_kernel, plane), out_shape=out_shap...  29.1 us
    pallas_call x2, Pallas kernels, synth_z(): pl.pallas_call(functools.partial(synth_z_kernel, plane), in_specs=[pl.Blo...  13.8 us
    pallas_call x1, Pallas kernels, finish(): pl.pallas_call(finish_kernel, in_specs=[pl.BlockSpec(memory_space=pltpu.H...  7.29 us
    ppermute x2, waiting for transfers between devices, forward(): lax.ppermute(tiles, 'narrow', [(LIGHT[0], HEAVY[0]), (LIGHT[1], HEAVY[1])])  5.76 us
    pallas_call x1, Pallas kernels, begin(): pl.pallas_call(begin_kernel, in_specs=[pl.BlockSpec(memory_space=pltpu.HB...  5.47 us
  transfers between devices with their start and end apart: 6, of which 6 were waited for; matrix products, arithmetic and copies ran while one was open for 0% of the time, Pallas kernels for 20%

profile of v11, /device:TPU:0, one launch (start us, length us, event | category | flops | bytes accessed | tf_op | source)
XLA Modules:
  0.0 210.3 jit_solution(444991748320977339)
XLA Ops:
  0.0 6.9 %synth_z.2 = f32[128,64,128]{2,1,0:T(8,128)} custom-call(f32[3,2,8,64,256]{4,3,2,1,0:T(8,128)} %adjoint_ref.5, f32[3,2,8,64,256]{4,3,2,1,0:T(8,128)} %velocity_ref.3, bf16[256,384]{1,0:T(8,128)(2,1)} %constant.14.clone.table_ref), custom_call_target="tpu_custom_call" | custom-call | tf_op jit(solution)/shard_map/synth_z/pallas_call | solution.py:199
  6.9 11.7 %all-to-all-start = ((f32[128,64,128]{2,1,0:T(8,128)}), f32[128,64,128]{2,1,0:T(8,128)}, u32[]{:S(2)}, u32[]{:S(2)}) async-start(f32[128,64,128]{2,1,0:T(8,128)} %synth_z.2), calls=%async_computation | async-start | bytes 8388608 | tf_op jit(solution)/shard_map/all_to_all | solution.py:663
  18.6 6.9 %synth_z.3 = f32[128,64,128]{2,1,0:T(8,128)} custom-call(f32[3,2,8,64,256]{4,3,2,1,0:T(8,128)} %adjoint_ref.5, f32[3,2,8,64,256]{4,3,2,1,0:T(8,128)} %velocity_ref.3, bf16[256,384]{1,0:T(8,128)(2,1)} %constant.15.clone.table_ref), custom_call_target="tpu_custom_call" | custom-call | tf_op jit(solution)/shard_map/synth_z/pallas_call | solution.py:199
  25.5 45.2 %all-to-all-done = f32[128,64,128]{2,1,0:T(8,128)} async-done(((f32[128,64,128]{2,1,0:T(8,128)}), f32[128,64,128]{2,1,0:T(8,128)}, u32[]{:S(2)}, u32[]{:S(2)}) %all-to-all-start) | async-done | bytes 4194336 | tf_op jit(solution)/shard_map/all_to_all | solution.py:663
  70.7 7.9 %all-to-all-start.2 = ((f32[128,64,128]{2,1,0:T(8,128)}), f32[128,64,128]{2,1,0:T(8,128)}, u32[]{:S(2)}, u32[]{:S(2)}) async-start(f32[128,64,128]{2,1,0:T(8,128)} %synth_z.3), calls=%async_computation.2 | async-start | bytes 8388608 | tf_op jit(solution)/shard_map/all_to_all | solution.py:663
  78.6 14.5 %plane.2 = (f32[32,4,24,128]{3,2,1,0:T(8,128)}, f32[32,2,8,128]{3,2,1,0:T(8,128)}) custom-call(f32[8192,128]{1,0:T(8,128)} %bitcast.got_ref, bf16[2,2,256,256]{3,2,1,0:T(8,128)(2,1)} %constant.16.clone.sy_ref, bf16[2,2,256,256]{3,2,1,0:T(8,128)(2,1)} %constant.17.clone.sx_ref, bf16[2,2,176,256]{3,2,1,0:T(8,128)(2,1)} %constant.18.clone.ax_ref, ...), custom_call_target="tpu_custom_call" | custom-call | tf_op jit(solution)/shard_map/plane/pallas_call | solution.py:379
  93.1 37.4 %all-to-all-done.2 = f32[128,64,128]{2,1,0:T(8,128)} async-done(((f32[128,64,128]{2,1,0:T(8,128)}), f32[128,64,128]{2,1,0:T(8,128)}, u32[]{:S(2)}, u32[]{:S(2)}) %all-to-all-start.2) | async-done | bytes 4194336 | tf_op jit(solution)/shard_map/all_to_all | solution.py:663
  130.6 7.2 %all-to-all-start.1 = ((f32[128,24,128]{2,1,0:T(8,128)}), f32[128,24,128]{2,1,0:T(8,128)S(1)}, u32[]{:S(2)}, u32[]{:S(2)}) async-start(f32[128,24,128]{2,1,0:T(8,128)} %bitcast.5), calls=%async_computation.1 | async-start | bytes 3145728 | tf_op jit(solution)/shard_map/all_to_all | solution.py:663
  137.8 14.6 %plane.3 = f32[32,4,32,128]{3,2,1,0:T(8,128)} custom-call(f32[8192,128]{1,0:T(8,128)} %bitcast.2.got_ref, bf16[2,2,256,256]{3,2,1,0:T(8,128)(2,1)} %constant.16.clone.sy_ref, bf16[2,2,256,256]{3,2,1,0:T(8,128)(2,1)} %constant.17.clone.sx_ref, bf16[2,2,176,256]{3,2,1,0:T(8,128)(2,1)} %constant.18.clone.ax_ref, ...), custom_call_target="tpu_custom_call" | custom-call | tf_op jit(solution)/shard_map/plane/pallas_call | solution.py:379
  152.5 9.9 %all-to-all-done.1.back_ref.back0_ref = f32[128,24,128]{2,1,0:T(8,128)S(1)} async-done(((f32[128,24,128]{2,1,0:T(8,128)}), f32[128,24,128]{2,1,0:T(8,128)S(1)}, u32[]{:S(2)}, u32[]{:S(2)}) %all-to-all-start.1) | async-done | bytes 1572896 | tf_op jit(solution)/shard_map/all_to_all | solution.py:663
  162.3 0.0 copy-start.1
  162.3 0.0 copy-start.4
  162.3 5.9 %all-to-all-start.3 = ((f32[128,32,128]{2,1,0:T(8,128)}), f32[128,32,128]{2,1,0:T(8,128)}, u32[]{:S(2)}, u32[]{:S(2)}) async-start(f32[128,32,128]{2,1,0:T(8,128)} %bitcast.4), calls=%async_computation.3 | async-start | bytes 4194304 | tf_op jit(solution)/shard_map/all_to_all | solution.py:663
  168.2 0.0 copy-done.1
  168.3 0.1 slice.8
  168.3 0.0 copy-start
  168.3 1.6 collective-permute-start
  169.9 3.3 %collective-permute-done.more_ref = f32[128,16,128]{2,1,0:T(8,128)S(1)} collective-permute-done((f32[128,16,128]{2,1,0:T(8,128)S(1)}, f32[128,16,128]{2,1,0:T(8,128)S(1)}, u32[]{:S(2)}, u32[]{:S(2)}) %collective-permute-start) | collective-permute-done | bytes 1048608 | tf_op jit(solution)/shard_map/ppermute | solution.py:667
  173.2 0.0 copy-done.4
  173.2 0.0 copy-start.2
  173.2 1.4 copy-done.2
  174.6 5.5 %begin.1.part_ref = f32[8,5,2,64,128]{4,3,2,1,0:T(8,128)S(1)} custom-call(f32[128,24,128]{2,1,0:T(8,128)S(1)} %copy-done.2, f32[128,16,128]{2,1,0:T(8,128)S(1)} %collective-permute-done.more_ref, bf16[2,384,256]{2,1,0:T(8,128)(2,1)S(1)} %copy-done.4), custom_call_target="tpu_custom_call" | custom-call | tf_op jit(solution)/shard_map/begin/pallas_call | solution.py:454
  180.1 0.0 copy-start.3
  180.1 1.5 copy-done.3
  181.6 16.4 %all-to-all-done.3.back1_ref = f32[128,32,128]{2,1,0:T(8,128)} async-done(((f32[128,32,128]{2,1,0:T(8,128)}), f32[128,32,128]{2,1,0:T(8,128)}, u32[]{:S(2)}, u32[]{:S(2)}) %all-to-all-start.3) | async-done | bytes 2097184 | tf_op jit(solution)/shard_map/all_to_all | solution.py:663
  198.0 1.1 slice.7
  199.1 1.3 collective-permute-start.1
  200.4 2.5 %collective-permute-done.1.more_ref = f32[128,8,128]{2,1,0:T(8,128)S(1)} collective-permute-done((f32[128,8,128]{2,1,0:T(8,128)S(1)}, f32[128,8,128]{2,1,0:T(8,128)S(1)}, u32[]{:S(2)}, u32[]{:S(2)}) %collective-permute-start.1) | collective-permute-done | bytes 524320 | tf_op jit(solution)/shard_map/ppermute | solution.py:667
  202.9 0.0 copy-done
  202.9 7.3 %finish.1 = f32[3,2,8,64,256]{4,3,2,1,0:T(8,128)} custom-call(f32[128,24,128]{2,1,0:T(8,128)} %copy-done.1, f32[128,32,128]{2,1,0:T(8,128)} %all-to-all-done.3.back1_ref, f32[128,8,128]{2,1,0:T(8,128)S(1)} %collective-permute-done.1.more_ref, f32[8,5,2,64,128]{4,3,2,1,0:T(8,128)} %copy-done.3, f32[3,2,8,64,256]{4,3,2,1,0:T(8,128)S(1)} %copy-done, ...), custom_call_target="tpu_custom_call" | custom-call | tf_op jit(solution)/shard_map/finish/pallas_call | solution.py:628
Async XLA Ops:
  6.9 63.8 %all-to-all-start = ((f32[128,64,128]{2,1,0:T(8,128)}), f32[128,64,128]{2,1,0:T(8,128)}, u32[]{:S(2)}, u32[]{:S(2)}) async-start(f32[128,64,128]{2,1,0:T(8,128)} %synth_z.2), calls=%async_computation | async-start | bytes 8388608 | tf_op jit(solution)/shard_map/all_to_all | solution.py:663
  70.7 59.9 %all-to-all-start.2 = ((f32[128,64,128]{2,1,0:T(8,128)}), f32[128,64,128]{2,1,0:T(8,128)}, u32[]{:S(2)}, u32[]{:S(2)}) async-start(f32[128,64,128]{2,1,0:T(8,128)} %synth_z.3), calls=%async_computation.2 | async-start | bytes 8388608 | tf_op jit(solution)/shard_map/all_to_all | solution.py:663
  130.6 31.7 %all-to-all-start.1 = ((f32[128,24,128]{2,1,0:T(8,128)}), f32[128,24,128]{2,1,0:T(8,128)S(1)}, u32[]{:S(2)}, u32[]{:S(2)}) async-start(f32[128,24,128]{2,1,0:T(8,128)} %bitcast.5), calls=%async_computation.1 | async-start | bytes 3145728 | tf_op jit(solution)/shard_map/all_to_all | solution.py:663
  162.3 5.9 %copy-start.1 = (f32[128,24,128]{2,1,0:T(8,128)}, f32[128,24,128]{2,1,0:T(8,128)S(1)}, u32[]{:S(2)}) copy-start(f32[128,24,128]{2,1,0:T(8,128)S(1)} %all-to-all-done.1.back_ref.back0_ref) | copy-start | bytes 4718596
  162.3 10.9 %copy-start.4 = (bf16[2,384,256]{2,1,0:T(8,128)(2,1)S(1)}, bf16[2,384,256]{2,1,0:T(8,128)(2,1)}, u32[]{:S(2)}) copy-start(bf16[2,384,256]{2,1,0:T(8,128)(2,1)} %constant.20.clone.table_ref) | copy-start | bytes 1179652
  162.3 35.7 %all-to-all-start.3 = ((f32[128,32,128]{2,1,0:T(8,128)}), f32[128,32,128]{2,1,0:T(8,128)}, u32[]{:S(2)}, u32[]{:S(2)}) async-start(f32[128,32,128]{2,1,0:T(8,128)} %bitcast.4), calls=%async_computation.3 | async-start | bytes 4194304 | tf_op jit(solution)/shard_map/all_to_all | solution.py:663
  168.3 34.5 %copy-start = (f32[3,2,8,64,256]{4,3,2,1,0:T(8,128)S(1)}, f32[3,2,8,64,256]{4,3,2,1,0:T(8,128)}, u32[]{:S(2)}) copy-start(f32[3,2,8,64,256]{4,3,2,1,0:T(8,128)} %adjoint_ref.5) | copy-start | bytes 9437188
  168.3 4.8 %collective-permute-start = (f32[128,16,128]{2,1,0:T(8,128)S(1)}, f32[128,16,128]{2,1,0:T(8,128)S(1)}, u32[]{:S(2)}, u32[]{:S(2)}) collective-permute-start(f32[128,16,128]{2,1,0:T(8,128)S(1)} %slice.8), channel_id=1, source_target_pairs={{32,0},{64,96},{33,1},{65,97},{34,2},{66,98},{35,3},{67,99},{36,4}... | collective-permute-start | bytes 3145736 | tf_op jit(solution)/shard_map/ppermute | solution.py:667
  173.2 1.4 copy-start.2
  180.1 1.5 copy-start.3
  199.1 3.8 %collective-permute-start.1 = (f32[128,8,128]{2,1,0:T(8,128)S(1)}, f32[128,8,128]{2,1,0:T(8,128)S(1)}, u32[]{:S(2)}, u32[]{:S(2)}) collective-permute-start(f32[128,8,128]{2,1,0:T(8,128)S(1)} %slice.7), channel_id=1, source_target_pairs={{32,0},{64,96},{33,1},{65,97},{34,2},{66,98},{35,3},{67,99},{36,4}... | collective-permute-start | bytes 1572872 | tf_op jit(solution)/shard_map/ppermute | solution.py:667
